TPU v7x, 32 devices: a whole 2x2x4 slice. The times are simulated.
32 devices in a mesh: rep: 4 (over y, x), shard: 8 (over z, core).
Axes of the slice: x: 2, y: 2, z: 4, core: 2. Of those that a mesh axis runs over, the one named last changes fastest.
Arguments:
- tokens: bfloat16 [32768, 768], P(('rep', 'shard')), may hold values from -6 to 6
- cotangent: bfloat16 [32768, 768], P(('rep', 'shard')), may hold values from -6 to 6
- qkv_weight: bfloat16 [768, 2304], P('shard'), may hold values from -0.21875 to 0.21875
- query_value_bias: bfloat16 [2, 768], P(None, 'shard'), may hold values from -3 to 3
- out_weight: bfloat16 [768, 768], P('shard'), may hold values from -0.875 to 0.875
- out_bias: bfloat16 [768], P('shard'), may hold values from -2 to 2
- norm_one_gain: bfloat16 [768], P('shard'), may hold values from 0.099609375 to 1.8984375
- norm_one_shift: bfloat16 [768], P('shard'), may hold values from -2 to 2
- up_weight: bfloat16 [768, 3072], P('shard'), may hold values from -0.21875 to 0.21875
- up_bias: bfloat16 [3072], P('shard'), may hold values from -3 to 3
- down_weight: bfloat16 [3072, 768], P('shard'), may hold values from -0.109375 to 0.109375
- down_bias: bfloat16 [768], P('shard'), may hold values from -2 to 2
- norm_two_gain: bfloat16 [768], P('shard'), may hold values from 0.099609375 to 1.8984375
- norm_two_shift: bfloat16 [768], P('shard'), may hold values from -2 to 2
- segment_ids: int32 [64, 512], P(('rep', 'shard')), may hold values from 0 to 7, never falling along the last dimension, each value on 1 to 256 neighbouring positions
- valid: int32 [64, 512], P(('rep', 'shard')), may hold values from 0 to 1, as said below
Outputs:
- layer_output: bfloat16 [32768, 768], P(('rep', 'shard'))
- input_grad: bfloat16 [32768, 768], P(('rep', 'shard'))
- grad_qkv_weight: float32 [768, 2304], P('shard')
- grad_query_value_bias: float32 [2, 768], P(None, 'shard')
- grad_out_weight: float32 [768, 768], P('shard')
- grad_out_bias: float32 [768], P('shard')
- grad_norm_one_gain: float32 [768], P('shard')
- grad_norm_one_shift: float32 [768], P('shard')
- grad_up_weight: float32 [768, 3072], P('shard')
- grad_up_bias: float32 [3072], P('shard')
- grad_down_weight: float32 [3072, 768], P('shard')
- grad_down_bias: float32 [768], P('shard')
- grad_norm_two_gain: float32 [768], P('shard')
- grad_norm_two_shift: float32 [768], P('shard')
Inputs may be any that keep to these rules, and one draw needn't show every extreme that they name: `segment_ids`: within each sequence of 512 positions the numbers never fall; a document covers 1 to 256 positions, and one covers exactly 256. `valid`: in each sequence of 512 positions the tokens come first, followed by 0 to 64 padding positions.
All inputs are finite; a program needn't handle non-finite values.
Results may differ from a plain program's by a relative error of at most 0.015.
Values may be sent and summed in bfloat16 or wider, within the bound.
No kernel may reach another device: no remote copies, remote signals or barrier semaphores. Data moves between devices by JAX's collectives and lax.ppermute only.
A program may use at most 192 MiB of HBM per device.

v0:
```python
import jax
import jax.numpy as jnp
from jax import lax
from jax.sharding import PartitionSpec as P

HD = 64


def layer_norm(values, gain_vec, shift_vec):
    centre = values - jnp.mean(values, axis=-1, keepdims=True)
    spread = jnp.mean(centre * centre, axis=-1, keepdims=True)
    return centre * lax.rsqrt(spread + 1e-05) * gain_vec + shift_vec


def gelu_exact(values):
    return jax.nn.gelu(values, approximate=False)


def contract_rows(left_mat, right_mat):
    return lax.dot_general(
        left_mat, right_mat, (((0,), (0,)), ((), ())), preferred_element_type=jnp.float32
    )


def contract_cols(left_mat, right_mat):
    return lax.dot_general(
        left_mat, right_mat, (((1,), (1,)), ((), ())), preferred_element_type=jnp.float32
    )


def masked_scores(query_head, key_head, allowed):
    scores = contract_cols(query_head, key_head) * 0.125
    return jnp.where(allowed, scores, -1e30)


def forward_local(rows, seg_row, valid_row, weights):
    (
        qkv_weight,
        query_value_bias,
        out_weight,
        out_bias,
        norm_one_gain,
        norm_one_shift,
        up_weight,
        up_bias,
        down_weight,
        down_bias,
        norm_two_gain,
        norm_two_shift,
    ) = weights
    length, model_width = rows.shape
    heads = model_width // HD
    bias_all = jnp.concatenate(
        [
            query_value_bias[0].astype(jnp.float32),
            jnp.zeros((model_width,), jnp.float32),
            query_value_bias[1].astype(jnp.float32),
        ]
    )
    projected = (jnp.dot(rows, qkv_weight, preferred_element_type=jnp.float32) + bias_all).astype(
        jnp.bfloat16
    )
    split_heads = projected.reshape(length, 3, heads, HD).transpose(1, 2, 0, 3)
    allowed = (seg_row[:, None] == seg_row[None, :]) & (valid_row[:, None] == valid_row[None, :])

    def head_forward(packed):
        query_head, key_head, value_head = packed
        scores = masked_scores(query_head, key_head, allowed)
        row_top = jnp.max(scores, axis=-1, keepdims=True)
        shifted_exp = jnp.exp(scores - row_top)
        row_total = jnp.sum(shifted_exp, axis=-1, keepdims=True)
        probabilities = (shifted_exp / row_total).astype(jnp.bfloat16)
        attended = jnp.dot(probabilities, value_head, preferred_element_type=jnp.float32)
        return (attended.astype(jnp.bfloat16), row_top[:, 0] + jnp.log(row_total[:, 0]))

    attended, log_totals = lax.map(head_forward, (split_heads[0], split_heads[1], split_heads[2]))
    context = attended.transpose(1, 0, 2).reshape(length, model_width)
    pre_one = (
        rows.astype(jnp.float32)
        + jnp.dot(context, out_weight, preferred_element_type=jnp.float32)
        + out_bias.astype(jnp.float32)
    )
    normed = layer_norm(
        pre_one, norm_one_gain.astype(jnp.float32), norm_one_shift.astype(jnp.float32)
    )
    normed_low = normed.astype(jnp.bfloat16)
    hidden_pre = jnp.dot(
        normed_low, up_weight, preferred_element_type=jnp.float32
    ) + up_bias.astype(jnp.float32)
    hidden_low = gelu_exact(hidden_pre).astype(jnp.bfloat16)
    pre_two = (
        normed
        + jnp.dot(hidden_low, down_weight, preferred_element_type=jnp.float32)
        + down_bias.astype(jnp.float32)
    )
    result = layer_norm(
        pre_two, norm_two_gain.astype(jnp.float32), norm_two_shift.astype(jnp.float32)
    )
    stored = (
        split_heads,
        log_totals,
        context,
        pre_one,
        normed_low,
        hidden_pre,
        hidden_low,
        pre_two,
        allowed,
    )
    return (result.astype(jnp.bfloat16), stored)


def backward_local(rows, cot_rows, stored, weights):
    (
        qkv_weight,
        query_value_bias,
        out_weight,
        out_bias,
        norm_one_gain,
        norm_one_shift,
        up_weight,
        up_bias,
        down_weight,
        down_bias,
        norm_two_gain,
        norm_two_shift,
    ) = weights
    (
        split_heads,
        log_totals,
        context,
        pre_one,
        normed_low,
        hidden_pre,
        hidden_low,
        pre_two,
        allowed,
    ) = stored
    length, model_width = rows.shape
    heads = model_width // HD
    unused_two, norm_two_back = jax.vjp(
        layer_norm, pre_two, norm_two_gain.astype(jnp.float32), norm_two_shift.astype(jnp.float32)
    )
    grad_pre_two, grad_gain_two, grad_shift_two = norm_two_back(cot_rows.astype(jnp.float32))
    grad_down = grad_pre_two.astype(jnp.bfloat16)
    grad_down_weight = contract_rows(hidden_low, grad_down)
    grad_down_bias = jnp.sum(grad_down, axis=0, dtype=jnp.float32)
    grad_hidden = contract_cols(grad_down, down_weight)
    unused_gelu, gelu_back = jax.vjp(gelu_exact, hidden_pre)
    grad_up = gelu_back(grad_hidden)[0].astype(jnp.bfloat16)
    grad_up_weight = contract_rows(normed_low, grad_up)
    grad_up_bias = jnp.sum(grad_up, axis=0, dtype=jnp.float32)
    grad_normed = contract_cols(grad_up, up_weight) + grad_pre_two
    unused_one, norm_one_back = jax.vjp(
        layer_norm, pre_one, norm_one_gain.astype(jnp.float32), norm_one_shift.astype(jnp.float32)
    )
    grad_pre_one, grad_gain_one, grad_shift_one = norm_one_back(grad_normed)
    grad_branch = grad_pre_one.astype(jnp.bfloat16)
    grad_out_weight = contract_rows(context, grad_branch)
    grad_out_bias = jnp.sum(grad_branch, axis=0, dtype=jnp.float32)
    grad_context = contract_cols(grad_branch, out_weight).astype(jnp.bfloat16)
    grad_context = grad_context.reshape(length, heads, HD).transpose(1, 0, 2)

    def head_backward(packed):
        query_head, key_head, value_head, grad_head, log_total = packed
        scores = masked_scores(query_head, key_head, allowed)
        probabilities = jnp.exp(scores - log_total[:, None])
        prob_low = probabilities.astype(jnp.bfloat16)
        grad_value = contract_rows(prob_low, grad_head)
        grad_probs = contract_cols(grad_head, value_head)
        delta_row = jnp.sum(grad_probs * probabilities, axis=-1, keepdims=True)
        grad_scores = (probabilities * (grad_probs - delta_row)).astype(jnp.bfloat16)
        grad_query = jnp.dot(grad_scores, key_head, preferred_element_type=jnp.float32) * 0.125
        grad_key = contract_rows(grad_scores, query_head) * 0.125
        return jnp.stack([grad_query, grad_key, grad_value]).astype(jnp.bfloat16)

    head_grads = lax.map(
        head_backward, (split_heads[0], split_heads[1], split_heads[2], grad_context, log_totals)
    )
    grad_projected = head_grads.transpose(2, 1, 0, 3).reshape(length, 3 * model_width)
    grad_qkv_weight = contract_rows(rows, grad_projected)
    column_sums = jnp.sum(grad_projected, axis=0, dtype=jnp.float32)
    grad_query_value = jnp.stack([column_sums[:model_width], column_sums[2 * model_width :]])
    row_grad = (contract_cols(grad_projected, qkv_weight) + grad_pre_one).astype(jnp.bfloat16)
    new_grads = (
        grad_qkv_weight,
        grad_query_value,
        grad_out_weight,
        grad_out_bias,
        grad_gain_one,
        grad_shift_one,
        grad_up_weight,
        grad_up_bias,
        grad_down_weight,
        grad_down_bias,
        grad_gain_two,
        grad_shift_two,
    )
    return (row_grad, new_grads)


def shards(
    tokens,
    cotangent,
    qkv_weight,
    query_value_bias,
    out_weight,
    out_bias,
    norm_one_gain,
    norm_one_shift,
    up_weight,
    up_bias,
    down_weight,
    down_bias,
    norm_two_gain,
    norm_two_shift,
    segment_ids,
    valid,
):
    micro_count, length = segment_ids.shape
    results = []
    input_grads = []
    totals = None
    for micro_step in range(micro_count):
        row_start = micro_step * length
        rows = tokens[row_start : row_start + length]
        cot_rows = cotangent[row_start : row_start + length]
        forward_full = (
            lax.all_gather(qkv_weight, "shard", axis=0, tiled=True),
            lax.all_gather(query_value_bias, "shard", axis=1, tiled=True),
            lax.all_gather(out_weight, "shard", axis=0, tiled=True),
            lax.all_gather(out_bias, "shard", axis=0, tiled=True),
            lax.all_gather(norm_one_gain, "shard", axis=0, tiled=True),
            lax.all_gather(norm_one_shift, "shard", axis=0, tiled=True),
            lax.all_gather(up_weight, "shard", axis=0, tiled=True),
            lax.all_gather(up_bias, "shard", axis=0, tiled=True),
            lax.all_gather(down_weight, "shard", axis=0, tiled=True),
            lax.all_gather(down_bias, "shard", axis=0, tiled=True),
            lax.all_gather(norm_two_gain, "shard", axis=0, tiled=True),
            lax.all_gather(norm_two_shift, "shard", axis=0, tiled=True),
        )
        result, stored = forward_local(
            rows, segment_ids[micro_step], valid[micro_step], forward_full
        )
        backward_full = (
            lax.all_gather(qkv_weight, "shard", axis=0, tiled=True),
            lax.all_gather(query_value_bias, "shard", axis=1, tiled=True),
            lax.all_gather(out_weight, "shard", axis=0, tiled=True),
            lax.all_gather(out_bias, "shard", axis=0, tiled=True),
            lax.all_gather(norm_one_gain, "shard", axis=0, tiled=True),
            lax.all_gather(norm_one_shift, "shard", axis=0, tiled=True),
            lax.all_gather(up_weight, "shard", axis=0, tiled=True),
            lax.all_gather(up_bias, "shard", axis=0, tiled=True),
            lax.all_gather(down_weight, "shard", axis=0, tiled=True),
            lax.all_gather(down_bias, "shard", axis=0, tiled=True),
            lax.all_gather(norm_two_gain, "shard", axis=0, tiled=True),
            lax.all_gather(norm_two_shift, "shard", axis=0, tiled=True),
        )
        row_grad, new_grads = backward_local(rows, cot_rows, stored, backward_full)
        results.append(result)
        input_grads.append(row_grad)
        if totals is None:
            totals = new_grads
        else:
            totals = tuple((summed + added for summed, added in zip(totals, new_grads)))
    partial_sums = (
        lax.psum_scatter(totals[0], "shard", scatter_dimension=0, tiled=True),
        lax.psum_scatter(totals[1], "shard", scatter_dimension=1, tiled=True),
        lax.psum_scatter(totals[2], "shard", scatter_dimension=0, tiled=True),
        lax.psum_scatter(totals[3], "shard", scatter_dimension=0, tiled=True),
        lax.psum_scatter(totals[4], "shard", scatter_dimension=0, tiled=True),
        lax.psum_scatter(totals[5], "shard", scatter_dimension=0, tiled=True),
        lax.psum_scatter(totals[6], "shard", scatter_dimension=0, tiled=True),
        lax.psum_scatter(totals[7], "shard", scatter_dimension=0, tiled=True),
        lax.psum_scatter(totals[8], "shard", scatter_dimension=0, tiled=True),
        lax.psum_scatter(totals[9], "shard", scatter_dimension=0, tiled=True),
        lax.psum_scatter(totals[10], "shard", scatter_dimension=0, tiled=True),
        lax.psum_scatter(totals[11], "shard", scatter_dimension=0, tiled=True),
    )
    owned = (
        lax.psum(partial_sums[0].astype(jnp.bfloat16), "rep").astype(jnp.float32),
        lax.psum(partial_sums[1].astype(jnp.bfloat16), "rep").astype(jnp.float32),
        lax.psum(partial_sums[2].astype(jnp.bfloat16), "rep").astype(jnp.float32),
        lax.psum(partial_sums[3].astype(jnp.bfloat16), "rep").astype(jnp.float32),
        lax.psum(partial_sums[4].astype(jnp.bfloat16), "rep").astype(jnp.float32),
        lax.psum(partial_sums[5].astype(jnp.bfloat16), "rep").astype(jnp.float32),
        lax.psum(partial_sums[6].astype(jnp.bfloat16), "rep").astype(jnp.float32),
        lax.psum(partial_sums[7].astype(jnp.bfloat16), "rep").astype(jnp.float32),
        lax.psum(partial_sums[8].astype(jnp.bfloat16), "rep").astype(jnp.float32),
        lax.psum(partial_sums[9].astype(jnp.bfloat16), "rep").astype(jnp.float32),
        lax.psum(partial_sums[10].astype(jnp.bfloat16), "rep").astype(jnp.float32),
        lax.psum(partial_sums[11].astype(jnp.bfloat16), "rep").astype(jnp.float32),
    )
    return (
        jnp.concatenate(results, axis=0),
        jnp.concatenate(input_grads, axis=0),
        owned[0],
        owned[1],
        owned[2],
        owned[3],
        owned[4],
        owned[5],
        owned[6],
        owned[7],
        owned[8],
        owned[9],
        owned[10],
        owned[11],
    )


def solution(mesh):
    placed = (
        P(("rep", "shard"), None),
        P(("rep", "shard"), None),
        P("shard", None),
        P(None, "shard"),
        P("shard", None),
        P("shard"),
        P("shard"),
        P("shard"),
        P("shard", None),
        P("shard"),
        P("shard", None),
        P("shard"),
        P("shard"),
        P("shard"),
        P(("rep", "shard"), None),
        P(("rep", "shard"), None),
    )
    return jax.shard_map(
        shards,
        mesh=mesh,
        in_specs=placed,
        out_specs=(
            P(("rep", "shard"), None),
            P(("rep", "shard"), None),
            P("shard", None),
            P(None, "shard"),
            P("shard", None),
            P("shard"),
            P("shard"),
            P("shard"),
            P("shard", None),
            P("shard"),
            P("shard", None),
            P("shard"),
            P("shard"),
            P("shard"),
        ),
        check_vma=False,
    )
```

profile of v0, /device:TPU:0, one launch (start us, length us, event | category | flops | bytes accessed | tf_op | source)
XLA Modules:
  0.0 892.0 jit_solution(15511281130230347443)
XLA Ops:
  17.0 32.6 %all-reduce.14 = (bf16[768]{0:T(1024)(128)(2,1)S(1)}, bf16[768]{0:T(1024)(128)(2,1)S(1)}, bf16[768]{0:T(1024)(128)(2,1)S(1)}, bf16[768]{0:T(1024)(128)(2,1)S(1)}...) all-reduce(bf16[768]{0:T(1024)(128)(2,1)S(1)} %dynamic-update-slice, ...), channel_id=1, replica_groups=mesh['rep'=4,'shard'=8] {'shard'}, use_global_device_ids=true, to_apply=%add | all-reduce | flops 4608 | bytes 18432
  50.4 12.7 %all-gather.1 = bf16[8,1,384]{2,1,0:T(2,128)(2,1)S(1)} all-gather(bf16[1,1,384]{2,1,0:T(2,128)(2,1)S(1)} %reshape.366), channel_id=1, replica_groups=mesh['rep'=4,'shard'=8] {'shard'}, dimensions={0}, use_global_device_ids=true | all-gather | bytes 6912 | tf_op jit(solution)/shard_map/all_gather | solution.py:236
  63.1 9.0 %all-gather = bf16[8,96,2]{1,2,0:T(2,128)(2,1)S(1)} all-gather(bf16[1,96,2]{1,2,0:T(2,128)(2,1)} %bitcast.307), channel_id=1, replica_groups=mesh['rep'=4,'shard'=8] {'shard'}, dimensions={0}, use_global_device_ids=true | all-gather | bytes 3456 | tf_op jit(solution)/shard_map/all_gather | solution.py:230
  73.9 5.7 fusion.105
  89.9 30.0 %while.49 = (s32[]{:T(128)}, bf16[12,512,64]{1,2,0:T(8,128)(2,1)}, f32[12,512]{1,0:T(8,128)S(1)}, bf16[12,512,64]{2,1,0:T(8,128)(2,1)S(1)}, bf16[12,512,64]{2,1,...) while((s32[]{:T(128)}, bf16[12,512,64]{1,2,0:T(8,128)(2,1)}, ...), condition=%wide.region_11.12_spmd.clone, body=%wide.region_8.11_spmd.clone.sunk | while | flops 70024704 | bytes 3635313 | solution.py:76
  142.8 40.9 %while.48 = (s32[]{:T(128)}, bf16[12,512,64]{1,2,0:T(8,128)(2,1)}, f32[12,512]{1,0:T(8,128)S(1)}, bf16[12,512,64]{2,1,0:T(8,128)(2,1)S(1)}, bf16[12,512,64]{2,1,...) while((s32[]{:T(128)}, bf16[12,512,64]{1,2,0:T(8,128)(2,1)}, ...), condition=%wide.region_3.4_spmd.clone, body=%wide.region_0.3_spmd.clone.sunk | while | flops 70024704 | bytes 3635313 | solution.py:76
  195.6 35.1 %multiply_convert_fusion.3 = (bf16[512,3072]{1,0:T(8,128)(2,1)}, f32[512,3072]{1,0:T(8,128)}, bf16[512,3072]{1,0:T(8,128)(2,1)}, f32[512,3072]{1,0:T(8,128)}, f32[512,3072]{1,0:T(8,128)}) fusion(f32[3072]{0:T(1024)S(1)} %bitcast.301, f32[512,3072]{1,0:T(8,128)S(1)} %fusion.128, bf16[768,3072]{1,0:T(8,128)(2,1)S(1)} %copy-done.33, ...), kind=kOutput, calls=%fused_computation.136 | convolution fusion | flops 2625503232 | bytes 37771264 | tf_op jit(solution)/shard_map/dot_general | solution.py:87
  230.7 6.2 fusion.149
  251.6 17.8 %convert_reduce_fusion.1 = (f32[3072]{0:T(1024)S(1)}, bf16[512,3072]{1,0:T(8,128)(2,1)}, f32[3072]{0:T(1024)S(1)}, bf16[512,3072]{1,0:T(8,128)(2,1)}) fusion(f32[512,3072]{1,0:T(8,128)} %get-tuple-element.508, f32[512,3072]{1,0:T(8,128)} %get-tuple-element.553, f32[3072]{0:T(1024)S(1)} %bitcast.302, f32[512,3072]{1,0:T(8,128)} %fusion.151, ...), kind=kOutput, calls=%fused_computation.120 | convolution fusion | flops 2469390336 | bytes 43290624 | tf_op jit(solution)/shard_map/dot_general | solution.py:26
  269.4 6.5 add_add_fusion.8
  275.9 5.8 multiply_reduce_fusion.3
  288.0 85.9 %while.51 = (s32[]{:T(128)}, bf16[12,3,512,64]{2,3,0,1:T(8,128)(2,1)S(1)}, bf16[12,512,64]{2,1,0:T(8,128)(2,1)}, bf16[12,512,64]{2,1,0:T(8,128)(2,1)}, f32[12,51...) while((s32[]{:T(128)}, ...), condition=%wide.region_29.30_spmd.clone, body=%wide.region_27.29_spmd.clone.sunk | while | flops 171671040 | bytes 9261185 | solution.py:177
  387.9 93.5 %while.50 = (s32[]{:T(128)}, bf16[12,3,512,64]{2,3,0,1:T(8,128)(2,1)}, bf16[12,512,64]{2,1,0:T(8,128)(2,1)}, bf16[12,512,64]{2,1,0:T(8,128)(2,1)}, f32[12,512]{1...) while((s32[]{:T(128)}, ...), condition=%wide.region_22.23_spmd.clone, body=%wide.region_20.22_spmd.clone.sunk | while | flops 171671040 | bytes 9261185 | solution.py:177
  490.3 8.0 copy.79
  498.4 5.4 fusion.130
  503.9 6.1 convolution_add_fusion.1
  510.0 5.0 fusion.153
  515.1 5.3 convolution_add_fusion
  526.0 49.0 %reduce-scatter.16.cloned.1.call-done = f32[96,2304]{1,0:T(8,128)} async-done(((f32[768,2304]{1,0:T(8,128)}), f32[96,2304]{1,0:T(8,128)}) %reduce-scatter.16.cloned.1.call-update) | async-done | bytes 884752
  577.2 98.0 %reduce-scatter.12.cloned.1.call-done = f32[96,3072]{1,0:T(8,128)} async-done(((f32[768,3072]{1,0:T(8,128)}), f32[96,3072]{1,0:T(8,128)}) %reduce-scatter.12.cloned.1.call-update) | async-done | bytes 1179664 | tf_op jit(solution)/shard_map/reduce_scatter | solution.py:273
  677.4 98.1 %reduce-scatter.14.cloned.1.call-done = f32[384,768]{1,0:T(8,128)} async-done(((f32[3072,768]{1,0:T(8,128)}), f32[384,768]{1,0:T(8,128)}) %reduce-scatter.14.cloned.1.call-update) | async-done | bytes 1179664 | tf_op jit(solution)/shard_map/reduce_scatter | solution.py:275
  779.0 26.5 %all-reduce.13 = (bf16[768]{0:T(1024)(128)(2,1)S(1)}, bf16[768]{0:T(1024)(128)(2,1)S(1)}, bf16[768]{0:T(1024)(128)(2,1)S(1)}, bf16[3072]{0:T(1024)(128)(2,1)S(1)...) all-reduce(f32[768]{0:T(1024)S(1)} %add.311, ...), channel_id=5, replica_groups=mesh['rep'=4,'shard'=8] {'shard'}, use_global_device_ids=true, to_apply=%region_40.41.clone | all-reduce | flops 7680 | bytes 46080
  816.9 10.9 %all-reduce.15 = (bf16[2,96]{1,0:T(2,128)(2,1)S(1)}, bf16[96]{0:T(256)(128)(2,1)S(1)}, bf16[96]{0:T(256)(128)(2,1)S(1)}, bf16[96]{0:T(256)(128)(2,1)S(1)}, bf16[...) all-reduce(bf16[2,96]{1,0:T(2,128)(2,1)S(1)} %copy.82, ...), channel_id=1, replica_groups=mesh['rep'=4,'shard'=8] {'rep'}, use_global_device_ids=true, to_apply=%region_35.36 | all-reduce | flops 1152 | bytes 4608 | tf_op jit(solution)/shard_map/psum | solution.py:282
  832.0 45.6 %all-reduce.19.cloned.1.call-done = (bf16[96,2304]{0,1:T(8,128)(2,1)}, bf16[96,768]{1,0:T(8,128)(2,1)}, bf16[96,3072]{1,0:T(8,128)(2,1)}, bf16[384,768]{1,0:T(8,128)(2,1)}) async-done(((bf16[96,2304]{0,1:T(8,128)(2,1)}, bf16[96,768]{1,0:T(8,128)(2,1)}, bf16[96,3072]{1,0:T(8,128)(2,1)}, bf16[384,768]{1,0:T(8,128)(2,1)}), (bf16[96,2304]{0,1:T(8,128)(2,1)}, bf16[96,768]{1,0:T(8,128)(2,1)}, ...) | async-done | bytes 1769488 | tf_op jit(solution)/shard_map/psum | solution.py:281
  (551 shorter events, 383.5 us)
Async XLA Ops:
  7.2 66.7 %all-gather.7.cloned.1.call-start = ((), (), s32[]{:S(2)}) async-start(), calls=%async_computation.5 | async-start | bytes 3981312 | tf_op jit(solution)/shard_map/all_gather | solution.py:229
  7.9 112.1 %all-gather.9.cloned.1.call-start = ((), (), s32[]{:S(2)}) async-start(), calls=%async_computation.6 | async-start | bytes 1327104 | tf_op jit(solution)/shard_map/all_gather | solution.py:231
  8.7 179.4 %all-gather.11.cloned.1.call-start = ((), (), s32[]{:S(2)}) async-start(), calls=%async_computation.7 | async-start | bytes 5308416 | tf_op jit(solution)/shard_map/all_gather | solution.py:235
  9.4 221.3 %all-gather.13.cloned.1.call-start = ((), (), s32[]{:S(2)}) async-start(), calls=%async_computation.8 | async-start | bytes 5308416 | tf_op jit(solution)/shard_map/all_gather | solution.py:237
  10.0 514.4 %reduce-scatter.10.cloned.1.call-start = ((), (), s32[]{:S(2)}) async-start(), calls=%async_computation.9 | async-start | bytes 2654208 | tf_op jit(solution)/shard_map/reduce_scatter | solution.py:269
  123.9 157.8 %copy-start.1 = (f32[512,768]{1,0:T(8,128)}, f32[512,768]{1,0:T(8,128)S(1)}, u32[]{:S(2)}) copy-start(f32[512,768]{1,0:T(8,128)S(1)} %get-tuple-element.552) | copy-start | bytes 4718596
  187.7 94.1 %copy-start.4 = (f32[512,768]{1,0:T(8,128)}, f32[512,768]{1,0:T(8,128)S(1)}, u32[]{:S(2)}) copy-start(f32[512,768]{1,0:T(8,128)S(1)} %get-tuple-element.550) | copy-start | bytes 4718596
  188.0 7.5 copy-start.33
  230.7 6.5 copy-start.34
  230.7 6.5 copy-start.39
  245.5 6.0 copy-start.16
  269.4 6.5 copy-start.41
  275.9 5.8 copy-start.24
  386.1 188.8 %reduce-scatter.16.cloned.1.call-start = ((), (), s32[]{:S(2)}) async-start(), calls=%async_computation.12 | async-start | bytes 7962624
  498.3 176.9 %reduce-scatter.12.cloned.1.call-start = ((), (), s32[]{:S(2)}) async-start(), calls=%async_computation.10 | async-start | bytes 10616832 | tf_op jit(solution)/shard_map/reduce_scatter | solution.py:273
  498.4 5.5 copy-start.2
  498.4 5.5 copy-start.13
  509.9 5.1 copy-start.17
  510.0 265.5 %reduce-scatter.14.cloned.1.call-start = ((), (), s32[]{:S(2)}) async-start(), calls=%async_computation.11 | async-start | bytes 10616832 | tf_op jit(solution)/shard_map/reduce_scatter | solution.py:275
  510.0 5.1 copy-start.3
  520.4 295.6 %reduce-scatter.18.cloned.1.call-start = ((), (), s32[]{:S(2)}) async-start(), calls=%async_computation.13 | async-start | bytes 442368
  524.3 353.3 %all-reduce.19.cloned.1.call-start = ((), (), s32[]{:S(2)}) async-start(), calls=%async_computation.14 | async-start | bytes 3833856 | tf_op jit(solution)/shard_map/psum | solution.py:281
  677.4 128.7 %copy-start.15 = (bf16[512,768]{1,0:T(8,128)(2,1)S(1)}, bf16[512,768]{1,0:T(8,128)(2,1)}, u32[]{:S(2)}) copy-start(bf16[512,768]{1,0:T(8,128)(2,1)} %get-tuple-element.526) | copy-start | bytes 2359300
  877.6 6.1 copy-start.20
  (28 other events, 78.8 us)
Sparse Core Ops, SparseCore 0:
  9.6 44.7 all-gather.6
  56.1 21.6 all-gather.8
  79.4 50.8 all-gather.10
  131.8 49.9 all-gather.12
  386.3 36.3 reduce-scatter.9
  498.5 76.4 reduce-scatter.15
  577.3 97.8 reduce-scatter.11
  677.5 97.8 reduce-scatter.13
  777.7 29.7 reduce-scatter.17
  812.0 65.5 all-reduce.18
where the time goes:
time: 907 us; the launch traced here: 892 us
  matrix products  355 us (39%)
  waiting for transfers between devices  293 us (32%)
  blocking collectives  91.8 us (10%)
  local copies, waits for them, and re-layouts  80.6 us (9%)
  other arithmetic  51.6 us (6%)
  between operations  17.4 us (2%)
    dot_general x80, matrix products, contract_cols(): lax.dot_general(left_mat, right_mat, (((1,), (1,)), ((), ())), preferred_...  126 us
    reduce_scatter x1, waiting for transfers between devices, shards(): lax.psum_scatter(totals[8], 'shard', scatter_dimension=0, tiled=True)  98.1 us
    reduce_scatter x1, waiting for transfers between devices, shards(): lax.psum_scatter(totals[6], 'shard', scatter_dimension=0, tiled=True)  98 us
    dot_general x56, matrix products, contract_rows(): lax.dot_general(left_mat, right_mat, (((0,), (0,)), ((), ())), preferred_...  92.9 us
    unnamed x2, blocking collectives  59.2 us
    unnamed x12, waiting for transfers between devices  51.7 us
    psum x1, waiting for transfers between devices, shards(): lax.psum(partial_sums[0].astype(jnp.bfloat16), 'rep').astype(jnp.float32)  45.6 us
    dot_general x24, matrix products, head_forward(): jnp.dot(probabilities, value_head, preferred_element_type=jnp.float32)  44.3 us
  transfers between devices with their start and end apart: 10, of which 4 were waited for; matrix products, arithmetic and copies ran while one was open for 36% of the time, Pallas kernels for 0%

commit v1 on v0

v1 whole, which is shorter than its diff:
```python
import jax
import jax.numpy as jnp
from jax import lax
from jax.experimental import pallas as pl
from jax.experimental.pallas import tpu as pltpu
from jax.sharding import PartitionSpec as P

HD = 64
GW = 256
SCALE = 0.125 * 1.4426950408889634
BIG = 1e30
VMEM_LIMIT = 60 * 1024 * 1024
bf16 = jnp.bfloat16
f32 = jnp.float32


def nn(a, b):
    return lax.dot_general(a, b, (((1,), (0,)), ((), ())), preferred_element_type=f32)


def nt(a, b):
    return lax.dot_general(a, b, (((1,), (1,)), ((), ())), preferred_element_type=f32)


def tn(a, b):
    return lax.dot_general(a, b, (((0,), (0,)), ((), ())), preferred_element_type=f32)


def attend_kernel(tok, wq, wk, wv, bq, bv, aq, ak, q_o, k_o, v_o, ctx_o, lse_o):
    x = tok[...]
    q = (nn(x, wq[...]) + bq[...].astype(f32)).astype(bf16)
    k = nn(x, wk[...]).astype(bf16)
    v = (nn(x, wv[...]) + bv[...].astype(f32)).astype(bf16)
    q_o[...] = q
    k_o[...] = k
    v_o[...] = v
    length, width = q.shape
    lane = lax.broadcasted_iota(jnp.int32, (length, width), 1) // HD
    slot = lax.broadcasted_iota(jnp.int32, (length, 128), 1)
    acc = None
    scale = jnp.zeros((length, width), f32)
    stat = jnp.zeros((length, 128), f32)
    for h in range(width // HD):
        mine = lane == h
        qa = jnp.where(mine, q, aq[...])
        ka = jnp.where(mine, k, ak[...])
        va = jnp.where(mine, v, jnp.zeros_like(v))
        t = nt(qa, ka) * SCALE
        m = jnp.max(t, axis=1, keepdims=True)
        p = jnp.exp2(t - m)
        total = jnp.sum(p, axis=1, keepdims=True)
        part = nn(p.astype(bf16), va)
        acc = part if acc is None else acc + part
        scale = jnp.where(mine, 1.0 / total, scale)
        stat = jnp.where(slot == h, m + jnp.log2(total), stat)
    ctx_o[...] = (acc * scale).astype(bf16)
    lse_o[0, 0] = stat.T[:8]


def attend(tokens, w, bias, aq, ak, length):
    rows, width = tokens.shape
    groups = width // GW
    seqs = rows // length
    col = lambda o: pl.BlockSpec((width, GW), lambda g, b: (0, o * groups + g))
    bcol = lambda o: pl.BlockSpec((1, GW), lambda g, b: (0, o * groups + g))
    seq = pl.BlockSpec((length, width), lambda g, b: (b, 0))
    aug = pl.BlockSpec((length, GW), lambda g, b: (b, 0))
    blk = pl.BlockSpec((length, GW), lambda g, b: (b, g))
    act = jax.ShapeDtypeStruct((rows, width), bf16)
    return pl.pallas_call(
        attend_kernel,
        grid=(groups, seqs),
        in_specs=[seq, col(0), col(1), col(2), bcol(0), bcol(1), aug, aug],
        out_specs=[blk, blk, blk, blk, pl.BlockSpec((1, 1, 8, length), lambda g, b: (b, g, 0, 0))],
        out_shape=[act, act, act, act, jax.ShapeDtypeStruct((seqs, groups, 8, length), f32)],
        compiler_params=pltpu.CompilerParams(vmem_limit_bytes=VMEM_LIMIT),
        name="attend",
    )(tokens, w, w, w, bias, bias, aq, ak)


def attend_back_kernel(q_r, k_r, v_r, do_r, ctx_r, lse_r, aq, ak, tok, wq, wk, wv, gb, dw_o, db_o, dx_o, dw_s, dx_s):
    g, b = pl.program_id(0), pl.program_id(1)
    q, k, v, do = q_r[...], k_r[...], v_r[...], do_r[...]
    length, width = q.shape
    lane = lax.broadcasted_iota(jnp.int32, (length, width), 1) // HD
    sel = lax.broadcasted_iota(jnp.int32, (8, width), 1) // HD == lax.broadcasted_iota(jnp.int32, (8, width), 0)
    sel = sel.astype(f32).astype(bf16)
    prod = do.astype(f32) * ctx_r[...].astype(f32)
    hi = prod.astype(bf16)
    lo = (prod - hi.astype(f32)).astype(bf16)
    delta = nt(sel, hi) + nt(sel, lo)
    dq = dk = dv = None
    zero = jnp.zeros_like(q)
    for h in range(width // HD):
        mine = lane == h
        qa = jnp.where(mine, q, aq[...])
        ka = jnp.where(mine, k, ak[...])
        va = jnp.where(mine, v, zero)
        p = jnp.exp2(nt(ka, qa) * SCALE - lse_r[0, 0, h : h + 1, :])
        dp = nt(va, do)
        ds = (p * (dp - delta[h : h + 1, :])).astype(bf16)
        dv_h = nn(p.astype(bf16), jnp.where(mine, do, zero))
        dk_h = nn(ds, jnp.where(mine, q, zero))
        dq_h = tn(ds, jnp.where(mine, k, zero))
        dv = dv_h if dv is None else dv + dv_h
        dk = dk_h if dk is None else dk + dk_h
        dq = dq_h if dq is None else dq + dq_h
    dq = (dq * 0.125).astype(bf16)
    dk = (dk * 0.125).astype(bf16)
    dv = dv.astype(bf16)
    back = jnp.concatenate([dq, dk, dv], axis=1)
    dw = tn(tok[...], back)
    dx = nt(dq, wq[...]) + nt(dk, wk[...]) + nt(dv, wv[...])
    sums = jnp.sum(back.astype(f32), axis=0, keepdims=True)

    @pl.when(b == 0)
    def _():
        dw_s[...] = dw
        db_o[0] = sums

    @pl.when(b > 0)
    def _():
        dw_s[...] += dw
        db_o[0] += sums

    @pl.when(g == 0)
    def _():
        dx_s[b] = dx + gb[...].astype(f32)

    @pl.when(g > 0)
    def _():
        dx_s[b] += dx

    @pl.when(b == pl.num_programs(1) - 1)
    def _():
        for i in range(3):
            dw_o[i] = dw_s[:, i * width : (i + 1) * width].astype(bf16)

    @pl.when(g == pl.num_programs(0) - 1)
    def _():
        dx_o[...] = dx_s[b].astype(bf16)


def attend_back(q, k, v, do, ctx, lse, aq, ak, tokens, w, gb, length):
    rows, width = tokens.shape
    groups = width // GW
    seqs = rows // length
    col = lambda o: pl.BlockSpec((width, GW), lambda g, b: (0, o * groups + g))
    seq = pl.BlockSpec((length, width), lambda g, b: (b, 0))
    aug = pl.BlockSpec((length, GW), lambda g, b: (b, 0))
    blk = pl.BlockSpec((length, GW), lambda g, b: (b, g))
    return pl.pallas_call(
        attend_back_kernel,
        grid=(groups, seqs),
        in_specs=[blk, blk, blk, blk, blk, pl.BlockSpec((1, 1, 8, length), lambda g, b: (b, g, 0, 0)), aug, aug, seq,
                  col(0), col(1), col(2), seq],
        out_specs=[
            pl.BlockSpec((3, width, GW), lambda g, b: (0, 0, g)),
            pl.BlockSpec((1, 1, 3 * GW), lambda g, b: (g, 0, 0)),
            pl.BlockSpec((length, width), lambda g, b: (jnp.where(g == groups - 1, b, 0), 0)),
        ],
        out_shape=[
            jax.ShapeDtypeStruct((3, width, width), bf16),
            jax.ShapeDtypeStruct((groups, 1, 3 * GW), f32),
            jax.ShapeDtypeStruct((rows, width), bf16),
        ],
        scratch_shapes=[pltpu.VMEM((width, 3 * GW), f32), pltpu.VMEM((seqs, length, width), f32)],
        compiler_params=pltpu.CompilerParams(vmem_limit_bytes=VMEM_LIMIT),
        name="attend_back",
    )(q, k, v, do, ctx, lse, aq, ak, tokens, w, w, w, gb)


def masks(segment_ids, valid):
    code = (segment_ids + 8 * valid).reshape(-1, 1)
    lane = lax.broadcasted_iota(jnp.int32, (1, GW), 1) % HD
    same = code == lane
    aq = same.astype(bf16)
    ak = jnp.where((lane < 16) & ~same, -BIG, 0.0).astype(bf16)
    return aq, ak


def phi(x):
    return 0.5 * (1.0 + lax.erf(x * 0.7071067811865476)), jnp.exp(-0.5 * x * x) * 0.3989422804014327


def middle_kernel(tok, ctx, cot, wo, bo, g1, s1, wu, bu, wd, bd, g2, s2,
                  out_o, low_o, hid_o, gd_o, gu_o, gb_o, gc_o, vec_o, bup_o, slope):
    i = pl.program_id(0)
    width = tok.shape[1]
    ff = wu.shape[1]
    step = width
    chunks = ff // step
    row = lambda r: r[...].astype(f32)
    pre = tok[...].astype(f32) + nn(ctx[...], wo[...]) + row(bo)
    mean = lambda v: jnp.mean(v, axis=1, keepdims=True)
    centre = pre - mean(pre)
    r1 = lax.rsqrt(mean(centre * centre) + 1e-05)
    n1 = centre * r1
    normed = n1 * row(g1) + row(s1)
    low = normed.astype(bf16)
    low_o[...] = low
    acc = normed + row(bd)
    for c in range(chunks):
        cols = slice(c * step, (c + 1) * step)
        hp = nn(low, wu[:, cols]) + bu[:, cols].astype(f32)
        cdf, pdf = phi(hp)
        slope[:, cols] = cdf + hp * pdf
        hid = (hp * cdf).astype(bf16)
        hid_o[:, cols] = hid
        acc = acc + nn(hid, wd[cols, :])
    centre = acc - mean(acc)
    r2 = lax.rsqrt(mean(centre * centre) + 1e-05)
    n2 = centre * r2
    out_o[...] = (n2 * row(g2) + row(s2)).astype(bf16)
    ct = cot[...].astype(f32)
    e = ct * row(g2)
    gp2 = r2 * (e - mean(e) - n2 * mean(e * n2))
    gd = gp2.astype(bf16)
    gd_o[...] = gd
    acc = gp2
    total = lambda v: jnp.sum(v, axis=0, keepdims=True)

    def put(ref, at, v):
        @pl.when(i == 0)
        def _():
            ref[at] = v

        @pl.when(i > 0)
        def _():
            ref[at] += v

    for c in range(chunks):
        cols = slice(c * step, (c + 1) * step)
        gu = (nt(gd, wd[cols, :]) * slope[:, cols]).astype(bf16)
        gu_o[:, cols] = gu
        put(bup_o, (slice(0, 1), cols), total(gu.astype(f32)))
        acc = acc + nt(gu, wu[:, cols])
    e = acc * row(g1)
    gp1 = r1 * (e - mean(e) - n1 * mean(e * n1))
    gb = gp1.astype(bf16)
    gb_o[...] = gb
    gc_o[...] = nt(gb, wo[...]).astype(bf16)
    for at, v in enumerate((gb.astype(f32), acc * n1, acc, gd.astype(f32), ct * n2, ct)):
        put(vec_o, (slice(at, at + 1), slice(None)), total(v))


def middle(tokens, ctx, cot, wo, bo, g1, s1, wu, bu, wd, bd, g2, s2, tile=256):
    rows, width = tokens.shape
    ff = wu.shape[1]
    act = pl.BlockSpec((tile, width), lambda i: (i, 0))
    wide = pl.BlockSpec((tile, ff), lambda i: (i, 0))
    whole = lambda a: pl.BlockSpec(a.shape, lambda i: (0, 0), pipeline_mode=pl.Buffered(1))
    S = jax.ShapeDtypeStruct
    return pl.pallas_call(
        middle_kernel,
        grid=(rows // tile,),
        in_specs=[act, act, act] + [whole(a) for a in (wo, bo, g1, s1, wu, bu, wd, bd, g2, s2)],
        out_specs=[act, act, wide, act, wide, act, act, pl.BlockSpec((8, width), lambda i: (0, 0)), pl.BlockSpec((8, ff), lambda i: (0, 0))],
        out_shape=[S((rows, width), bf16), S((rows, width), bf16), S((rows, ff), bf16), S((rows, width), bf16), S((rows, ff), bf16),
                   S((rows, width), bf16), S((rows, width), bf16), S((8, width), f32), S((8, ff), f32)],
        scratch_shapes=[pltpu.VMEM((tile, ff), f32)],
        compiler_params=pltpu.CompilerParams(vmem_limit_bytes=VMEM_LIMIT),
        name="middle",
    )(tokens, ctx, cot, wo, bo, g1, s1, wu, bu, wd, bd, g2, s2)


def spread(args):
    flat = [a.reshape(-1) for a in args]
    packed = jnp.concatenate(flat)
    every = lax.all_gather(packed, "shard", axis=0)
    out, at = [], 0
    for a in args:
        part = every[:, at : at + a.size].reshape((-1,) + a.shape)
        at += a.size
        out.append(jnp.moveaxis(part, 0, -2).reshape(a.shape[:-1] + (-1,)))
    return out


def shards(
    tokens,
    cotangent,
    qkv_weight,
    query_value_bias,
    out_weight,
    out_bias,
    norm_one_gain,
    norm_one_shift,
    up_weight,
    up_bias,
    down_weight,
    down_bias,
    norm_two_gain,
    norm_two_shift,
    segment_ids,
    valid,
):
    length = segment_ids.shape[1]
    width = tokens.shape[1]
    groups = width // GW
    gather = lambda a: lax.all_gather(a, "shard", axis=0, tiled=True)
    bqv, bo, g1, s1, bu, bd, g2, s2 = spread(
        (query_value_bias, out_bias, norm_one_gain, norm_one_shift, up_bias, down_bias, norm_two_gain, norm_two_shift)
    )
    wqkv, wo, wu, wd = gather(qkv_weight), gather(out_weight), gather(up_weight), gather(down_weight)
    bias = bqv.reshape(1, -1)
    aq, ak = masks(segment_ids, valid)
    q, k, v, ctx, lse = attend(tokens, wqkv, bias, aq, ak, length)
    result, low, hid, gd, gu, gb, gc, vec, bup = middle(
        tokens, ctx, cotangent, wo, bo[None], g1[None], s1[None], wu, bu[None], wd, bd[None], g2[None], s2[None]
    )
    dwd = tn(hid, gd).astype(bf16)
    dwu = tn(low, gu).astype(bf16)
    dwo = tn(ctx, gb).astype(bf16)
    dw, db, dx = attend_back(q, k, v, gc, ctx, lse, aq, ak, tokens, wqkv, gb, length)
    dwq = jnp.concatenate([dw[0], dw[1], dw[2]], axis=1)
    db = db.reshape(groups, 3, GW).transpose(1, 0, 2).reshape(3, width)
    small = jnp.concatenate([db[0], db[2], vec[:6].reshape(-1), bup[0]])
    small = lax.psum(small.reshape(-1, 128), ("rep", "shard")).reshape(-1)

    def owned(a):
        part = lax.psum_scatter(a, "shard", scatter_dimension=0, tiled=True)
        return lax.psum(part, "rep").astype(f32)

    rank = lax.axis_index("shard")
    own = lambda at, size: lax.dynamic_slice(small, (at + rank * size,), (size,))
    piece = out_bias.shape[0]
    vecs = [own(width * i, piece) for i in range(8)]
    dbu = own(8 * width, up_bias.shape[0])
    gd_w, gu_w, go_w, gq_w = owned(dwd), owned(dwu), owned(dwo), owned(dwq)
    return (
        result,
        dx,
        gq_w,
        jnp.stack([vecs[0], vecs[1]]),
        go_w,
        vecs[2],
        vecs[3],
        vecs[4],
        gu_w,
        dbu,
        gd_w,
        vecs[5],
        vecs[6],
        vecs[7],
    )


def solution(mesh):
    rows, one = P(("rep", "shard"), None), P("shard")
    mat, two = P("shard", None), P(None, "shard")
    return jax.shard_map(
        shards,
        mesh=mesh,
        in_specs=(rows, rows, mat, two, mat, one, one, one, mat, one, mat, one, one, one, rows, rows),
        out_specs=(rows, rows, mat, two, mat, one, one, one, mat, one, mat, one, one, one),
        check_vma=False,
    )
```

time: 907 us -> 499 us (0.55); the launches traced: 892 us -> 498 us
  matrix products: 355 us -> 23.2 us
  Pallas kernels: 0 us -> 96 us
  local copies, waits for them, and re-layouts: 80.6 us -> 13 us
  other arithmetic: 51.6 us -> 9.66 us
  blocking collectives: 91.8 us -> 54.5 us
    dot_general x192 -> x3, matrix products: 355 us -> 23.2 us  [tn(): lax.dot_general(a, b, (((0,), (0,)), ((), ())), preferred_element_type=f32)]
    all_gather x4, waiting for transfers between devices: 0.06 us -> 128 us  [shards(): gather = lambda a: lax.all_gather(a, 'shard', axis=0, tiled=True)]
    pallas_call x0 -> x3, Pallas kernels: none -> 96 us  [the longest x1 43 us: middle(): pl.pallas_call(middle_kernel, grid=(rows // tile,), in_specs=[act, act, a...]
    reduce_scatter x3 -> x4, waiting for transfers between devices: 196 us -> 132 us  [owned(): part = lax.psum_scatter(a, 'shard', scatter_dimension=0, tiled=True)]
    unnamed x2 -> x0, blocking collectives: 59.2 us -> none
    unnamed x12 -> x9, waiting for transfers between devices: 51.7 us -> 2.66 us
    unnamed x117 -> x41, local copies, waits for them, and re-layouts: 41.6 us -> 3.46 us
    psum x1, blocking collectives: 10.9 us -> 38.6 us  [shards(): small = lax.psum(small.reshape(-1, 128), ('rep', 'shard')).reshape(-1)]
  transfers between devices with their start and end apart: 10 -> 9, of which waited for: 4 -> 8; matrix products, arithmetic and copies ran while one was open for 36% -> 7% of each run, Pallas kernels for 0% -> 11%
where the time goes in v1:
time: 499 us; the launch traced here: 498 us
  waiting for transfers between devices  287 us (58%)
  Pallas kernels  96 us (19%)
  blocking collectives  54.5 us (11%)
  matrix products  23.2 us (5%)
  between operations  14.1 us (3%)
  local copies, waits for them, and re-layouts  13 us (3%)
  other arithmetic  9.66 us (2%)
    reduce_scatter x4, waiting for transfers between devices, owned(): part = lax.psum_scatter(a, 'shard', scatter_dimension=0, tiled=True)  132 us
    all_gather x4, waiting for transfers between devices, shards(): gather = lambda a: lax.all_gather(a, 'shard', axis=0, tiled=True)  128 us
    pallas_call x1, Pallas kernels, middle(): pl.pallas_call(middle_kernel, grid=(rows // tile,), in_specs=[act, act, a...  43 us
    psum x1, blocking collectives, shards(): small = lax.psum(small.reshape(-1, 128), ('rep', 'shard')).reshape(-1)  38.6 us
    pallas_call x1, Pallas kernels, attend_back(): pl.pallas_call(attend_back_kernel, grid=(groups, seqs), in_specs=[blk, bl...  33.8 us
    psum x1, waiting for transfers between devices, owned(): return lax.psum(part, 'rep').astype(f32)  24.8 us
    dot_general x3, matrix products, tn(): lax.dot_general(a, b, (((0,), (0,)), ((), ())), preferred_element_type=f32)  23.2 us
    pallas_call x1, Pallas kernels, attend(): pl.pallas_call(attend_kernel, grid=(groups, seqs), in_specs=[seq, col(0),...  19.1 us
  transfers between devices with their start and end apart: 9, of which 8 were waited for; matrix products, arithmetic and copies ran while one was open for 7% of the time, Pallas kernels for 11%

profile of v1, /device:TPU:0, one launch (start us, length us, event | category | flops | bytes accessed | tf_op | source)
XLA Modules:
  0.0 498.2 jit_solution(15481570142682949563)
XLA Ops:
  10.4 15.9 %all-gather.1 = bf16[8,1,1152]{2,1,0:T(2,128)(2,1)S(1)} all-gather(bf16[1,1,1152]{2,1,0:T(2,128)(2,1)S(1)} %reshape.79), channel_id=2, replica_groups=mesh['rep'=4,'shard'=8] {'shard'}, dimensions={0}, use_global_device_ids=true | all-gather | bytes 20736 | tf_op jit(solution)/shard_map/all_gather | solution.py:270
  31.9 1.0 compare_convert_fusion.aq
  32.9 1.1 select_convert_fusion.ak
  34.0 20.0 %all-gather.7.cloned.1.call-done.wq.wk.wv = bf16[768,2304]{1,0:T(8,128)(2,1)} async-done(((bf16[96,2304]{1,0:T(8,128)(2,1)}), bf16[768,2304]{1,0:T(8,128)(2,1)}) %all-gather.7.cloned.1.call-update) | async-done | bytes 3538960 | tf_op jit(solution)/shard_map/all_gather | solution.py:300
  54.0 19.1 %attend.1 = (bf16[1024,768]{1,0:T(8,128)(2,1)}, bf16[1024,768]{1,0:T(8,128)(2,1)}, bf16[1024,768]{1,0:T(8,128)(2,1)}, bf16[1024,768]{1,0:T(8,128)(2,1)}, f32[2,3,8,512]{3,2,1,0:T(8,128)}) custom-call(bf16[1024,768]{1,0:T(8,128)(2,1)} %tok.5, bf16[768,2304]{1,0:T(8,128)(2,1)} %all-gather.7.cloned.1.call-done.wq.wk.wv, ...), custom_call_target="tpu_custom_call" | custom-call | tf_op jit(solution)/shard_map/attend/pallas_call | solution.py:70
  73.1 4.1 all-gather.9.cloned.1.call-done.wo
  77.3 52.5 %all-gather.11.cloned.1.call-done.wu = bf16[768,3072]{1,0:T(8,128)(2,1)} async-done(((bf16[96,3072]{1,0:T(8,128)(2,1)}), bf16[768,3072]{1,0:T(8,128)(2,1)}) %all-gather.11.cloned.1.call-update) | async-done | bytes 4718608 | tf_op jit(solution)/shard_map/all_gather | solution.py:300
  129.8 51.5 %all-gather.13.cloned.1.call-done.wd = bf16[3072,768]{1,0:T(8,128)(2,1)} async-done(((bf16[384,768]{1,0:T(8,128)(2,1)}), bf16[3072,768]{1,0:T(8,128)(2,1)}) %all-gather.13.cloned.1.call-update) | async-done | bytes 4718608 | tf_op jit(solution)/shard_map/all_gather | solution.py:300
  181.3 43.0 %middle.1 = (bf16[1024,768]{1,0:T(8,128)(2,1)}, bf16[1024,768]{1,0:T(8,128)(2,1)}, bf16[1024,3072]{1,0:T(8,128)(2,1)}, bf16[1024,768]{1,0:T(8,128)(2,1)}, bf16[1...) custom-call(bf16[1024,768]{1,0:T(8,128)(2,1)} %tok.5, ...), custom_call_target="tpu_custom_call" | custom-call | tf_op jit(solution)/shard_map/middle/pallas_call | solution.py:254
  224.3 3.9 convolution_convert_fusion.2
  228.3 33.8 %attend_back.1 = (bf16[3,768,768]{2,1,0:T(8,128)(2,1)}, f32[3,1,768]{2,1,0:T(1,128)}, bf16[1024,768]{1,0:T(8,128)(2,1)}) custom-call(bf16[1024,768]{1,0:T(8,128)(2,1)} %get-tuple-element.33.q_r, bf16[1024,768]{1,0:T(8,128)(2,1)} %get-tuple-element.34.k_r, bf16[1024,768]{1,0:T(8,128)(2,1)} %get-tuple-element.35.v_r, ...), custom_call_target="tpu_custom_call" | custom-call | tf_op jit(solution)/shard_map/attend_back/pallas_call | solution.py:152
  262.1 2.2 slice_bitcast_fusion.2
  264.3 1.9 pad_maximum_fusion
  266.3 1.3 copy-done.16
  267.6 9.7 %convolution_convert_fusion = bf16[3072,768]{1,0:T(8,128)(2,1)} fusion(bf16[1024,3072]{1,0:T(8,128)(2,1)} %get-tuple-element.46, bf16[1024,768]{1,0:T(8,128)(2,1)S(1)} %copy-done.16), kind=kOutput, calls=%fused_computation | convolution fusion | flops 4834197504 | bytes 12582912 | tf_op jit(solution)/shard_map/dot_general | solution.py:26
  277.4 1.4 copy-done.15
  278.8 9.6 %convolution_convert_fusion.1 = bf16[768,3072]{1,0:T(8,128)(2,1)} fusion(bf16[1024,768]{1,0:T(8,128)(2,1)S(1)} %copy-done.15, bf16[1024,3072]{1,0:T(8,128)(2,1)} %get-tuple-element.45), kind=kOutput, calls=%fused_computation.1 | convolution fusion | flops 4834197504 | bytes 12582912 | tf_op jit(solution)/shard_map/dot_general | solution.py:26
  288.5 20.3 %reduce-scatter.5.cloned.1.call-done = bf16[96,2304]{1,0:T(8,128)(2,1)} async-done(((bf16[768,2304]{1,0:T(8,128)(2,1)}), bf16[96,2304]{1,0:T(8,128)(2,1)}) %reduce-scatter.5.cloned.1.call-update) | async-done | bytes 442384 | tf_op jit(solution)/shard_map/reduce_scatter | solution.py:321
  308.9 55.8 %reduce-scatter.11.cloned.1.call-done = bf16[384,768]{1,0:T(8,128)(2,1)} async-done(((bf16[3072,768]{1,0:T(8,128)(2,1)}), bf16[384,768]{1,0:T(8,128)(2,1)}) %reduce-scatter.11.cloned.1.call-update) | async-done | bytes 589840 | tf_op jit(solution)/shard_map/reduce_scatter | solution.py:321
  364.6 55.7 %reduce-scatter.9.cloned.1.call-done = bf16[96,3072]{1,0:T(8,128)(2,1)} async-done(((bf16[768,3072]{1,0:T(8,128)(2,1)}), bf16[96,3072]{1,0:T(8,128)(2,1)}) %reduce-scatter.9.cloned.1.call-update) | async-done | bytes 589840 | tf_op jit(solution)/shard_map/reduce_scatter | solution.py:321
  421.4 38.6 %psum.36 = f32[9216]{0:T(1024)S(1)} all-reduce(f32[9216]{0:T(1024)S(1)} %pad_maximum_fusion.1), channel_id=1, replica_groups=mesh['rep'=4,'shard'=8] {'rep','shard'}, use_global_device_ids=true, to_apply=%region_2.3 | all-reduce | flops 9216 | bytes 73728 | tf_op jit(solution)/shard_map/psum | solution.py:318
  461.8 24.8 %all-reduce.3.cloned.1.call-done = (bf16[96,2304]{1,0:T(8,128)(2,1)}, bf16[96,768]{1,0:T(8,128)(2,1)}, bf16[96,3072]{1,0:T(8,128)(2,1)}, bf16[384,768]{1,0:T(8,128)(2,1)}) async-done(((bf16[96,2304]{1,0:T(8,128)(2,1)}, bf16[96,768]{1,0:T(8,128)(2,1)}, bf16[96,3072]{1,0:T(8,128)(2,1)}, bf16[384,768]{1,0:T(8,128)(2,1)}), (bf16[96,2304]{1,0:T(8,128)(2,1)}, bf16[96,768]{1,0:T(8,128)(2,1)}, ...) | async-done | bytes 1769488 | tf_op jit(solution)/shard_map/psum | solution.py:322
  486.6 2.3 convert_element_type.33
  488.9 1.1 convert_element_type.35
  (87 shorter events, 13.4 us)
Async XLA Ops:
  7.2 2.9 copy-start.6
  7.2 2.9 copy-start.7
  7.2 3.0 copy-start.17
  7.2 3.1 copy-start.9
  7.2 3.0 copy-start.10
  7.2 3.0 copy-start.11
  7.2 3.0 copy-start.8
  7.3 3.0 copy-start.12
  7.3 3.0 copy-start.13
  7.3 3.0 copy-start.14
  7.3 46.7 %all-gather.7.cloned.1.call-start = ((), (), s32[]{:S(2)}) async-start(), calls=%async_computation.4 | async-start | bytes 3981312 | tf_op jit(solution)/shard_map/all_gather | solution.py:300
  8.0 69.3 %all-gather.9.cloned.1.call-start = ((), (), s32[]{:S(2)}) async-start(), calls=%async_computation.5 | async-start | bytes 1327104 | tf_op jit(solution)/shard_map/all_gather | solution.py:300
  8.8 121.0 %all-gather.11.cloned.1.call-start = ((), (), s32[]{:S(2)}) async-start(), calls=%async_computation.6 | async-start | bytes 5308416 | tf_op jit(solution)/shard_map/all_gather | solution.py:300
  9.5 171.8 %all-gather.13.cloned.1.call-start = ((), (), s32[]{:S(2)}) async-start(), calls=%async_computation.7 | async-start | bytes 5308416 | tf_op jit(solution)/shard_map/all_gather | solution.py:300
  10.1 278.4 %reduce-scatter.7.cloned.1.call-start = ((), (), s32[]{:S(2)}) async-start(), calls=%async_computation.9 | async-start | bytes 1327104 | tf_op jit(solution)/shard_map/reduce_scatter | solution.py:321
  181.3 43.0 %copy-start = (bf16[1024,768]{1,0:T(8,128)(2,1)S(1)}, bf16[1024,768]{1,0:T(8,128)(2,1)}, u32[]{:S(2)}) copy-start(bf16[1024,768]{1,0:T(8,128)(2,1)} %get-tuple-element.31.ctx.ctx_r) | copy-start | bytes 4718596
  228.2 80.6 %reduce-scatter.5.cloned.1.call-start = ((), (), s32[]{:S(2)}) async-start(), calls=%async_computation.8 | async-start | bytes 3981312 | tf_op jit(solution)/shard_map/reduce_scatter | solution.py:321
  266.2 98.4 %reduce-scatter.11.cloned.1.call-start = ((), (), s32[]{:S(2)}) async-start(), calls=%async_computation.11 | async-start | bytes 5308416 | tf_op jit(solution)/shard_map/reduce_scatter | solution.py:321
  277.4 142.9 %reduce-scatter.9.cloned.1.call-start = ((), (), s32[]{:S(2)}) async-start(), calls=%async_computation.10 | async-start | bytes 5308416 | tf_op jit(solution)/shard_map/reduce_scatter | solution.py:321
  288.4 131.9 %copy-start.5 = (f32[3,1,768]{2,1,0:T(1,128)S(1)}, f32[3,1,768]{2,1,0:T(1,128)}, u32[]{:S(2)}) copy-start(f32[3,1,768]{2,1,0:T(1,128)} %get-tuple-element.41) | copy-start | bytes 27652
  288.4 132.0 %copy-start.4 = (f32[8,768]{1,0:T(8,128)S(1)}, f32[8,768]{1,0:T(8,128)}, u32[]{:S(2)}) copy-start(f32[8,768]{1,0:T(8,128)} %get-tuple-element.42) | copy-start | bytes 73732
  288.4 198.1 %all-reduce.3.cloned.1.call-start = ((), (), s32[]{:S(2)}) async-start(), calls=%async_computation.12 | async-start | bytes 3538944 | tf_op jit(solution)/shard_map/psum | solution.py:322
  486.6 2.3 copy-start.1
  486.6 3.4 copy-start.2
  (3 other events, 4.9 us)
Sparse Core Ops, SparseCore 0:
  9.7 44.2 all-gather.6
  55.6 21.5 all-gather.8
  78.9 50.8 all-gather.10
  131.3 49.9 all-gather.12
  228.3 31.7 reduce-scatter.6
  266.3 42.4 reduce-scatter.4
  311.2 53.4 reduce-scatter.10
  366.9 53.3 reduce-scatter.8
  423.8 62.7 all-reduce.2

commit v2 on v1

--- a/solution.py
+++ b/solution.py
@@ -1,3 +1,5 @@
+import functools
+
 import jax
 import jax.numpy as jnp
 from jax import lax
@@ -26,11 +28,11 @@
     return lax.dot_general(a, b, (((0,), (0,)), ((), ())), preferred_element_type=f32)
 
 
-def attend_kernel(tok, wq, wk, wv, bq, bv, aq, ak, q_o, k_o, v_o, ctx_o, lse_o):
+def attend_kernel(tok, wq, wk, wv, vecs, aq, ak, q_o, k_o, v_o, ctx_o, lse_o):
     x = tok[...]
-    q = (nn(x, wq[...]) + bq[...].astype(f32)).astype(bf16)
+    q = (nn(x, wq[...]) + vecs[0:1, :].astype(f32)).astype(bf16)
     k = nn(x, wk[...]).astype(bf16)
-    v = (nn(x, wv[...]) + bv[...].astype(f32)).astype(bf16)
+    v = (nn(x, wv[...]) + vecs[1:2, :].astype(f32)).astype(bf16)
     q_o[...] = q
     k_o[...] = k
     v_o[...] = v
@@ -57,12 +59,11 @@
     lse_o[0, 0] = stat.T[:8]
 
 
-def attend(tokens, w, bias, aq, ak, length):
+def attend(tokens, w, vecs, aq, ak, length):
     rows, width = tokens.shape
     groups = width // GW
     seqs = rows // length
     col = lambda o: pl.BlockSpec((width, GW), lambda g, b: (0, o * groups + g))
-    bcol = lambda o: pl.BlockSpec((1, GW), lambda g, b: (0, o * groups + g))
     seq = pl.BlockSpec((length, width), lambda g, b: (b, 0))
     aug = pl.BlockSpec((length, GW), lambda g, b: (b, 0))
     blk = pl.BlockSpec((length, GW), lambda g, b: (b, g))
@@ -70,15 +71,26 @@
     return pl.pallas_call(
         attend_kernel,
         grid=(groups, seqs),
-        in_specs=[seq, col(0), col(1), col(2), bcol(0), bcol(1), aug, aug],
+        in_specs=[seq, col(0), col(1), col(2), pl.BlockSpec((16, GW), lambda g, b: (0, g)), aug, aug],
         out_specs=[blk, blk, blk, blk, pl.BlockSpec((1, 1, 8, length), lambda g, b: (b, g, 0, 0))],
         out_shape=[act, act, act, act, jax.ShapeDtypeStruct((seqs, groups, 8, length), f32)],
         compiler_params=pltpu.CompilerParams(vmem_limit_bytes=VMEM_LIMIT),
+        cost_estimate=pl.CostEstimate(flops=20_000_000_000, bytes_accessed=12_000_000, transcendentals=0),
         name="attend",
-    )(tokens, w, w, w, bias, bias, aq, ak)
-
-
-def attend_back_kernel(q_r, k_r, v_r, do_r, ctx_r, lse_r, aq, ak, tok, wq, wk, wv, gb, dw_o, db_o, dx_o, dw_s, dx_s):
+    )(tokens, w, w, w, vecs, aq, ak)
+
+
+def select_lanes(s, piece, width):
+    i = lax.broadcasted_iota(jnp.int32, (128, width), 0)
+    j = lax.broadcasted_iota(jnp.int32, (128, width), 1)
+    return ((j == s * piece + i) & (i < piece)).astype(f32).astype(bf16)
+
+
+def attend_back_kernel(rel, at_r, q_r, k_r, v_r, do_r, ctx_r, lse_r, aq, ak, tok, wq, wk, wv, gb, tbl, *rest):
+    if rel:
+        own_o, other_o, dx_o, dw_s, dx_s, db_o = rest
+    else:
+        dw_o, db_o, dx_o, dw_s, dx_s = rest
     g, b = pl.program_id(0), pl.program_id(1)
     q, k, v, do = q_r[...], k_r[...], v_r[...], do_r[...]
     length, width = q.shape
@@ -116,12 +128,12 @@
     @pl.when(b == 0)
     def _():
         dw_s[...] = dw
-        db_o[0] = sums
+        db_o[pl.ds(0 if not rel else g, 1)] = sums[None]
 
     @pl.when(b > 0)
     def _():
         dw_s[...] += dw
-        db_o[0] += sums
+        db_o[pl.ds(0 if not rel else g, 1)] += sums[None]
 
     @pl.when(g == 0)
     def _():
@@ -133,15 +145,65 @@
 
     @pl.when(b == pl.num_programs(1) - 1)
     def _():
-        for i in range(3):
-            dw_o[i] = dw_s[:, i * width : (i + 1) * width].astype(bf16)
+        if not rel:
+            for i in range(3):
+                dw_o[i] = dw_s[:, i * width : (i + 1) * width].astype(bf16)
+        else:
+            scatter_rows(dw_s[...].astype(bf16), at_r, own_o, other_o, g * 48, 0, 0, 2 * 384)
+
+    if rel:
+
+        @pl.when((b == pl.num_programs(1) - 1) & (g == pl.num_programs(0) - 1))
+        def _():
+            x, z, c = at_r[1], at_r[2], at_r[3]
+            dbq = jnp.concatenate([db_o[i, :, :width] for i in range(3)], axis=1)
+            dbv = jnp.concatenate([db_o[i, :, 2 * width :] for i in range(3)], axis=1)
+            table = jnp.concatenate([dbq, dbv, tbl[...]], axis=0).astype(bf16)
+            zero16 = jnp.zeros((4, 16, 384), bf16)
+            for ab in range(2):
+                for h in range(2):
+                    own_o[ab, h, :, 144:160, :] = zero16
+                    other_o[ab, h, :, 144:160, :] = zero16
+            for s in range(8):
+                blk = nt(table, select_lanes(s, 96, table.shape[1])).astype(bf16)
+                kk = lax.rem(s // 2 - z + 4, 4)
+
+                @pl.when(c == s % 2)
+                def _(blk=blk, kk=kk):
+                    own_o[0, x, kk, 144:160, 0:128] = blk
+
+                @pl.when(c != s % 2)
+                def _(blk=blk, kk=kk):
+                    other_o[0, x, kk, 144:160, 0:128] = blk
 
     @pl.when(g == pl.num_programs(0) - 1)
     def _():
         dx_o[...] = dx_s[b].astype(bf16)
 
 
-def attend_back(q, k, v, do, ctx, lse, aq, ak, tokens, w, gb, length):
+def scatter_rows(res, at_r, own_o, other_o, row, col, lo, hi):
+    y, x, z, c = at_r[0], at_r[1], at_r[2], at_r[3]
+    piece = res.shape[0] // 8
+    half = piece // 2
+    wide = (hi - lo) // 2
+    for s in range(8):
+        kk = lax.rem(s // 2 - z + 4, 4)
+        for ab, turn in ((0, x), (1, y)):
+            part = res[s * piece + ab * half : s * piece + (ab + 1) * half]
+            for h in range(2):
+                val = part[:, h * wide : (h + 1) * wide]
+                rel_h = lax.rem(h + turn, 2)
+
+                @pl.when(c == s % 2)
+                def _(val=val, rel_h=rel_h, kk=kk, ab=ab):
+                    own_o[ab, rel_h, kk, pl.ds(row, half), pl.ds(col, wide)] = val
+
+                @pl.when(c != s % 2)
+                def _(val=val, rel_h=rel_h, kk=kk, ab=ab):
+                    other_o[ab, rel_h, kk, pl.ds(row, half), pl.ds(col, wide)] = val
+
+
+def attend_back(at, q, k, v, do, ctx, lse, aq, ak, tokens, w, gb, table, length, rel):
     rows, width = tokens.shape
     groups = width // GW
     seqs = rows // length
@@ -149,25 +211,33 @@
     seq = pl.BlockSpec((length, width), lambda g, b: (b, 0))
     aug = pl.BlockSpec((length, GW), lambda g, b: (b, 0))
     blk = pl.BlockSpec((length, GW), lambda g, b: (b, g))
-    return pl.pallas_call(
-        attend_back_kernel,
-        grid=(groups, seqs),
-        in_specs=[blk, blk, blk, blk, blk, pl.BlockSpec((1, 1, 8, length), lambda g, b: (b, g, 0, 0)), aug, aug, seq,
-                  col(0), col(1), col(2), seq],
-        out_specs=[
+    dx_spec = pl.BlockSpec((length, width), lambda g, b: (jnp.where(g == groups - 1, b, 0), 0))
+    dx_shape = jax.ShapeDtypeStruct((rows, width), bf16)
+    scratch = [pltpu.VMEM((width, 3 * GW), f32), pltpu.VMEM((seqs, length, width), f32)]
+    if rel:
+        part = (2, 2, 4, 160, 384)
+        out_specs = [pl.BlockSpec(part, lambda g, b: (0, 0, 0, 0, 0))] * 2 + [dx_spec]
+        out_shape = [jax.ShapeDtypeStruct(part, bf16)] * 2 + [dx_shape]
+        scratch = scratch + [pltpu.VMEM((groups, 1, 3 * GW), f32)]
+    else:
+        out_specs = [
             pl.BlockSpec((3, width, GW), lambda g, b: (0, 0, g)),
             pl.BlockSpec((1, 1, 3 * GW), lambda g, b: (g, 0, 0)),
-            pl.BlockSpec((length, width), lambda g, b: (jnp.where(g == groups - 1, b, 0), 0)),
-        ],
-        out_shape=[
-            jax.ShapeDtypeStruct((3, width, width), bf16),
-            jax.ShapeDtypeStruct((groups, 1, 3 * GW), f32),
-            jax.ShapeDtypeStruct((rows, width), bf16),
-        ],
-        scratch_shapes=[pltpu.VMEM((width, 3 * GW), f32), pltpu.VMEM((seqs, length, width), f32)],
+            dx_spec,
+        ]
+        out_shape = [jax.ShapeDtypeStruct((3, width, width), bf16), jax.ShapeDtypeStruct((groups, 1, 3 * GW), f32), dx_shape]
+    return pl.pallas_call(
+        functools.partial(attend_back_kernel, rel),
+        grid=(groups, seqs),
+        in_specs=[pl.BlockSpec(memory_space=pltpu.SMEM), blk, blk, blk, blk, blk, pl.BlockSpec((1, 1, 8, length), lambda g, b: (b, g, 0, 0)), aug, aug, seq,
+                  col(0), col(1), col(2), seq, pl.BlockSpec(table.shape, lambda g, b: (0, 0))],
+        out_specs=out_specs,
+        out_shape=out_shape,
+        scratch_shapes=scratch,
         compiler_params=pltpu.CompilerParams(vmem_limit_bytes=VMEM_LIMIT),
+        cost_estimate=pl.CostEstimate(flops=34_000_000_000, bytes_accessed=16_000_000, transcendentals=0),
         name="attend_back",
-    )(q, k, v, do, ctx, lse, aq, ak, tokens, w, w, w, gb)
+    )(at, q, k, v, do, ctx, lse, aq, ak, tokens, w, w, w, gb, table)
 
 
 def masks(segment_ids, valid):
@@ -183,26 +253,27 @@
     return 0.5 * (1.0 + lax.erf(x * 0.7071067811865476)), jnp.exp(-0.5 * x * x) * 0.3989422804014327
 
 
-def middle_kernel(tok, ctx, cot, wo, bo, g1, s1, wu, bu, wd, bd, g2, s2,
+def middle_kernel(tok, ctx, cot, wou, vecs, bu, wd,
                   out_o, low_o, hid_o, gd_o, gu_o, gb_o, gc_o, vec_o, bup_o, slope):
     i = pl.program_id(0)
     width = tok.shape[1]
-    ff = wu.shape[1]
+    ff = wd.shape[0]
     step = width
     chunks = ff // step
-    row = lambda r: r[...].astype(f32)
-    pre = tok[...].astype(f32) + nn(ctx[...], wo[...]) + row(bo)
+    bo, g1, s1, bd, g2, s2 = (vecs[j : j + 1, :].astype(f32) for j in range(2, 8))
+    up = lambda c: wou[:, (c + 1) * step : (c + 2) * step]
+    pre = tok[...].astype(f32) + nn(ctx[...], wou[:, :width]) + bo
     mean = lambda v: jnp.mean(v, axis=1, keepdims=True)
     centre = pre - mean(pre)
     r1 = lax.rsqrt(mean(centre * centre) + 1e-05)
     n1 = centre * r1
-    normed = n1 * row(g1) + row(s1)
+    normed = n1 * g1 + s1
     low = normed.astype(bf16)
     low_o[...] = low
-    acc = normed + row(bd)
+    acc = normed + bd
     for c in range(chunks):
         cols = slice(c * step, (c + 1) * step)
-        hp = nn(low, wu[:, cols]) + bu[:, cols].astype(f32)
+        hp = nn(low, up(c)) + bu[:, cols].astype(f32)
         cdf, pdf = phi(hp)
         slope[:, cols] = cdf + hp * pdf
         hid = (hp * cdf).astype(bf16)
@@ -211,9 +282,9 @@
     centre = acc - mean(acc)
     r2 = lax.rsqrt(mean(centre * centre) + 1e-05)
     n2 = centre * r2
-    out_o[...] = (n2 * row(g2) + row(s2)).astype(bf16)
+    out_o[...] = (n2 * g2 + s2).astype(bf16)
     ct = cot[...].astype(f32)
-    e = ct * row(g2)
+    e = ct * g2
     gp2 = r2 * (e - mean(e) - n2 * mean(e * n2))
     gd = gp2.astype(bf16)
     gd_o[...] = gd
@@ -234,19 +305,19 @@
         gu = (nt(gd, wd[cols, :]) * slope[:, cols]).astype(bf16)
         gu_o[:, cols] = gu
         put(bup_o, (slice(0, 1), cols), total(gu.astype(f32)))
-        acc = acc + nt(gu, wu[:, cols])
-    e = acc * row(g1)
+        acc = acc + nt(gu, up(c))
+    e = acc * g1
     gp1 = r1 * (e - mean(e) - n1 * mean(e * n1))
     gb = gp1.astype(bf16)
     gb_o[...] = gb
-    gc_o[...] = nt(gb, wo[...]).astype(bf16)
+    gc_o[...] = nt(gb, wou[:, :width]).astype(bf16)
     for at, v in enumerate((gb.astype(f32), acc * n1, acc, gd.astype(f32), ct * n2, ct)):
         put(vec_o, (slice(at, at + 1), slice(None)), total(v))
 
 
-def middle(tokens, ctx, cot, wo, bo, g1, s1, wu, bu, wd, bd, g2, s2, tile=256):
+def middle(tokens, ctx, cot, wou, vecs, bu, wd, tile=256):
     rows, width = tokens.shape
-    ff = wu.shape[1]
+    ff = wd.shape[0]
     act = pl.BlockSpec((tile, width), lambda i: (i, 0))
     wide = pl.BlockSpec((tile, ff), lambda i: (i, 0))
     whole = lambda a: pl.BlockSpec(a.shape, lambda i: (0, 0), pipeline_mode=pl.Buffered(1))
@@ -254,14 +325,351 @@
     return pl.pallas_call(
         middle_kernel,
         grid=(rows // tile,),
-        in_specs=[act, act, act] + [whole(a) for a in (wo, bo, g1, s1, wu, bu, wd, bd, g2, s2)],
+        in_specs=[act, act, act] + [whole(a) for a in (wou, vecs, bu, wd)],
         out_specs=[act, act, wide, act, wide, act, act, pl.BlockSpec((8, width), lambda i: (0, 0)), pl.BlockSpec((8, ff), lambda i: (0, 0))],
         out_shape=[S((rows, width), bf16), S((rows, width), bf16), S((rows, ff), bf16), S((rows, width), bf16), S((rows, ff), bf16),
                    S((rows, width), bf16), S((rows, width), bf16), S((8, width), f32), S((8, ff), f32)],
         scratch_shapes=[pltpu.VMEM((tile, ff), f32)],
         compiler_params=pltpu.CompilerParams(vmem_limit_bytes=VMEM_LIMIT),
+        cost_estimate=pl.CostEstimate(flops=43_000_000_000, bytes_accessed=30_000_000, transcendentals=0),
         name="middle",
-    )(tokens, ctx, cot, wo, bo, g1, s1, wu, bu, wd, bd, g2, s2)
+    )(tokens, ctx, cot, wou, vecs, bu, wd)
+
+
+def assemble_kernel(at_r, own, ring, across, along, own2, ring2, across2, along2, out):
+    y, x, z, c = at_r[0], at_r[1], at_r[2], at_r[3]
+    rows, cols = own.shape
+    half, wide = rows // 2, cols // 2
+    for turn, parts in ((c, (own, ring, across, along)), (1 - c, (own2, ring2, across2, along2))):
+        mine, ringed, xs, ys = parts
+        base = (2 * z + turn) * rows
+        out[pl.ds(pl.multiple_of(base, 16), rows), :] = mine[...]
+        for k in range(1, 4):
+            base = (2 * lax.rem(z - k + 4, 4) + turn) * rows
+            for ab, flip, far in ((0, x, xs), (1, y, ys)):
+                at = pl.ds(pl.multiple_of(base + ab * half, 16), half)
+                near = pl.multiple_of(flip * wide, 128)
+                away = pl.multiple_of((1 - flip) * wide, 128)
+                out[at, pl.ds(near, wide)] = ringed[k - 1, ab * half : (ab + 1) * half, :]
+                out[at, pl.ds(away, wide)] = far[k - 1]
+
+
+def assemble(at, parts):
+    rows, cols = parts[0].shape
+    vm = pl.BlockSpec(memory_space=pltpu.VMEM)
+    return pl.pallas_call(
+        assemble_kernel,
+        in_specs=[pl.BlockSpec(memory_space=pltpu.SMEM)] + [vm] * 8,
+        out_specs=vm,
+        out_shape=jax.ShapeDtypeStruct((8 * rows, cols), bf16),
+        compiler_params=pltpu.CompilerParams(vmem_limit_bytes=VMEM_LIMIT),
+        cost_estimate=pl.CostEstimate(flops=0, bytes_accessed=32 * rows * cols, transcendentals=0),
+        name="assemble",
+    )(at, *parts)
+
+
+def grad_down_kernel(at_r, hid, gd, own_o, other_o):
+    p = pl.program_id(0)
+    res = tn(hid[...], gd[...]).astype(bf16)
+    rows, cols = res.shape
+    half, wide = rows // 2, cols // 2
+    for ab, turn in ((0, at_r[1]), (1, at_r[0])):
+        for h in range(2):
+            val = res[ab * half : (ab + 1) * half, h * wide : (h + 1) * wide]
+            rel_h = lax.rem(h + turn, 2)
+
+            @pl.when(p < 4)
+            def _(val=val, rel_h=rel_h, ab=ab):
+                other_o[ab, rel_h, lax.rem(p, 4)] = val
+
+            @pl.when(p >= 4)
+            def _(val=val, rel_h=rel_h, ab=ab):
+                own_o[ab, rel_h, lax.rem(p, 4)] = val
+
+
+def grad_down(at, hid, gd):
+    rows, ff = hid.shape
+    width = gd.shape[1]
+    piece = ff // 8
+    part = (2, 2, 4, piece // 2, width // 2)
+
+    def owner(p, at_r):
+        z = lax.rem(at_r[2] + lax.rem(p, 4), 4)
+        return 0, 2 * z + jnp.where(p < 4, 1 - at_r[3], at_r[3])
+
+    whole = pl.BlockSpec(part, lambda p, at_r: (0, 0, 0, 0, 0))
+    return pl.pallas_call(
+        grad_down_kernel,
+        grid_spec=pltpu.PrefetchScalarGridSpec(
+            num_scalar_prefetch=1,
+            grid=(8,),
+            in_specs=[pl.BlockSpec((rows, piece), owner), pl.BlockSpec((rows, width), lambda p, at_r: (0, 0))],
+            out_specs=[whole, whole],
+        ),
+        out_shape=[jax.ShapeDtypeStruct(part, bf16)] * 2,
+        compiler_params=pltpu.CompilerParams(vmem_limit_bytes=VMEM_LIMIT),
+        cost_estimate=pl.CostEstimate(flops=9_000_000_000, bytes_accessed=14_000_000, transcendentals=0),
+        name="grad_down",
+    )(at, hid, gd)
+
+
+def grad_up_kernel(at_r, ctx, gb, low, gu, own_o, other_o, turned):
+    j = pl.program_id(0)
+    step = gb.shape[1]
+    half = pl.num_programs(0) // 2
+    first = 2 * ctx.shape[1] // (2 * step)
+    y, x, z, c = at_r[0], at_r[1], at_r[2], at_r[3]
+
+    @pl.when(j == 0)
+    def _():
+        turned[...] = ctx[...].T
+
+    @pl.when(j == first)
+    def _():
+        turned[...] = low[...].T
+
+    def emit(rhs):
+        res = nn(turned[...], rhs[...]).astype(bf16)
+        piece = res.shape[0] // 8
+        rows = piece // 2
+        h = j // half
+        col = pl.multiple_of(lax.rem(j, half) * step, 128)
+        for s in range(8):
+            kk = lax.rem(s // 2 - z + 4, 4)
+            for ab, turn in ((0, x), (1, y)):
+                val = res[s * piece + ab * rows : s * piece + (ab + 1) * rows]
+                rel_h = lax.rem(h + turn, 2)
+
+                @pl.when(c == s % 2)
+                def _(val=val, rel_h=rel_h, kk=kk, ab=ab):
+                    own_o[ab, rel_h, kk, :, pl.ds(col, step)] = val
+
+                @pl.when(c != s % 2)
+                def _(val=val, rel_h=rel_h, kk=kk, ab=ab):
+                    other_o[ab, rel_h, kk, :, pl.ds(col, step)] = val
+
+    @pl.when(j < first)
+    def _():
+        emit(gb)
+
+    @pl.when(j >= first)
+    def _():
+        emit(gu)
+
+
+def grad_up(at, ctx, gb, low, gu):
+    rows, width = gb.shape
+    ff = gu.shape[1]
+    step = width // 2
+    steps = (width + ff) // step
+    part = (2, 2, 4, width // 16, (width + ff) // 2)
+    act = pl.BlockSpec((rows, width), lambda j: (0, 0))
+    whole = pl.BlockSpec(part, lambda j: (0, 0, 0, 0, 0))
+    return pl.pallas_call(
+        grad_up_kernel,
+        grid=(steps,),
+        in_specs=[
+            pl.BlockSpec(memory_space=pltpu.SMEM),
+            act,
+            pl.BlockSpec((rows, step), lambda j: (0, jnp.minimum(j, 1))),
+            act,
+            pl.BlockSpec((rows, step), lambda j: (0, jnp.maximum(j - 2, 0))),
+        ],
+        out_specs=[whole, whole],
+        out_shape=[jax.ShapeDtypeStruct(part, bf16)] * 2,
+        scratch_shapes=[pltpu.VMEM((width, rows), bf16)],
+        compiler_params=pltpu.CompilerParams(vmem_limit_bytes=VMEM_LIMIT),
+        cost_estimate=pl.CostEstimate(flops=11_000_000_000, bytes_accessed=16_000_000, transcendentals=0),
+        name="grad_up",
+    )(at, ctx, gb, low, gu)
+
+
+AXES = ("rep", "shard")
+
+
+def pairs(move):
+    found = []
+    for y in range(2):
+        for x in range(2):
+            for z in range(4):
+                for c in range(2):
+                    j, i, k, d = move(y, x, z, c)
+                    found.append(((y * 2 + x) * 8 + z * 2 + c, (j * 2 + i) * 8 + k * 2 + d))
+    return found
+
+
+CORE = pairs(lambda y, x, z, c: (y, x, z, 1 - c))
+ACROSS = pairs(lambda y, x, z, c: (y, 1 - x, z, c))
+ALONG = pairs(lambda y, x, z, c: (1 - y, x, z, c))
+RING = pairs(lambda y, x, z, c: (y, x, (z + 1) % 4, c))
+
+
+def send(a, where):
+    return lax.ppermute(a, AXES, where)
+
+
+def fetch(w, x, y):
+    rows, cols = w.shape
+    half, wide = rows // 2, cols // 2
+    a = lax.dynamic_slice(w[:half], (0, x * wide), (half, wide))
+    b = lax.dynamic_slice(w[half:], (0, y * wide), (half, wide))
+    held = jnp.concatenate([a, b], axis=0)
+    ring = []
+    for _ in range(3):
+        held = send(held, RING)
+        ring.append(held)
+    ring = jnp.stack(ring)
+    far_x = send(ring[:, :half], ACROSS)
+    far_y = send(ring[:, half:], ALONG)
+    return [w, ring, far_x, far_y] + [send(t, CORE) for t in (w, ring, far_x, far_y)]
+
+
+def total(*terms):
+    out = terms[0].astype(f32)
+    for t in terms[1:]:
+        out = out + t.astype(f32)
+    return out.astype(bf16)
+
+
+def reduce(own, other):
+    got = send(other, CORE)
+    far_x = send(total(own[0, 1], got[0, 1]), ACROSS)
+    far_y = send(total(own[1, 1], got[1, 1]), ALONG)
+    a = total(own[0, 0], got[0, 0], far_x)
+    b = total(own[1, 0], got[1, 0], far_y)
+    held = jnp.stack([a[3], b[3]])
+    for k in (2, 1, 0):
+        held = send(held, RING)
+        held = total(held, jnp.stack([a[k], b[k]]))
+    a, b = held[0], held[1]
+    a = total(a, send(a, ALONG))
+    b = total(b, send(b, ACROSS))
+    return a, send(a, ACROSS), b, send(b, ALONG)
+
+
+def finish_kernel(kind, at_r, a, a2, b, b2, *outs):
+    y, x = at_r[0], at_r[1]
+    for ab, turn, near, far in ((0, x, a, a2), (1, y, b, b2)):
+        one, two = near[...].astype(f32), far[...].astype(f32)
+        left = jnp.where(turn == 0, one, two)
+        right = jnp.where(turn == 0, two, one)
+        if kind == "down":
+            half = left.shape[0]
+            outs[0][ab * half : (ab + 1) * half, :] = jnp.concatenate([left, right], axis=1)
+        elif kind == "up":
+            half = left.shape[0]
+            at = slice(ab * half, (ab + 1) * half)
+            both = jnp.concatenate([left, right], axis=1)
+            width = outs[0].shape[1]
+            outs[0][at, :] = both[:, :width]
+            outs[1][at, :] = both[:, width:]
+        else:
+            half = outs[0].shape[0] // 2
+            at = slice(ab * half, (ab + 1) * half)
+            width = outs[0].shape[1] // 3
+            for g in range(width // GW):
+                both = jnp.concatenate([left[g * half : (g + 1) * half], right[g * half : (g + 1) * half]], axis=1)
+                for i in range(3):
+                    outs[0][at, i * width + g * GW : i * width + (g + 1) * GW] = both[:, i * GW : (i + 1) * GW]
+            if ab == 0:
+                outs[1][...] = left[3 * half :, :128]
+
+
+def finish(at, kind, blocks, shapes):
+    vm = pl.BlockSpec(memory_space=pltpu.VMEM)
+    return pl.pallas_call(
+        functools.partial(finish_kernel, kind),
+        in_specs=[pl.BlockSpec(memory_space=pltpu.SMEM)] + [vm] * 4,
+        out_specs=[vm] * len(shapes),
+        out_shape=[jax.ShapeDtypeStruct(s, f32) for s in shapes],
+        compiler_params=pltpu.CompilerParams(vmem_limit_bytes=VMEM_LIMIT),
+        cost_estimate=pl.CostEstimate(flops=0, bytes_accessed=4_000_000, transcendentals=0),
+        name="finish_" + kind,
+    )(at, *blocks)
+
+
+def pack(vectors, wide):
+    block = jnp.concatenate([v.reshape(-1, vectors[1].shape[0]) for v in vectors] + [wide.reshape(4, -1)], axis=0)
+    return jnp.pad(block, ((0, 16 - block.shape[0]), (0, 128 - block.shape[1])))
+
+
+def fetch_vectors(block, z, c):
+    piece = 96
+    ring = [block]
+    for _ in range(3):
+        ring.append(send(ring[-1], RING))
+    ring = jnp.stack(ring)
+    every = jnp.stack([ring, send(ring, CORE)])
+    k = lax.broadcasted_iota(jnp.int32, (2, 4, 8), 1)
+    d = lax.broadcasted_iota(jnp.int32, (2, 4, 8), 0)
+    s = lax.broadcasted_iota(jnp.int32, (2, 4, 8), 2)
+    pick = (s == 2 * ((z - k) % 4) + (c + d) % 2).astype(bf16)
+    table = jnp.einsum("dks,dkrl->srl", pick, every, preferred_element_type=f32).astype(bf16)
+    table = table[:, :, :piece]
+    wide = table[:, 8:12].reshape(1, -1)
+    return table.transpose(1, 0, 2).reshape(16, -1), wide
+
+
+def shards_near(
+    tokens,
+    cotangent,
+    qkv_weight,
+    query_value_bias,
+    out_weight,
+    out_bias,
+    norm_one_gain,
+    norm_one_shift,
+    up_weight,
+    up_bias,
+    down_weight,
+    down_bias,
+    norm_two_gain,
+    norm_two_shift,
+    segment_ids,
+    valid,
+):
+    length = segment_ids.shape[1]
+    width = tokens.shape[1]
+    r, s = lax.axis_index("rep"), lax.axis_index("shard")
+    y, x, z, c = r // 2, r % 2, s // 2, s % 2
+    at = jnp.stack([y, x, z, c]).astype(jnp.int32)
+    block = pack(
+        (query_value_bias, out_bias, norm_one_gain, norm_one_shift, down_bias, norm_two_gain, norm_two_shift), up_bias
+    )
+    vecs, bu = fetch_vectors(block, z, c)
+    wqkv = assemble(at, fetch(qkv_weight, x, y))
+    aq, ak = masks(segment_ids, valid)
+    q, k, v, ctx, lse = attend(tokens, wqkv, vecs, aq, ak, length)
+    wou = assemble(at, fetch(jnp.concatenate([out_weight, up_weight], axis=1), x, y))
+    wd = assemble(at, fetch(down_weight, x, y))
+    result, low, hid, gd, gu, gb, gc, vec, bup = middle(tokens, ctx, cotangent, wou, vecs, bu, wd)
+    down = reduce(*grad_down(at, hid, gd))
+    up = reduce(*grad_up(at, ctx, gb, low, gu))
+    wide = bup[0].reshape(8, 4, 96).transpose(1, 0, 2).reshape(4, width)
+    table = jnp.concatenate([vec[:6], wide, jnp.zeros((4, width), f32)], axis=0)
+    own, other, dx = attend_back(at, q, k, v, gc, ctx, lse, aq, ak, tokens, wqkv, gb, table, length, True)
+    qkv = reduce(own, other)
+    (dwd,) = finish(at, "down", down, [down_weight.shape])
+    dwo, dwu = finish(at, "up", up, [out_weight.shape, up_weight.shape])
+    dwq, small = finish(at, "qkv", qkv, [qkv_weight.shape, (16, 128)])
+    piece = out_bias.shape[0]
+    one = lambda i: small[i, :piece]
+    return (
+        result,
+        dx,
+        dwq,
+        small[:2, :piece],
+        dwo,
+        one(2),
+        one(3),
+        one(4),
+        dwu,
+        small[8:12, :piece].reshape(-1),
+        dwd,
+        one(5),
+        one(6),
+        one(7),
+    )
 
 
 def spread(args):
@@ -298,20 +706,20 @@
     width = tokens.shape[1]
     groups = width // GW
     gather = lambda a: lax.all_gather(a, "shard", axis=0, tiled=True)
-    bqv, bo, g1, s1, bu, bd, g2, s2 = spread(
-        (query_value_bias, out_bias, norm_one_gain, norm_one_shift, up_bias, down_bias, norm_two_gain, norm_two_shift)
+    *rest, bu = spread(
+        (query_value_bias, out_bias, norm_one_gain, norm_one_shift, down_bias, norm_two_gain, norm_two_shift, up_bias)
     )
-    wqkv, wo, wu, wd = gather(qkv_weight), gather(out_weight), gather(up_weight), gather(down_weight)
-    bias = bqv.reshape(1, -1)
+    vecs = jnp.concatenate([v.reshape(-1, width) for v in rest] + [jnp.zeros((8, width), bf16)], axis=0)
+    wqkv, wd = gather(qkv_weight), gather(down_weight)
+    wou = jnp.concatenate([gather(out_weight), gather(up_weight)], axis=1)
+    at = jnp.zeros((4,), jnp.int32)
     aq, ak = masks(segment_ids, valid)
-    q, k, v, ctx, lse = attend(tokens, wqkv, bias, aq, ak, length)
-    result, low, hid, gd, gu, gb, gc, vec, bup = middle(
-        tokens, ctx, cotangent, wo, bo[None], g1[None], s1[None], wu, bu[None], wd, bd[None], g2[None], s2[None]
-    )
+    q, k, v, ctx, lse = attend(tokens, wqkv, vecs, aq, ak, length)
+    result, low, hid, gd, gu, gb, gc, vec, bup = middle(tokens, ctx, cotangent, wou, vecs, bu[None], wd)
     dwd = tn(hid, gd).astype(bf16)
     dwu = tn(low, gu).astype(bf16)
     dwo = tn(ctx, gb).astype(bf16)
-    dw, db, dx = attend_back(q, k, v, gc, ctx, lse, aq, ak, tokens, wqkv, gb, length)
+    dw, db, dx = attend_back(at, q, k, v, gc, ctx, lse, aq, ak, tokens, wqkv, gb, vec, length, False)
     dwq = jnp.concatenate([dw[0], dw[1], dw[2]], axis=1)
     db = db.reshape(groups, 3, GW).transpose(1, 0, 2).reshape(3, width)
     small = jnp.concatenate([db[0], db[2], vec[:6].reshape(-1), bup[0]])
@@ -324,32 +732,18 @@
     rank = lax.axis_index("shard")
     own = lambda at, size: lax.dynamic_slice(small, (at + rank * size,), (size,))
     piece = out_bias.shape[0]
-    vecs = [own(width * i, piece) for i in range(8)]
+    vs = [own(width * i, piece) for i in range(8)]
     dbu = own(8 * width, up_bias.shape[0])
     gd_w, gu_w, go_w, gq_w = owned(dwd), owned(dwu), owned(dwo), owned(dwq)
-    return (
-        result,
-        dx,
-        gq_w,
-        jnp.stack([vecs[0], vecs[1]]),
-        go_w,
-        vecs[2],
-        vecs[3],
-        vecs[4],
-        gu_w,
-        dbu,
-        gd_w,
-        vecs[5],
-        vecs[6],
-        vecs[7],
-    )
+    return result, dx, gq_w, jnp.stack(vs[:2]), go_w, vs[2], vs[3], vs[4], gu_w, dbu, gd_w, vs[5], vs[6], vs[7]
 
 
 def solution(mesh):
     rows, one = P(("rep", "shard"), None), P("shard")
     mat, two = P("shard", None), P(None, "shard")
+    near = mesh.shape["rep"] == 4 and mesh.shape["shard"] == 8
     return jax.shard_map(
-        shards,
+        shards_near if near else shards,
         mesh=mesh,
         in_specs=(rows, rows, mat, two, mat, one, one, one, mat, one, mat, one, one, one, rows, rows),
         out_specs=(rows, rows, mat, two, mat, one, one, one, mat, one, mat, one, one, one),

time: 499 us -> 356 us (0.71)
  waiting for transfers between devices: 287 us -> 132 us
  Pallas kernels: 96 us -> 151 us
  blocking collectives: 54.5 us -> 0 us
  starting transfers between devices: 0.36 us -> 42.3 us
  matrix products: 23.2 us -> 0.27 us
  between operations: 14.1 us -> 1.65 us
    ppermute x0 -> x61, waiting for transfers between devices: none -> 132 us  [send(): return lax.ppermute(a, AXES, where)]
    reduce_scatter x4 -> x0, waiting for transfers between devices: 132 us -> none  [owned(): part = lax.psum_scatter(a, 'shard', scatter_dimension=0, tiled=True)]
    all_gather x4 -> x0, waiting for transfers between devices: 128 us -> none  [shards(): gather = lambda a: lax.all_gather(a, 'shard', axis=0, tiled=True)]
    pallas_call x1 -> x9, Pallas kernels: 33.8 us -> 88.6 us  [the longest x1 36.8 us: attend_back(): pl.pallas_call(functools.partial(attend_back_kernel, rel), grid=(groups,...]
    ppermute x0 -> x61, starting transfers between devices: none -> 42.3 us  [send(): return lax.ppermute(a, AXES, where)]
    psum x1 -> x0, blocking collectives: 38.6 us -> none  [shards(): small = lax.psum(small.reshape(-1, 128), ('rep', 'shard')).reshape(-1)]
    psum x1 -> x0, waiting for transfers between devices: 24.8 us -> none  [owned(): return lax.psum(part, 'rep').astype(f32)]
    dot_general x3 -> x1, matrix products: 23.2 us -> 0.27 us  [fetch_vectors(): jnp.einsum('dks,dkrl->srl', pick, every, preferred_element_type=f32)]
  transfers between devices with their start and end apart: 9 -> 61, of which waited for: 8 -> 27; matrix products, arithmetic and copies ran while one was open for 7% -> 5% of each run, Pallas kernels for 11% -> 18%
where the time goes in v2:
time: 356 us; the launch traced here: 355 us
  Pallas kernels  151 us (42%)
  waiting for transfers between devices  132 us (37%)
  starting transfers between devices  42.3 us (12%)
  local copies, waits for them, and re-layouts  16.3 us (5%)
  other arithmetic  11.6 us (3%)
    ppermute x61, waiting for transfers between devices, send(): return lax.ppermute(a, AXES, where)  132 us
    pallas_call x1, Pallas kernels, middle(): pl.pallas_call(middle_kernel, grid=(rows // tile,), in_specs=[act, act, a...  42.7 us
    ppermute x61, starting transfers between devices, send(): return lax.ppermute(a, AXES, where)  42.3 us
    pallas_call x1, Pallas kernels, attend_back(): pl.pallas_call(functools.partial(attend_back_kernel, rel), grid=(groups,...  36.8 us
    pallas_call x1, Pallas kernels, attend(): pl.pallas_call(attend_kernel, grid=(groups, seqs), in_specs=[seq, col(0),...  19.3 us
    pallas_call x1, Pallas kernels, grad_up(): pl.pallas_call(grad_up_kernel, grid=(steps,), in_specs=[pl.BlockSpec(memo...  18 us
    pallas_call x3, Pallas kernels, assemble(): pl.pallas_call(assemble_kernel, in_specs=[pl.BlockSpec(memory_space=pltpu...  14.4 us
    pallas_call x1, Pallas kernels, grad_down(): pl.pallas_call(grad_down_kernel, grid_spec=pltpu.PrefetchScalarGridSpec(n...  12.7 us
  transfers between devices with their start and end apart: 61, of which 27 were waited for; matrix products, arithmetic and copies ran while one was open for 5% of the time, Pallas kernels for 18%

profile of v2, /device:TPU:0, one launch (start us, length us, event | category | flops | bytes accessed | tf_op | source)
XLA Modules:
  0.0 355.2 jit_solution(5156023149585505787)
XLA Ops:
  2.7 3.1 collective-permute-start.22
  12.8 14.8 %collective-permute-done = bf16[96,1152]{1,0:T(8,128)(2,1)S(1)} collective-permute-done((bf16[96,1152]{1,0:T(8,128)(2,1)S(1)}, bf16[96,1152]{1,0:T(8,128)(2,1)S(1)}, u32[]{:S(2)}, u32[]{:S(2)}) %collective-permute-start) | collective-permute-done | bytes 221216 | tf_op jit(solution)/shard_map/ppermute | solution.py:508
  30.6 11.8 %collective-permute-done.10 = bf16[16,128]{1,0:T(8,128)(2,1)S(1)} collective-permute-done((bf16[16,128]{1,0:T(8,128)(2,1)S(1)}, bf16[16,128]{1,0:T(8,128)(2,1)S(1)}, u32[]{:S(2)}, u32[]{:S(2)}) %collective-permute-start.10) | collective-permute-done | bytes 4128 | tf_op jit(solution)/shard_map/ppermute | solution.py:508
  43.3 4.5 %collective-permute-done.11 = bf16[16,128]{1,0:T(8,128)(2,1)S(1)} collective-permute-done((bf16[16,128]{1,0:T(8,128)(2,1)S(1)}, bf16[16,128]{1,0:T(8,128)(2,1)S(1)}, u32[]{:S(2)}, u32[]{:S(2)}) %collective-permute-start.11) | collective-permute-done | bytes 4128 | tf_op jit(solution)/shard_map/ppermute | solution.py:508
  48.1 12.4 %collective-permute-done.2 = bf16[96,1152]{1,0:T(8,128)(2,1)S(1)} collective-permute-done((bf16[96,1152]{1,0:T(8,128)(2,1)S(1)}, bf16[96,1152]{1,0:T(8,128)(2,1)S(1)}, u32[]{:S(2)}, u32[]{:S(2)}) %collective-permute-start.2) | collective-permute-done | bytes 221216 | tf_op jit(solution)/shard_map/ppermute | solution.py:508
  60.7 6.1 %collective-permute-done.24 = bf16[384,384]{1,0:T(8,128)(2,1)S(1)} collective-permute-done((bf16[384,384]{1,0:T(8,128)(2,1)S(1)}, bf16[384,384]{1,0:T(8,128)(2,1)S(1)}, u32[]{:S(2)}, u32[]{:S(2)}) %collective-permute-start.24) | collective-permute-done | bytes 294944 | tf_op jit(solution)/shard_map/ppermute | solution.py:508
  72.8 8.3 %collective-permute-done.3.across = bf16[3,48,1152]{2,1,0:T(8,128)(2,1)S(1)} collective-permute-done((bf16[3,48,1152]{2,1,0:T(8,128)(2,1)S(1)}, bf16[3,48,1152]{2,1,0:T(8,128)(2,1)S(1)}, u32[]{:S(2)}, u32[]{:S(2)}) %collective-permute-start.3) | collective-permute-done | bytes 331808 | tf_op jit(solution)/shard_map/ppermute | solution.py:508
  83.7 7.7 %collective-permute-done.26.along = bf16[3,192,384]{2,1,0:T(8,128)(2,1)} collective-permute-done((bf16[3,192,384]{2,1,0:T(8,128)(2,1)S(1)}, bf16[3,192,384]{2,1,0:T(8,128)(2,1)}, u32[]{:S(2)}, u32[]{:S(2)}) %collective-permute-start.26) | collective-permute-done | bytes 442400 | tf_op jit(solution)/shard_map/ppermute | solution.py:508
  97.5 4.0 %assemble.3.wq.wk.wv = bf16[768,2304]{1,0:T(8,128)(2,1)} custom-call(s32[4]{0:T(128)} %pad_add_fusion.at_r, bf16[96,2304]{1,0:T(8,128)(2,1)} %own.2, bf16[3,96,1152]{2,1,0:T(8,128)(2,1)} %copy-done.2, bf16[3,48,1152]{2,1,0:T(8,128)(2,1)} %copy-done.18, bf16[3,48,1152]{2,1,0:T(8,128)(2,1)} %copy-done.19, bf16[96,2304]{1,0:T(8,128)(2,1)} %collective-permute-done.5.own2, ...), custom_call_target="tpu_custom_call" | custom-call | bytes 7077888 | tf_op jit(solution)/shard_map/assemble/pallas_call | solution.py:360
  102.8 19.3 %attend.1 = (bf16[1024,768]{1,0:T(8,128)(2,1)}, bf16[1024,768]{1,0:T(8,128)(2,1)}, bf16[1024,768]{1,0:T(8,128)(2,1)}, bf16[1024,768]{1,0:T(8,128)(2,1)}, f32[2,3,8,512]{3,2,1,0:T(8,128)}) custom-call(bf16[1024,768]{1,0:T(8,128)(2,1)} %tok.5, bf16[768,2304]{1,0:T(8,128)(2,1)} %assemble.3.wq.wk.wv, bf16[768,2304]{1,0:T(8,128)(2,1)} %assemble.3.wq.wk.wv, ...), custom_call_target="tpu_custom_call" | custom-call | flops 20000000000 | bytes 12000000 | tf_op jit(solution)/shard_map/attend/pallas_call | solution.py:71
  122.1 4.8 %assemble.5.wd = bf16[3072,768]{1,0:T(8,128)(2,1)} custom-call(s32[4]{0:T(128)} %pad_add_fusion.at_r, bf16[384,768]{1,0:T(8,128)(2,1)} %own.3, bf16[3,384,384]{2,1,0:T(8,128)(2,1)} %copy-done.1, bf16[3,192,384]{2,1,0:T(8,128)(2,1)} %collective-permute-done.25.across, bf16[3,192,384]{2,1,0:T(8,128)(2,1)} %collective-permute-done.26.along, ...), custom_call_target="tpu_custom_call" | custom-call | bytes 9437184 | tf_op jit(solution)/shard_map/assemble/pallas_call | solution.py:360
  128.0 5.6 %assemble.4.wou = bf16[768,3840]{1,0:T(8,128)(2,1)} custom-call(s32[4]{0:T(128)} %pad_add_fusion.at_r, bf16[96,3840]{1,0:T(8,128)(2,1)} %copy-done.3, bf16[3,96,1920]{2,1,0:T(8,128)(2,1)} %copy-done, bf16[3,48,1920]{2,1,0:T(8,128)(2,1)} %collective-permute-done.16.across, bf16[3,48,1920]{2,1,0:T(8,128)(2,1)} %collective-permute-done.17.along, ...), custom_call_target="tpu_custom_call" | custom-call | bytes 11796480 | tf_op jit(solution)/shard_map/assemble/pallas_call | solution.py:360
  133.6 42.7 %middle.1 = (bf16[1024,768]{1,0:T(8,128)(2,1)}, bf16[1024,768]{1,0:T(8,128)(2,1)}, bf16[1024,3072]{1,0:T(8,128)(2,1)}, bf16[1024,768]{1,0:T(8,128)(2,1)}, bf16[1...) custom-call(bf16[1024,768]{1,0:T(8,128)(2,1)} %tok.5, ...), custom_call_target="tpu_custom_call" | custom-call | flops 43000000512 | bytes 30000000 | tf_op jit(solution)/shard_map/middle/pallas_call | solution.py:325
  178.8 36.8 %attend_back.1 = (bf16[2,2,4,160,384]{4,3,2,1,0:T(8,128)(2,1)}, bf16[2,2,4,160,384]{4,3,2,1,0:T(8,128)(2,1)}, bf16[1024,768]{1,0:T(8,128)(2,1)}) custom-call(s32[4]{0:T(128)} %pad_add_fusion.at_r, bf16[1024,768]{1,0:T(8,128)(2,1)} %get-tuple-element.41.q_r, bf16[1024,768]{1,0:T(8,128)(2,1)} %get-tuple-element.42.k_r, ...), custom_call_target="tpu_custom_call" | custom-call | flops 33999998976 | bytes 16000000 | tf_op jit(solution)/shard_map/attend_back/pallas_call | solution.py:229
  216.0 12.7 %grad_down.1 = (bf16[2,2,4,192,384]{4,3,2,1,0:T(8,128)(2,1)}, bf16[2,2,4,192,384]{4,3,2,1,0:T(8,128)(2,1)}) custom-call(s32[4]{0:T(128)} %pad_add_fusion.at_r, bf16[1024,3072]{1,0:T(8,128)(2,1)} %get-tuple-element.60.hid, bf16[1024,768]{1,0:T(8,128)(2,1)} %get-tuple-element.61.gd), custom_call_target="tpu_custom_call" | custom-call | flops 8999999488 | bytes 14000000 | tf_op jit(solution)/shard_map/grad_down/pallas_call | solution.py:401
  228.9 18.0 %grad_up.1 = (bf16[2,2,4,48,1920]{4,3,2,1,0:T(8,128)(2,1)}, bf16[2,2,4,48,1920]{4,3,2,1,0:T(8,128)(2,1)}) custom-call(s32[4]{0:T(128)} %pad_add_fusion.at_r, bf16[1024,768]{1,0:T(8,128)(2,1)} %get-tuple-element.39.ctx.ctx_r, bf16[1024,768]{1,0:T(8,128)(2,1)} %get-tuple-element.46.gb, bf16[1024,768]{1,0:T(8,128)(2,1)} %get-tuple-element.54.low, ...), custom_call_target="tpu_custom_call" | custom-call | flops 11000000512 | bytes 16000000 | tf_op jit(solution)/shard_map/grad_up/pallas_call | solution.py:468
  253.4 9.7 %collective-permute-done.32 = bf16[4,160,384]{2,1,0:T(8,128)(2,1)S(1)} collective-permute-done((bf16[4,160,384]{2,1,0:T(8,128)(2,1)S(1)}, bf16[4,160,384]{2,1,0:T(8,128)(2,1)S(1)}, u32[]{:S(2)}, u32[]{:S(2)}) %collective-permute-start.32) | collective-permute-done | bytes 491552 | tf_op jit(solution)/shard_map/ppermute | solution.py:508
  265.8 8.0 %collective-permute-done.34 = bf16[2,160,384]{2,1,0:T(8,128)(2,1)S(1)} collective-permute-done((bf16[2,160,384]{2,1,0:T(8,128)(2,1)S(1)}, bf16[2,160,384]{2,1,0:T(8,128)(2,1)S(1)}, u32[]{:S(2)}, u32[]{:S(2)}) %collective-permute-start.34) | collective-permute-done | bytes 245792 | tf_op jit(solution)/shard_map/ppermute | solution.py:508
  282.5 10.4 %collective-permute-done.36 = bf16[2,160,384]{2,1,0:T(8,128)(2,1)S(1)} collective-permute-done((bf16[2,160,384]{2,1,0:T(8,128)(2,1)S(1)}, bf16[2,160,384]{2,1,0:T(8,128)(2,1)S(1)}, u32[]{:S(2)}, u32[]{:S(2)}) %collective-permute-start.36) | collective-permute-done | bytes 245792 | tf_op jit(solution)/shard_map/ppermute | solution.py:508
  292.9 2.7 collective-permute-done.42
  300.0 10.8 %collective-permute-done.44 = bf16[2,48,1920]{2,1,0:T(8,128)(2,1)S(1)} collective-permute-done((bf16[2,48,1920]{2,1,0:T(8,128)(2,1)S(1)}, bf16[2,48,1920]{2,1,0:T(8,128)(2,1)S(1)}, u32[]{:S(2)}, u32[]{:S(2)}) %collective-permute-start.44) | collective-permute-done | bytes 368672 | tf_op jit(solution)/shard_map/ppermute | solution.py:508
  313.3 2.7 collective-permute-done.38.a2
  324.4 8.1 %collective-permute-done.56 = bf16[2,192,384]{2,1,0:T(8,128)(2,1)S(1)} collective-permute-done((bf16[2,192,384]{2,1,0:T(8,128)(2,1)S(1)}, bf16[2,192,384]{2,1,0:T(8,128)(2,1)S(1)}, u32[]{:S(2)}, u32[]{:S(2)}) %collective-permute-start.56) | collective-permute-done | bytes 294944 | tf_op jit(solution)/shard_map/ppermute | solution.py:508
  352.8 2.4 finish_up.1
  (271 shorter events, 86.2 us)
Async XLA Ops:
  2.7 25.0 %collective-permute-start.22 = (bf16[384,384]{1,0:T(8,128)(2,1)}, bf16[384,384]{1,0:T(8,128)(2,1)S(1)}, u32[]{:S(2)}, u32[]{:S(2)}) collective-permute-start(bf16[384,384]{1,0:T(8,128)(2,1)} %pad_maximum_fusion.5), channel_id=1, source_target_pairs={{0,2},{1,3},{2,4},{3,5},{4,6},{5,7},{6,0},{7,1},{8,10},{9,11},{10,... | collective-permute-start | bytes 884744 | tf_op jit(solution)/shard_map/ppermute | solution.py:508
  6.1 36.3 %collective-permute-start.13 = (bf16[96,1920]{1,0:T(8,128)(2,1)S(1)}, bf16[96,1920]{1,0:T(8,128)(2,1)S(1)}, u32[]{:S(2)}, u32[]{:S(2)}) collective-permute-start(bf16[96,1920]{1,0:T(8,128)(2,1)S(1)} %pad_maximum_fusion.3), channel_id=1, source_target_pairs={{0,2},{1,3},{2,4},{3,5},{4,6},{5,7},{6,0},{7,1},{8,10},{9,11},{10,... | collective-permute-start | bytes 1105928 | tf_op jit(solution)/shard_map/ppermute | solution.py:508
  7.7 64.5 %collective-permute-start.5 = (bf16[96,2304]{1,0:T(8,128)(2,1)S(1)}, bf16[96,2304]{1,0:T(8,128)(2,1)}, u32[]{:S(2)}, u32[]{:S(2)}) collective-permute-start(bf16[96,2304]{1,0:T(8,128)(2,1)S(1)} %copy-done.7), channel_id=1, source_target_pairs={{0,1},{1,0},{2,3},{3,2},{4,5},{5,4},{6,7},{7,6},{8,9},{9,8},{10,11... | collective-permute-start | bytes 1327112 | tf_op jit(solution)/shard_map/ppermute | solution.py:508
  7.8 19.8 %collective-permute-start = (bf16[96,1152]{1,0:T(8,128)(2,1)S(1)}, bf16[96,1152]{1,0:T(8,128)(2,1)S(1)}, u32[]{:S(2)}, u32[]{:S(2)}) collective-permute-start(bf16[96,1152]{1,0:T(8,128)(2,1)S(1)} %pad_maximum_fusion.8), channel_id=1, source_target_pairs={{0,2},{1,3},{2,4},{3,5},{4,6},{5,7},{6,0},{7,1},{8,10},{9,11},{10,... | collective-permute-start | bytes 663560 | tf_op jit(solution)/shard_map/ppermute | solution.py:508
  9.7 19.3 %collective-permute-start.9 = (bf16[16,128]{1,0:T(8,128)(2,1)S(1)}, bf16[16,128]{1,0:T(8,128)(2,1)S(1)}, u32[]{:S(2)}, u32[]{:S(2)}) collective-permute-start(bf16[16,128]{1,0:T(8,128)(2,1)S(1)} %get-tuple-element.131), channel_id=1, source_target_pairs={{0,2},{1,3},{2,4},{3,5},{4,6},{5,7},{6,0},{7,1},{8,10},{9,11},{10,... | collective-permute-start | bytes 12296 | tf_op jit(solution)/shard_map/ppermute | solution.py:508
  27.6 20.2 %collective-permute-start.23 = (bf16[384,384]{1,0:T(8,128)(2,1)S(1)}, bf16[384,384]{1,0:T(8,128)(2,1)S(1)}, u32[]{:S(2)}, u32[]{:S(2)}) collective-permute-start(bf16[384,384]{1,0:T(8,128)(2,1)S(1)} %collective-permute-done.22), channel_id=1, source_target_pairs={{0,2},{1,3},{2,4},{3,5},{4,6},{5,7},{6,0},{7,1},{8,10},{9,11},{10,... | collective-permute-start | bytes 884744 | tf_op jit(solution)/shard_map/ppermute | solution.py:508
  42.4 18.2 %collective-permute-start.14 = (bf16[96,1920]{1,0:T(8,128)(2,1)S(1)}, bf16[96,1920]{1,0:T(8,128)(2,1)S(1)}, u32[]{:S(2)}, u32[]{:S(2)}) collective-permute-start(bf16[96,1920]{1,0:T(8,128)(2,1)S(1)} %collective-permute-done.13), channel_id=1, source_target_pairs={{0,2},{1,3},{2,4},{3,5},{4,6},{5,7},{6,0},{7,1},{8,10},{9,11},{10,... | collective-permute-start | bytes 1105928 | tf_op jit(solution)/shard_map/ppermute | solution.py:508
  42.4 18.1 %collective-permute-start.2 = (bf16[96,1152]{1,0:T(8,128)(2,1)S(1)}, bf16[96,1152]{1,0:T(8,128)(2,1)S(1)}, u32[]{:S(2)}, u32[]{:S(2)}) collective-permute-start(bf16[96,1152]{1,0:T(8,128)(2,1)S(1)} %collective-permute-done.1), channel_id=1, source_target_pairs={{0,2},{1,3},{2,4},{3,5},{4,6},{5,7},{6,0},{7,1},{8,10},{9,11},{10,... | collective-permute-start | bytes 663560 | tf_op jit(solution)/shard_map/ppermute | solution.py:508
  47.9 18.9 %collective-permute-start.24 = (bf16[384,384]{1,0:T(8,128)(2,1)S(1)}, bf16[384,384]{1,0:T(8,128)(2,1)S(1)}, u32[]{:S(2)}, u32[]{:S(2)}) collective-permute-start(bf16[384,384]{1,0:T(8,128)(2,1)S(1)} %collective-permute-done.23), channel_id=1, source_target_pairs={{0,2},{1,3},{2,4},{3,5},{4,6},{5,7},{6,0},{7,1},{8,10},{9,11},{10,... | collective-permute-start | bytes 884744 | tf_op jit(solution)/shard_map/ppermute | solution.py:508
  48.0 21.3 %collective-permute-start.12 = (bf16[4,16,128]{2,0,1:T(4,128)(2,1)S(1)}, bf16[4,16,128]{2,0,1:T(4,128)(2,1)S(1)}, u32[]{:S(2)}, u32[]{:S(2)}) collective-permute-start(bf16[4,16,128]{2,0,1:T(4,128)(2,1)S(1)} %pad_maximum_fusion.9), channel_id=1, source_target_pairs={{0,1},{1,0},{2,3},{3,2},{4,5},{5,4},{6,7},{7,6},{8,9},{9,8},{10,11... | collective-permute-start | bytes 49160 | tf_op jit(solution)/shard_map/ppermute | solution.py:508
  72.1 22.4 %collective-permute-start.6 = (bf16[3,96,1152]{2,1,0:T(8,128)(2,1)S(1)}, bf16[3,96,1152]{2,1,0:T(8,128)(2,1)S(1)}, u32[]{:S(2)}, u32[]{:S(2)}) collective-permute-start(bf16[3,96,1152]{2,1,0:T(8,128)(2,1)S(1)} %pad_maximum_fusion.2.ring), channel_id=1, source_target_pairs={{0,1},{1,0},{2,3},{3,2},{4,5},{5,4},{6,7},{7,6},{8,9},{9,8},{10,11... | collective-permute-start | bytes 1990664 | tf_op jit(solution)/shard_map/ppermute | solution.py:508
  72.3 29.2 %collective-permute-start.27 = (bf16[384,768]{1,0:T(8,128)(2,1)}, bf16[384,768]{1,0:T(8,128)(2,1)}, u32[]{:S(2)}, u32[]{:S(2)}) collective-permute-start(bf16[384,768]{1,0:T(8,128)(2,1)} %own.3), channel_id=1, source_target_pairs={{0,1},{1,0},{2,3},{3,2},{4,5},{5,4},{6,7},{7,6},{8,9},{9,8},{10,11... | collective-permute-start | bytes 1769480 | tf_op jit(solution)/shard_map/ppermute | solution.py:508
  101.5 25.4 %collective-permute-start.18 = (bf16[96,3840]{1,0:T(8,128)(2,1)S(1)}, bf16[96,3840]{1,0:T(8,128)(2,1)S(1)}, u32[]{:S(2)}, u32[]{:S(2)}) collective-permute-start(bf16[96,3840]{1,0:T(8,128)(2,1)S(1)} %constant_dynamic-update-slice_fusion.own), channel_id=1, source_target_pairs={{0,1},{1,0},{2,3},{3,2},{4,5},{5,4},{6,7},{7,6},{8,9},{9,8},{10,11... | collective-permute-start | bytes 2211848 | tf_op jit(solution)/shard_map/ppermute | solution.py:508
  101.6 20.5 %collective-permute-start.28 = (bf16[3,384,384]{2,1,0:T(8,128)(2,1)S(1)}, bf16[3,384,384]{2,1,0:T(8,128)(2,1)}, u32[]{:S(2)}, u32[]{:S(2)}) collective-permute-start(bf16[3,384,384]{2,1,0:T(8,128)(2,1)S(1)} %pad_maximum_fusion.1.ring), channel_id=1, source_target_pairs={{0,1},{1,0},{2,3},{3,2},{4,5},{5,4},{6,7},{7,6},{8,9},{9,8},{10,11... | collective-permute-start | bytes 2654216 | tf_op jit(solution)/shard_map/ppermute | solution.py:508
  102.3 24.7 %collective-permute-start.19 = (bf16[3,96,1920]{2,1,0:T(8,128)(2,1)S(1)}, bf16[3,96,1920]{2,1,0:T(8,128)(2,1)}, u32[]{:S(2)}, u32[]{:S(2)}) collective-permute-start(bf16[3,96,1920]{2,1,0:T(8,128)(2,1)S(1)} %pad_maximum_fusion.ring), channel_id=1, source_target_pairs={{0,1},{1,0},{2,3},{3,2},{4,5},{5,4},{6,7},{7,6},{8,9},{9,8},{10,11... | collective-permute-start | bytes 3317768 | tf_op jit(solution)/shard_map/ppermute | solution.py:508
  102.3 24.7 %collective-permute-start.20 = (bf16[3,48,1920]{2,1,0:T(8,128)(2,1)}, bf16[3,48,1920]{2,1,0:T(8,128)(2,1)S(1)}, u32[]{:S(2)}, u32[]{:S(2)}) collective-permute-start(bf16[3,48,1920]{2,1,0:T(8,128)(2,1)} %collective-permute-done.16.across), channel_id=1, source_target_pairs={{0,1},{1,0},{2,3},{3,2},{4,5},{5,4},{6,7},{7,6},{8,9},{9,8},{10,11... | collective-permute-start | bytes 1658888 | tf_op jit(solution)/shard_map/ppermute | solution.py:508
  102.8 24.2 %collective-permute-start.21 = (bf16[3,48,1920]{2,1,0:T(8,128)(2,1)}, bf16[3,48,1920]{2,1,0:T(8,128)(2,1)}, u32[]{:S(2)}, u32[]{:S(2)}) collective-permute-start(bf16[3,48,1920]{2,1,0:T(8,128)(2,1)} %collective-permute-done.17.along), channel_id=1, source_target_pairs={{0,1},{1,0},{2,3},{3,2},{4,5},{5,4},{6,7},{7,6},{8,9},{9,8},{10,11... | collective-permute-start | bytes 1658888 | tf_op jit(solution)/shard_map/ppermute | solution.py:508
  215.7 31.4 %collective-permute-start.31 = (bf16[2,2,4,160,384]{4,3,2,1,0:T(8,128)(2,1)}, bf16[2,2,4,160,384]{4,3,2,1,0:T(8,128)(2,1)}, u32[]{:S(2)}, u32[]{:S(2)}) collective-permute-start(bf16[2,2,4,160,384]{4,3,2,1,0:T(8,128)(2,1)} %get-tuple-element.51), channel_id=1, source_target_pairs={{0,1},{1,0},{2,3},{3,2},{4,5},{5,4},{6,7},{7,6},{8,9},{9,8},{10,11... | collective-permute-start | bytes 5898248 | tf_op jit(solution)/shard_map/ppermute | solution.py:508
  228.7 22.5 %collective-permute-start.51 = (bf16[2,2,4,192,384]{4,3,2,1,0:T(8,128)(2,1)}, bf16[2,2,4,192,384]{4,3,2,1,0:T(8,128)(2,1)S(1)}, u32[]{:S(2)}, u32[]{:S(2)}) collective-permute-start(bf16[2,2,4,192,384]{4,3,2,1,0:T(8,128)(2,1)} %get-tuple-element.63), channel_id=1, source_target_pairs={{0,1},{1,0},{2,3},{3,2},{4,5},{5,4},{6,7},{7,6},{8,9},{9,8},{10,11... | collective-permute-start | bytes 7077896 | tf_op jit(solution)/shard_map/ppermute | solution.py:508
  246.9 29.4 %collective-permute-start.41 = (bf16[2,2,4,48,1920]{4,3,2,1,0:T(8,128)(2,1)}, bf16[2,2,4,48,1920]{4,3,2,1,0:T(8,128)(2,1)S(1)}, u32[]{:S(2)}, u32[]{:S(2)}) collective-permute-start(bf16[2,2,4,48,1920]{4,3,2,1,0:T(8,128)(2,1)} %get-tuple-element.57), channel_id=1, source_target_pairs={{0,1},{1,0},{2,3},{3,2},{4,5},{5,4},{6,7},{7,6},{8,9},{9,8},{10,11... | collective-permute-start | bytes 8847368 | tf_op jit(solution)/shard_map/ppermute | solution.py:508
  251.5 23.7 %collective-permute-start.52 = (bf16[4,192,384]{2,1,0:T(8,128)(2,1)S(1)}, bf16[4,192,384]{2,1,0:T(8,128)(2,1)S(1)}, u32[]{:S(2)}, u32[]{:S(2)}) collective-permute-start(bf16[4,192,384]{2,1,0:T(8,128)(2,1)S(1)} %get-tuple-element.70), channel_id=1, source_target_pairs={{0,8},{1,9},{2,10},{3,11},{4,12},{5,13},{6,14},{7,15},{8,0},{9,1},... | collective-permute-start | bytes 1769480 | tf_op jit(solution)/shard_map/ppermute | solution.py:508
  253.3 22.5 %collective-permute-start.53 = (bf16[4,192,384]{2,1,0:T(8,128)(2,1)S(1)}, bf16[4,192,384]{2,1,0:T(8,128)(2,1)S(1)}, u32[]{:S(2)}, u32[]{:S(2)}) collective-permute-start(bf16[4,192,384]{2,1,0:T(8,128)(2,1)S(1)} %get-tuple-element.71), channel_id=1, source_target_pairs={{0,16},{1,17},{2,18},{3,19},{4,20},{5,21},{6,22},{7,23},{8,24},{9,... | collective-permute-start | bytes 1769480 | tf_op jit(solution)/shard_map/ppermute | solution.py:508
  277.9 17.7 %collective-permute-start.42 = (bf16[4,48,1920]{2,1,0:T(8,128)(2,1)S(1)}, bf16[4,48,1920]{2,1,0:T(8,128)(2,1)S(1)}, u32[]{:S(2)}, u32[]{:S(2)}) collective-permute-start(bf16[4,48,1920]{2,1,0:T(8,128)(2,1)S(1)} %get-tuple-element.66), channel_id=1, source_target_pairs={{0,8},{1,9},{2,10},{3,11},{4,12},{5,13},{6,14},{7,15},{8,0},{9,1},... | collective-permute-start | bytes 2211848 | tf_op jit(solution)/shard_map/ppermute | solution.py:508
  299.9 22.1 %collective-permute-start.55 = (bf16[2,192,384]{2,1,0:T(8,128)(2,1)S(1)}, bf16[2,192,384]{2,1,0:T(8,128)(2,1)S(1)}, u32[]{:S(2)}, u32[]{:S(2)}) collective-permute-start(bf16[2,192,384]{2,1,0:T(8,128)(2,1)S(1)} %add_convert_fusion.11), channel_id=1, source_target_pairs={{0,2},{1,3},{2,4},{3,5},{4,6},{5,7},{6,0},{7,1},{8,10},{9,11},{10,... | collective-permute-start | bytes 884744 | tf_op jit(solution)/shard_map/ppermute | solution.py:508
  (76 other events, 706.9 us)

commit v3 on v1

v3 whole, which is shorter than its diff:
```python
import functools

import jax
import jax.numpy as jnp
from jax import lax
from jax.experimental import pallas as pl
from jax.experimental.pallas import tpu as pltpu
from jax.sharding import PartitionSpec as P

HD = 64
GW = 256
SCALE = 0.125 * 1.4426950408889634
BIG = 1e30
VMEM_LIMIT = 60 * 1024 * 1024
bf16 = jnp.bfloat16
f32 = jnp.float32
SMEM = pl.BlockSpec(memory_space=pltpu.SMEM)
VMEM = pl.BlockSpec(memory_space=pltpu.VMEM)


def nn(a, b):
    return lax.dot_general(a, b, (((1,), (0,)), ((), ())), preferred_element_type=f32)


def nt(a, b):
    return lax.dot_general(a, b, (((1,), (1,)), ((), ())), preferred_element_type=f32)


def tn(a, b):
    return lax.dot_general(a, b, (((0,), (0,)), ((), ())), preferred_element_type=f32)


def params(**more):
    return pltpu.CompilerParams(vmem_limit_bytes=VMEM_LIMIT, **more)


def cost(flops, moved):
    return pl.CostEstimate(flops=flops, bytes_accessed=moved, transcendentals=0)


def attend_kernel(tok, wq, wk, wv, vecs, aq, ak, q_o, k_o, v_o, ctx_o, lse_o):
    x = tok[...]
    q = (nn(x, wq[...]) + vecs[0:1, :].astype(f32)).astype(bf16)
    k = nn(x, wk[...]).astype(bf16)
    v = (nn(x, wv[...]) + vecs[1:2, :].astype(f32)).astype(bf16)
    q_o[...] = q
    k_o[...] = k
    v_o[...] = v
    length, width = q.shape
    lane = lax.broadcasted_iota(jnp.int32, (length, width), 1) // HD
    slot = lax.broadcasted_iota(jnp.int32, (length, 128), 1)
    acc = None
    scale = jnp.zeros((length, width), f32)
    stat = jnp.zeros((length, 128), f32)
    for h in range(width // HD):
        mine = lane == h
        qa = jnp.where(mine, q, aq[...])
        ka = jnp.where(mine, k, ak[...])
        va = jnp.where(mine, v, jnp.zeros_like(v))
        t = nt(qa, ka) * SCALE
        m = jnp.max(t, axis=1, keepdims=True)
        p = jnp.exp2(t - m)
        total = jnp.sum(p, axis=1, keepdims=True)
        part = nn(p.astype(bf16), va)
        acc = part if acc is None else acc + part
        scale = jnp.where(mine, 1.0 / total, scale)
        stat = jnp.where(slot == h, m + jnp.log2(total), stat)
    ctx_o[...] = (acc * scale).astype(bf16)
    lse_o[0] = stat.T[:8]


def attend(g, tokens, w, vecs, aq, ak, length):
    rows, width = tokens.shape
    groups = width // GW
    seqs = rows // length
    col = lambda o: pl.BlockSpec((width, GW), lambda b: (0, o * groups + g))
    seq = pl.BlockSpec((length, width), lambda b: (b, 0))
    blk = pl.BlockSpec((length, GW), lambda b: (b, 0))
    act = jax.ShapeDtypeStruct((rows, GW), bf16)
    return pl.pallas_call(
        attend_kernel,
        grid=(seqs,),
        in_specs=[seq, col(0), col(1), col(2), pl.BlockSpec((16, GW), lambda b: (0, g)), blk, blk],
        out_specs=[blk, blk, blk, blk, pl.BlockSpec((1, 8, length), lambda b: (b, 0, 0))],
        out_shape=[act, act, act, act, jax.ShapeDtypeStruct((seqs, 8, length), f32)],
        compiler_params=params(),
        cost_estimate=cost(4_000_000_000, 5_000_000),
        name="attend",
    )(tokens, w, w, w, vecs, aq, ak)


def owner_of(s, at_r):
    return lax.rem(s // 2 - at_r[2] + 4, 4), at_r[3] != s % 2


def select_lanes(s, piece, width):
    i = lax.broadcasted_iota(jnp.int32, (128, width), 0)
    j = lax.broadcasted_iota(jnp.int32, (128, width), 1)
    return ((j == s * piece + i) & (i < piece)).astype(f32).astype(bf16)


def attend_back_kernel(mode, at_r, q_r, k_r, v_r, do_r, ctx_r, lse_r, aq, ak, tok, wq, wk, wv, dx_i, *rest):
    b = pl.program_id(0)
    last = b == pl.num_programs(0) - 1
    if mode == "plain":
        dw_o, dx_o, db_o, dw_s = rest
    elif mode == "first":
        own_o, other_o, dx_o, db_o, dw_s = rest
    elif mode == "second":
        _, _, own_o, other_o, dx_o, db_o, dw_s = rest
    else:
        db0, db1, tbl, own_o, other_o, dx_o, db_o, dw_s = rest
    q, k, v, do = q_r[...], k_r[...], v_r[...], do_r[...]
    length, width = q.shape
    lane = lax.broadcasted_iota(jnp.int32, (length, width), 1) // HD
    sel = lax.broadcasted_iota(jnp.int32, (8, width), 1) // HD == lax.broadcasted_iota(jnp.int32, (8, width), 0)
    sel = sel.astype(f32).astype(bf16)
    prod = do.astype(f32) * ctx_r[...].astype(f32)
    hi = prod.astype(bf16)
    lo = (prod - hi.astype(f32)).astype(bf16)
    delta = nt(sel, hi) + nt(sel, lo)
    dq = dk = dv = None
    zero = jnp.zeros_like(q)
    for h in range(width // HD):
        mine = lane == h
        qa = jnp.where(mine, q, aq[...])
        ka = jnp.where(mine, k, ak[...])
        va = jnp.where(mine, v, zero)
        p = jnp.exp2(nt(ka, qa) * SCALE - lse_r[0, h : h + 1, :])
        dp = nt(va, do)
        ds = (p * (dp - delta[h : h + 1, :])).astype(bf16)
        dv_h = nn(p.astype(bf16), jnp.where(mine, do, zero))
        dk_h = nn(ds, jnp.where(mine, q, zero))
        dq_h = tn(ds, jnp.where(mine, k, zero))
        dv = dv_h if dv is None else dv + dv_h
        dk = dk_h if dk is None else dk + dk_h
        dq = dq_h if dq is None else dq + dq_h
    dq = (dq * 0.125).astype(bf16)
    dk = (dk * 0.125).astype(bf16)
    dv = dv.astype(bf16)
    back = jnp.concatenate([dq, dk, dv], axis=1)
    dw = tn(tok[...], back)
    dx = nt(dq, wq[...]) + nt(dk, wk[...]) + nt(dv, wv[...])
    dx_o[...] = (dx_i[...].astype(f32) + dx).astype(dx_o.dtype)
    sums = jnp.sum(back.astype(f32), axis=0, keepdims=True)

    @pl.when(b == 0)
    def _():
        dw_s[...] = dw
        db_o[...] = sums

    @pl.when(b > 0)
    def _():
        dw_s[...] += dw
        db_o[...] += sums

    @pl.when(last)
    def _():
        if mode == "plain":
            for i in range(3):
                dw_o[i] = dw_s[:, i * width : (i + 1) * width].astype(bf16)
            return
        res = dw_s[...].astype(bf16)
        piece = res.shape[0] // 8
        half, wide = piece // 2, res.shape[1] // 2
        for s in range(8):
            kk, far = owner_of(s, at_r)
            for ab, turn in ((0, at_r[1]), (1, at_r[0])):
                for h in range(2):
                    val = res[s * piece + ab * half : s * piece + (ab + 1) * half, h * wide : (h + 1) * wide]
                    rel = lax.rem(h + turn, 2)
                    for ref, cond in ((other_o, far), (own_o, ~far)):

                        @pl.when(cond)
                        def _(val=val, rel=rel, kk=kk, ab=ab, ref=ref):
                            ref[ab, rel, kk, 0:half] = val

        if mode == "third":
            sums = [r[...] for r in (db0, db1, db_o)]
            dbq = jnp.concatenate([r[:, :width] for r in sums], axis=1)
            dbv = jnp.concatenate([r[:, 2 * width :] for r in sums], axis=1)
            table = jnp.concatenate([dbq, dbv, tbl[...]], axis=0).astype(bf16)
            extra = jnp.zeros((4, 16, wide), bf16)
            for ab in range(2):
                for h in range(2):
                    own_o[ab, h, :, half : half + 16, :] = extra
                    other_o[ab, h, :, half : half + 16, :] = extra
            for s in range(8):
                blk = nt(table, select_lanes(s, piece, table.shape[1])).astype(bf16)
                kk, far = owner_of(s, at_r)
                for ref, cond in ((other_o, far), (own_o, ~far)):

                    @pl.when(cond)
                    def _(blk=blk, kk=kk, ref=ref):
                        ref[0, at_r[1], kk, half : half + 16, 0:128] = blk


def attend_back(mode, g, at, saved, gc, aq, ak, tokens, w, dx, length, extra=()):
    rows, width = tokens.shape
    groups = width // GW
    seqs = rows // length
    half = width // 16
    col = lambda o: pl.BlockSpec((width, GW), lambda b: (0, o * groups + g))
    seq = pl.BlockSpec((length, width), lambda b: (b, 0))
    blk = pl.BlockSpec((length, GW), lambda b: (b, 0))
    whole = lambda s: pl.BlockSpec(s, lambda b: (0,) * len(s))
    S = jax.ShapeDtypeStruct
    tall = {"first": 2 * half, "second": 2 * half, "third": half + 16, "plain": 0}[mode]
    at_row = 1 if mode == "second" else 0
    block = half + 16 if mode == "third" else half
    part = pl.BlockSpec((2, 2, 4, block, 3 * GW // 2), lambda b: (0, 0, 0, at_row, 0))
    if mode == "plain":
        out_specs, out_shape = [whole((3, width, GW))], [S((3, width, GW), bf16)]
    else:
        out_specs, out_shape = [part, part], [S((2, 2, 4, tall, 3 * GW // 2), bf16)] * 2
    out_specs += [seq, whole((1, 3 * GW))]
    out_shape += [S((rows, width), bf16 if mode == "third" or g == groups - 1 else f32), S((1, 3 * GW), f32)]
    in_specs = [SMEM, blk, blk, blk, pl.BlockSpec((length, GW), lambda b: (b, g)), blk]
    in_specs += [pl.BlockSpec((1, 8, length), lambda b: (b, 0, 0)), blk, blk, seq, col(0), col(1), col(2), seq]
    aliases = {}
    if mode == "second":
        in_specs += [pl.BlockSpec(memory_space=pl.ANY)] * 2
        aliases = {len(in_specs) - 2: 0, len(in_specs) - 1: 1}
    elif mode == "third":
        in_specs += [whole(e.shape) for e in extra]
    q, k, v, ctx, lse = saved
    return pl.pallas_call(
        functools.partial(attend_back_kernel, mode),
        grid=(seqs,),
        in_specs=in_specs,
        out_specs=out_specs,
        out_shape=out_shape,
        scratch_shapes=[pltpu.VMEM((width, 3 * GW), f32)],
        input_output_aliases=aliases,
        compiler_params=params(),
        cost_estimate=cost(8_000_000_000, 8_000_000),
        name="attend_back",
    )(at, q, k, v, gc, ctx, lse, aq, ak, tokens, w, w, w, dx, *extra)


def masks(segment_ids, valid):
    code = (segment_ids + 8 * valid).reshape(-1, 1)
    lane = lax.broadcasted_iota(jnp.int32, (1, GW), 1) % HD
    same = code == lane
    aq = same.astype(bf16)
    ak = jnp.where((lane < 16) & ~same, -BIG, 0.0).astype(bf16)
    return aq, ak


def phi(x):
    return 0.5 * (1.0 + lax.erf(x * 0.7071067811865476)), jnp.exp(-0.5 * x * x) * 0.3989422804014327


def middle_kernel(groups, tok, *refs):
    ctx_r = refs[:groups]
    cot, wo, vecs, wu, bu, wd, out_o, low_o, hid_o, gd_o, gu_o, gb_o, gc_o, vec_o, bup_o, slope = refs[groups:]
    i = pl.program_id(0)
    width = tok.shape[1]
    ff = wd.shape[0]
    step = width
    chunks = ff // step
    bo, g1, s1, bd, g2, s2 = (vecs[j : j + 1, :].astype(f32) for j in range(2, 8))
    ctx = jnp.concatenate([r[...] for r in ctx_r], axis=1)
    pre = tok[...].astype(f32) + nn(ctx, wo[...]) + bo
    mean = lambda v: jnp.mean(v, axis=1, keepdims=True)
    centre = pre - mean(pre)
    r1 = lax.rsqrt(mean(centre * centre) + 1e-05)
    n1 = centre * r1
    normed = n1 * g1 + s1
    low = normed.astype(bf16)
    low_o[...] = low
    acc = normed + bd
    for c in range(chunks):
        cols = slice(c * step, (c + 1) * step)
        hp = nn(low, wu[:, cols]) + bu[:, cols].astype(f32)
        cdf, pdf = phi(hp)
        slope[:, cols] = cdf + hp * pdf
        hid = (hp * cdf).astype(bf16)
        hid_o[:, cols] = hid
        acc = acc + nn(hid, wd[cols, :])
    centre = acc - mean(acc)
    r2 = lax.rsqrt(mean(centre * centre) + 1e-05)
    n2 = centre * r2
    out_o[...] = (n2 * g2 + s2).astype(bf16)
    ct = cot[...].astype(f32)
    e = ct * g2
    gp2 = r2 * (e - mean(e) - n2 * mean(e * n2))
    gd = gp2.astype(bf16)
    gd_o[...] = gd
    acc = gp2
    total = lambda v: jnp.sum(v, axis=0, keepdims=True)

    def put(ref, at, v):
        @pl.when(i == 0)
        def _():
            ref[at] = v

        @pl.when(i > 0)
        def _():
            ref[at] += v

    for c in range(chunks):
        cols = slice(c * step, (c + 1) * step)
        gu = (nt(gd, wd[cols, :]) * slope[:, cols]).astype(bf16)
        gu_o[:, cols] = gu
        put(bup_o, (slice(0, 1), cols), total(gu.astype(f32)))
        acc = acc + nt(gu, wu[:, cols])
    e = acc * g1
    gp1 = r1 * (e - mean(e) - n1 * mean(e * n1))
    gb = gp1.astype(bf16)
    gb_o[...] = gb
    gc_o[...] = nt(gb, wo[...]).astype(bf16)
    for at, v in enumerate((gb.astype(f32), acc * n1, acc, gd.astype(f32), ct * n2, ct)):
        put(vec_o, (slice(at, at + 1), slice(None)), total(v))


def middle(tokens, ctx, cot, wo, vecs, wu, bu, wd, tile=256):
    rows, width = tokens.shape
    ff = wd.shape[0]
    act = pl.BlockSpec((tile, width), lambda i: (i, 0))
    wide = pl.BlockSpec((tile, ff), lambda i: (i, 0))
    whole = lambda a: pl.BlockSpec(a.shape, lambda i: (0, 0), pipeline_mode=pl.Buffered(1))
    S = jax.ShapeDtypeStruct
    shapes = [(rows, width), (rows, width), (rows, ff), (rows, width), (rows, ff), (rows, width), (rows, width)]
    return pl.pallas_call(
        functools.partial(middle_kernel, len(ctx)),
        grid=(rows // tile,),
        in_specs=[act] + [pl.BlockSpec((tile, GW), lambda i: (i, 0)) for _ in ctx] + [act] + [whole(a) for a in (wo, vecs, wu, bu, wd)],
        out_specs=[act, act, wide, act, wide, act, act, pl.BlockSpec((8, width), lambda i: (0, 0)), pl.BlockSpec((8, ff), lambda i: (0, 0))],
        out_shape=[S(s, bf16) for s in shapes] + [S((8, width), f32), S((8, ff), f32)],
        scratch_shapes=[pltpu.VMEM((tile, ff), f32)],
        compiler_params=params(),
        cost_estimate=cost(30_000_000_000, 40_000_000),
        name="middle",
    )(tokens, *ctx, cot, wo, vecs, wu, bu, wd)


def grad_down_kernel(groups, at_r, *refs):
    ctx = refs[:groups]
    gb, hid, gd, own_o, other_o = refs[groups:]
    p = pl.program_id(0)
    turns = ((0, at_r[1]), (1, at_r[0]))
    wide = gd.shape[1] // 2
    tall = hid.shape[1] // 2

    @pl.when(p == 0)
    def _():
        lhs = jnp.concatenate([r[...] for r in ctx], axis=1)
        res = tn(lhs, gb[...]).astype(bf16)
        piece = res.shape[0] // 8
        half = piece // 2
        for s in range(8):
            kk, far = owner_of(s, at_r)
            for ab, turn in turns:
                for h in range(2):
                    val = res[s * piece + ab * half : s * piece + (ab + 1) * half, h * wide : (h + 1) * wide]
                    rel = lax.rem(h + turn, 2)
                    for ref, cond in ((other_o, far), (own_o, ~far)):

                        @pl.when(cond)
                        def _(val=val, rel=rel, kk=kk, ab=ab, ref=ref):
                            ref[ab, rel, kk, tall : tall + half] = val

    @pl.when(p > 0)
    def _():
        res = tn(hid[...], gd[...]).astype(bf16)
        kk = lax.rem(p - 1, 4)
        for ab, turn in turns:
            for h in range(2):
                val = res[ab * tall : (ab + 1) * tall, h * wide : (h + 1) * wide]
                rel = lax.rem(h + turn, 2)
                for ref, cond in ((other_o, p < 5), (own_o, p >= 5)):

                    @pl.when(cond)
                    def _(val=val, rel=rel, ab=ab, ref=ref):
                        ref[ab, rel, kk, 0:tall] = val


def grad_down(at, ctx, gb, hid, gd):
    rows, ff = hid.shape
    width = gd.shape[1]
    piece = ff // 8
    part = (2, 2, 4, (piece + width // 8) // 2, width // 2)

    def owner(p, at_r):
        j = jnp.maximum(p - 1, 0)
        z = lax.rem(at_r[2] + lax.rem(j, 4), 4)
        return 0, 2 * z + jnp.where(j < 4, 1 - at_r[3], at_r[3])

    whole = lambda s: pl.BlockSpec(s, lambda p, at_r: (0,) * len(s))
    return pl.pallas_call(
        functools.partial(grad_down_kernel, len(ctx)),
        grid_spec=pltpu.PrefetchScalarGridSpec(
            num_scalar_prefetch=1,
            grid=(9,),
            in_specs=[whole(c.shape) for c in ctx] + [whole(gb.shape), pl.BlockSpec((rows, piece), owner), whole(gd.shape)],
            out_specs=[whole(part), whole(part)],
        ),
        out_shape=[jax.ShapeDtypeStruct(part, bf16)] * 2,
        compiler_params=params(),
        cost_estimate=cost(9_000_000_000, 14_000_000),
        name="grad_down",
    )(at, *ctx, gb, hid, gd)


def grad_up_kernel(at_r, low, gu, own_o, other_o, turned):
    j = pl.program_id(0)
    y, x = at_r[0], at_r[1]

    @pl.when(j == 0)
    def _():
        turned[...] = low[...].T

    res = nn(turned[...], gu[...]).astype(bf16)
    step = res.shape[1]
    piece = res.shape[0] // 8
    half = piece // 2
    i, l = lax.rem(j // 4 + x, 2), lax.rem(lax.rem(j // 2, 2) + y, 2)
    col = pl.multiple_of(lax.rem(j, 2) * step, 128)
    for s in range(8):
        kk, far = owner_of(s, at_r)
        for ab, one, two in ((0, i, l), (1, l, i)):
            val = res[s * piece + ab * half : s * piece + (ab + 1) * half]
            for ref, cond in ((other_o, far), (own_o, ~far)):

                @pl.when(cond)
                def _(val=val, kk=kk, ab=ab, one=one, two=two, ref=ref):
                    ref[ab, one, two, kk, :, pl.ds(col, step)] = val


def grad_up(at, low, gu):
    rows, width = low.shape
    ff = gu.shape[1]
    step = ff // 8
    part = (2, 2, 2, 4, width // 16, ff // 4)
    whole = pl.BlockSpec(part, lambda j: (0, 0, 0, 0, 0, 0))
    return pl.pallas_call(
        grad_up_kernel,
        grid=(8,),
        in_specs=[SMEM, pl.BlockSpec((rows, width), lambda j: (0, 0)), pl.BlockSpec((rows, step), lambda j: (0, j))],
        out_specs=[whole, whole],
        out_shape=[jax.ShapeDtypeStruct(part, bf16)] * 2,
        scratch_shapes=[pltpu.VMEM((width, rows), bf16)],
        compiler_params=params(),
        cost_estimate=cost(9_000_000_000, 14_000_000),
        name="grad_up",
    )(at, low, gu)


AXES = ("rep", "shard")


def pairs(move):
    found = []
    for y in range(2):
        for x in range(2):
            for z in range(4):
                for c in range(2):
                    j, i, k, d = move(y, x, z, c)
                    found.append(((y * 2 + x) * 8 + z * 2 + c, (j * 2 + i) * 8 + k * 2 + d))
    return found


CORE = pairs(lambda y, x, z, c: (y, x, z, 1 - c))
ACROSS = pairs(lambda y, x, z, c: (y, 1 - x, z, c))
ALONG = pairs(lambda y, x, z, c: (1 - y, x, z, c))
SHIFT = [None] + [pairs(lambda y, x, z, c, n=n: (y, x, (z + n) % 4, c)) for n in (1, 2, 3)]


def send(a, where):
    return lax.ppermute(a, AXES, where)


def tie(values, *after):
    flat, tree = jax.tree.flatten(values)
    return jax.tree.unflatten(tree, lax.optimization_barrier(tuple(flat) + tuple(jax.tree.leaves(after)))[: len(flat)])


def place(own, received, at_r, rows, out, base, quarter):
    y, x, z = at_r[0], at_r[1], at_r[2]
    cols = out.shape[1]
    half = rows // 2
    out[pl.ds(pl.multiple_of(base(z), 16), rows), :] = own
    for k in range(1, 4):
        start = base(lax.rem(z - k + 4, 4))
        for ab in range(2):
            at = pl.ds(pl.multiple_of(start + ab * half, 16), half)
            if quarter:
                wide = cols // 4
                for i in range(2):
                    for l in range(2):
                        one, two = (i, l) if ab == 0 else (l, i)
                        col = (lax.rem(x + i, 2) * 2 + lax.rem(y + l, 2)) * wide
                        out[at, pl.ds(pl.multiple_of(col, 128), wide)] = received(ab, one, two, k)
            else:
                wide = cols // 2
                for one in range(2):
                    col = lax.rem((x, y)[ab] + one, 2) * wide
                    out[at, pl.ds(pl.multiple_of(col, 128), wide)] = received(ab, one, 0, k)


def assemble_half_kernel(out_rows, at_r, *refs):
    n = len(out_rows)
    outs = refs[-n:]
    c = at_r[3]
    for turn, (own, ring, far_x, far_y) in ((c, refs[:4]), (1 - c, refs[4:8])):
        off = 0
        total_half = own.shape[0] // 2
        for out, rows in zip(outs, out_rows):
            half = rows // 2

            def received(ab, one, two, k):
                if one == 0:
                    return ring[k - 1, ab * total_half + off : ab * total_half + off + half, :]
                return (far_x, far_y)[ab][k - 1, off : off + half, :]

            whole = jnp.concatenate([own[off : off + half], own[total_half + off : total_half + off + half]], axis=0)
            place(whole, received, at_r, rows, out, lambda z: (2 * z + turn) * rows, False)
            off += half


def assemble_quarter_kernel(at_r, *refs):
    out = refs[-1]
    c = at_r[3]
    for turn, (own, mine, first_a, first_b, second_a, second_b) in ((c, refs[:6]), (1 - c, refs[6:12])):
        rows = own.shape[0]
        half = rows // 2

        def received(ab, one, two, k):
            if two == 1:
                return (second_a, second_b)[ab][one, k - 1]
            if one == 1:
                return (first_a, first_b)[ab][k - 1]
            return mine[k - 1, ab * half : (ab + 1) * half, :]

        place(own[...], received, at_r, rows, out, lambda z: (2 * z + turn) * rows, True)


def assemble(kernel, at, parts, shapes):
    return pl.pallas_call(
        kernel,
        in_specs=[SMEM] + [VMEM] * len(parts),
        out_specs=[VMEM] * len(shapes),
        out_shape=[jax.ShapeDtypeStruct(s, bf16) for s in shapes],
        compiler_params=params(),
        cost_estimate=cost(0, sum(4 * s[0] * s[1] for s in shapes)),
        name="assemble",
    )(at, *parts)


def halves(w, x, y):
    half, wide = w.shape[0] // 2, w.shape[1] // 2
    a = lax.dynamic_slice(w, (0, x * wide), (half, wide))
    b = lax.dynamic_slice(w, (half, y * wide), (half, wide))
    return jnp.concatenate([a, b], axis=0)


def spread_half(ring):
    half = ring.shape[1] // 2
    return send(ring[:, :half], ACROSS), send(ring[:, half:], ALONG)


def swap(parts):
    return tuple(send(p, CORE) for p in parts)


def total(*terms):
    out = terms[0].astype(f32)
    for t in terms[1:]:
        out = out + t.astype(f32)
    return out.astype(bf16)


def finish_kernel(kind, at_r, *refs):
    y, x = at_r[0], at_r[1]
    if kind == "up":
        fa, fb, ga, gb, ha, hb, out = refs
        half, wide = out.shape[0] // 2, out.shape[1] // 4
        for i in range(2):
            for l in range(2):
                col = pl.ds(pl.multiple_of((lax.rem(x + i, 2) * 2 + lax.rem(y + l, 2)) * wide, 128), wide)
                a = ha[i] if l else (ga if i else fa)[...]
                b = hb[l] if i else (gb if l else fb)[...]
                out[0:half, col] = a.astype(f32)
                out[half:, col] = b.astype(f32)
        return
    blocks, outs = refs[:4], refs[4:]
    for ab, turn in ((0, x), (1, y)):
        one, two = (blocks[2 * ab + i][...].astype(f32) for i in range(2))
        left = jnp.where(turn == 0, one, two)
        right = jnp.where(turn == 0, two, one)
        both = jnp.concatenate([left, right], axis=1)
        if kind == "down":
            off = 0
            for out in outs:
                half = out.shape[0] // 2
                out[ab * half : (ab + 1) * half, :] = both[off : off + half]
                off += half
        elif ab == 0 and len(outs) > 1:
            outs[0][0] = both[0:48]
            outs[1][...] = left[48:64, :128]
        else:
            n = outs[0].shape[1] // 48
            for g in range(n):
                outs[0][ab, g * 48 : (g + 1) * 48] = both[g * 48 : (g + 1) * 48]


def finish(at, kind, blocks, shapes):
    return pl.pallas_call(
        functools.partial(finish_kernel, kind),
        in_specs=[SMEM] + [VMEM] * len(blocks),
        out_specs=[VMEM] * len(shapes),
        out_shape=[jax.ShapeDtypeStruct(s, f32) for s in shapes],
        compiler_params=params(),
        cost_estimate=cost(0, 4_000_000),
        name="finish_" + kind,
    )(at, *blocks)


def pack(vectors, wide):
    block = jnp.concatenate([v.reshape(-1, vectors[1].shape[0]) for v in vectors] + [wide.reshape(4, -1)], axis=0)
    return jnp.pad(block, ((0, 16 - block.shape[0]), (0, 128 - block.shape[1])))


def whole_vectors(every, z, c, piece):
    k = lax.broadcasted_iota(jnp.int32, (2, 4, 8), 1)
    d = lax.broadcasted_iota(jnp.int32, (2, 4, 8), 0)
    s = lax.broadcasted_iota(jnp.int32, (2, 4, 8), 2)
    pick = (s == 2 * ((z - k) % 4) + (c + d) % 2).astype(bf16)
    table = jnp.einsum("dks,dkrl->srl", pick, every, preferred_element_type=f32).astype(bf16)
    table = table[:, :, :piece]
    wide = table[:, 8:12].reshape(1, -1)
    return table.transpose(1, 0, 2).reshape(16, -1), wide


class HalfSum:
    def __init__(self, own, other):
        self.own, self.got = own, send(other, CORE)

    def halve(self):
        own, got = self.own, self.got
        self.sent = total(own[0, 1], got[0, 1]), total(own[1, 1], got[1, 1])
        self.far = send(self.sent[0], ACROSS), send(self.sent[1], ALONG)

    def along_z(self):
        own, got, far = self.own, self.got, self.far
        self.mine = [jnp.stack([total(own[i, 0, k], got[i, 0, k], far[i][k]) for i in range(2)]) for k in range(4)]
        self.sent = self.mine[1:]
        self.parts = [send(self.mine[k], SHIFT[k]) for k in range(1, 4)]

    def across(self):
        both = total(self.mine[0], *self.parts)
        self.sent = both[0], both[1]
        self.far = send(both[0], ALONG), send(both[1], ACROSS)

    def share(self):
        a, b = (total(self.sent[i], self.far[i]) for i in range(2))
        self.sent = a, b
        self.out = a, send(a, ACROSS), b, send(b, ALONG)


class QuarterSum:
    def __init__(self, own, other):
        self.own, self.got = own, send(other, CORE)

    def halve(self):
        own, got = self.own, self.got
        self.sent = total(own[0, 1], got[0, 1]), total(own[1, 1], got[1, 1])
        self.far = send(self.sent[0], ACROSS), send(self.sent[1], ALONG)

    def quarter(self):
        own, got, far = self.own, self.got, self.far
        part = lambda i, j: total(own[i, 0, j], got[i, 0, j], far[i][j])
        self.sent = part(0, 1), part(1, 1)
        self.near = part(0, 0), part(1, 0)
        self.far = send(self.sent[0], ALONG), send(self.sent[1], ACROSS)

    def along_z(self):
        self.mine = [jnp.stack([total(self.near[i][k], self.far[i][k]) for i in range(2)]) for k in range(4)]
        self.sent = self.mine[1:]
        self.parts = [send(self.mine[k], SHIFT[k]) for k in range(1, 4)]

    def share(self):
        both = total(self.mine[0], *self.parts)
        self.sent = both[0], both[1]
        self.far = send(both[0], ACROSS), send(both[1], ALONG)

    def share_more(self):
        a, b = (jnp.stack([self.sent[i], self.far[i]]) for i in range(2))
        self.out = self.sent + self.far + (send(a, ALONG), send(b, ACROSS))


def shards_near(
    tokens,
    cotangent,
    qkv_weight,
    query_value_bias,
    out_weight,
    out_bias,
    norm_one_gain,
    norm_one_shift,
    up_weight,
    up_bias,
    down_weight,
    down_bias,
    norm_two_gain,
    norm_two_shift,
    segment_ids,
    valid,
):
    length = segment_ids.shape[1]
    width = tokens.shape[1]
    groups = width // GW
    ff = up_bias.shape[0] * 8
    piece = out_bias.shape[0]
    r, s = lax.axis_index("rep"), lax.axis_index("shard")
    y, x, z, c = r // 2, r % 2, s // 2, s % 2
    at = jnp.stack([y, x, z, c]).astype(jnp.int32)

    held = halves(qkv_weight, x, y)
    ring = []
    for _ in range(3):
        held = send(held, SHIFT[1])
        ring.append(held)
    ring_q = jnp.stack(ring)
    far_q = spread_half(ring_q)
    parts_q = (qkv_weight, ring_q) + far_q
    (wqkv,) = assemble(
        functools.partial(assemble_half_kernel, [qkv_weight.shape[0]]), at, parts_q + swap(parts_q), [(width, 3 * width)]
    )

    block = pack(
        (query_value_bias, out_bias, norm_one_gain, norm_one_shift, down_bias, norm_two_gain, norm_two_shift), up_bias
    )
    ring_v = jnp.stack([block] + [send(block, SHIFT[k]) for k in range(1, 4)])
    vecs, bu = whole_vectors(jnp.stack([ring_v, send(ring_v, CORE)]), z, c, piece)

    half, wide = piece // 2, ff // 4
    first = lax.dynamic_slice(up_weight, (0, (2 * x + y) * wide), (piece, wide))
    first = tie(first, held)
    ring_u = jnp.stack([send(first, SHIFT[k]) for k in range(1, 4)])
    a, b = ring_u[:, :half], ring_u[:, half:]
    a2, b2 = send(a, ACROSS), send(b, ALONG)
    a4, b4 = send(jnp.stack([a, a2]), ALONG), send(jnp.stack([b, b2]), ACROSS)
    parts_u = (up_weight, ring_u, a2, b2, a4, b4)
    (wu,) = assemble(assemble_quarter_kernel, at, parts_u + swap(parts_u), [(width, ff)])

    dr = down_weight.shape[0] // 2
    both = jnp.concatenate([down_weight[:dr], out_weight[:half], down_weight[dr:], out_weight[half:]], axis=0)
    first = tie(halves(both, x, y), ring_u)
    ring_d = jnp.stack([send(first, SHIFT[k]) for k in range(1, 4)])
    far_d = spread_half(ring_d)
    parts_d = (both, ring_d) + far_d
    wd, wo = assemble(
        functools.partial(assemble_half_kernel, [2 * dr, piece]), at, parts_d + swap(parts_d), [(ff, width), (width, width)]
    )

    aq, ak = masks(segment_ids, valid)
    saved = [attend(g, tokens, wqkv, vecs, aq, ak, length) for g in range(groups)]
    ctx = [f[3] for f in saved]
    result, low, hid, gd, gu, gb, gc, vec, bup = middle(tokens, ctx, cotangent, wo, vecs, wu, bu, wd)

    own, other = grad_down(at, ctx, gb, hid, gd)
    down = HalfSum(own, other)
    own, other = grad_up(at, *tie((low, gu), other))
    up = QuarterSum(own, other)
    down.halve()
    gc = tie(gc, down.sent, other)
    own, other, dx, db0 = attend_back("first", 0, at, saved[0], gc, aq, ak, tokens, wqkv, gb, length)
    down.along_z()
    up.halve()
    gc = tie(gc, down.sent, up.sent, dx)
    own, other, dx, db1 = attend_back("second", 1, at, saved[1], gc, aq, ak, tokens, wqkv, dx, length, (own, other))
    first_two = HalfSum(own, other)
    up.quarter()
    gc = tie(gc, up.sent, dx)
    wide = bup[0].reshape(8, 4, piece).transpose(1, 0, 2).reshape(4, width)
    table = jnp.concatenate([vec[:6], wide, jnp.zeros((4, width), f32)], axis=0)
    own, other, dx, _ = attend_back(
        "third", 2, at, saved[2], gc, aq, ak, tokens, wqkv, dx, length, (db0, db1, table)
    )
    third = HalfSum(own, other)
    down.across()
    up.along_z()
    first_two.halve()
    third.halve()
    first_two.along_z()
    third.along_z()
    down.share()
    up.share()
    up.share_more()
    first_two.across()
    third.across()
    first_two.share()
    third.share()
    dwd, dwo = finish(at, "down", down.out, [down_weight.shape, out_weight.shape])
    (dwu,) = finish(at, "up", up.out, [up_weight.shape])
    (q01,) = finish(at, "qkv", first_two.out, [(2, piece, 3 * GW)])
    q2, small = finish(at, "qkv", third.out, [(2, half, 3 * GW), (16, 128)])
    by_group = [q01[:, :half], q01[:, half:], q2]
    by_group = [q.reshape(piece, 3, GW) for q in by_group]
    dwq = jnp.concatenate([q[:, i] for i in range(3) for q in by_group], axis=1)
    one = lambda i: small[i, :piece]
    return (
        result,
        dx,
        dwq,
        small[:2, :piece],
        dwo,
        one(2),
        one(3),
        one(4),
        dwu,
        small[8:12, :piece].reshape(-1),
        dwd,
        one(5),
        one(6),
        one(7),
    )


def spread(args):
    flat = [a.reshape(-1) for a in args]
    packed = jnp.concatenate(flat)
    every = lax.all_gather(packed, "shard", axis=0)
    out, at = [], 0
    for a in args:
        part = every[:, at : at + a.size].reshape((-1,) + a.shape)
        at += a.size
        out.append(jnp.moveaxis(part, 0, -2).reshape(a.shape[:-1] + (-1,)))
    return out


def shards(
    tokens,
    cotangent,
    qkv_weight,
    query_value_bias,
    out_weight,
    out_bias,
    norm_one_gain,
    norm_one_shift,
    up_weight,
    up_bias,
    down_weight,
    down_bias,
    norm_two_gain,
    norm_two_shift,
    segment_ids,
    valid,
):
    length = segment_ids.shape[1]
    width = tokens.shape[1]
    groups = width // GW
    gather = lambda a: lax.all_gather(a, "shard", axis=0, tiled=True)
    *rest, bu = spread(
        (query_value_bias, out_bias, norm_one_gain, norm_one_shift, down_bias, norm_two_gain, norm_two_shift, up_bias)
    )
    vecs = jnp.concatenate([v.reshape(-1, width) for v in rest] + [jnp.zeros((8, width), bf16)], axis=0)
    wqkv, wd, wo, wu = gather(qkv_weight), gather(down_weight), gather(out_weight), gather(up_weight)
    at = jnp.zeros((4,), jnp.int32)
    aq, ak = masks(segment_ids, valid)
    saved = [attend(g, tokens, wqkv, vecs, aq, ak, length) for g in range(groups)]
    ctx = [f[3] for f in saved]
    result, low, hid, gd, gu, gb, gc, vec, bup = middle(tokens, ctx, cotangent, wo, vecs, wu, bu[None], wd)
    dwd = tn(hid, gd).astype(bf16)
    dwu = tn(low, gu).astype(bf16)
    dwo = tn(jnp.concatenate(ctx, axis=1), gb).astype(bf16)
    dx, dws, dbs = gb, [], []
    for g in range(groups):
        dw, dx, db = attend_back("plain", g, at, saved[g], gc, aq, ak, tokens, wqkv, dx, length)
        dws.append(dw)
        dbs.append(db)
    dwq = jnp.concatenate([dw[i] for i in range(3) for dw in dws], axis=1)
    db = jnp.stack(dbs).reshape(groups, 3, GW).transpose(1, 0, 2).reshape(3, width)
    small = jnp.concatenate([db[0], db[2], vec[:6].reshape(-1), bup[0]])
    small = lax.psum(small.reshape(-1, 128), ("rep", "shard")).reshape(-1)

    def owned(a):
        part = lax.psum_scatter(a, "shard", scatter_dimension=0, tiled=True)
        return lax.psum(part, "rep").astype(f32)

    rank = lax.axis_index("shard")
    own = lambda at, size: lax.dynamic_slice(small, (at + rank * size,), (size,))
    piece = out_bias.shape[0]
    vs = [own(width * i, piece) for i in range(8)]
    dbu = own(8 * width, up_bias.shape[0])
    gd_w, gu_w, go_w, gq_w = owned(dwd), owned(dwu), owned(dwo), owned(dwq)
    return result, dx, gq_w, jnp.stack(vs[:2]), go_w, vs[2], vs[3], vs[4], gu_w, dbu, gd_w, vs[5], vs[6], vs[7]


def solution(mesh):
    rows, one = P(("rep", "shard"), None), P("shard")
    mat, two = P("shard", None), P(None, "shard")
    near = mesh.shape["rep"] == 4 and mesh.shape["shard"] == 8
    return jax.shard_map(
        shards_near if near else shards,
        mesh=mesh,
        in_specs=(rows, rows, mat, two, mat, one, one, one, mat, one, mat, one, one, one, rows, rows),
        out_specs=(rows, rows, mat, two, mat, one, one, one, mat, one, mat, one, one, one),
        check_vma=False,
    )
```

time: 499 us -> 390 us (0.78)
  waiting for transfers between devices: 287 us -> 94.8 us
  starting transfers between devices: 0.36 us -> 82.6 us
  Pallas kernels: 96 us -> 164 us
  blocking collectives: 54.5 us -> 0 us
  matrix products: 23.2 us -> 0.28 us
  other arithmetic: 9.66 us -> 23.4 us
  between operations: 14.1 us -> 2.12 us
  local copies, waits for them, and re-layouts: 13 us -> 19.1 us
    reduce_scatter x4 -> x0, waiting for transfers between devices: 132 us -> none  [owned(): part = lax.psum_scatter(a, 'shard', scatter_dimension=0, tiled=True)]
    all_gather x4 -> x0, waiting for transfers between devices: 128 us -> none  [shards(): gather = lambda a: lax.all_gather(a, 'shard', axis=0, tiled=True)]
    ppermute x0 -> x77, waiting for transfers between devices: none -> 94.8 us  [send(): return lax.ppermute(a, AXES, where)]
    ppermute x0 -> x77, starting transfers between devices: none -> 82.6 us  [send(): return lax.ppermute(a, AXES, where)]
    pallas_call x3 -> x16, Pallas kernels: 96 us -> 164 us  [the longest x3 44 us: attend_back(): pl.pallas_call(functools.partial(attend_back_kernel, mode), grid=(seqs,),...]
    psum x1 -> x0, blocking collectives: 38.6 us -> none  [shards(): small = lax.psum(small.reshape(-1, 128), ('rep', 'shard')).reshape(-1)]
    psum x1 -> x0, waiting for transfers between devices: 24.8 us -> none  [owned(): return lax.psum(part, 'rep').astype(f32)]
    dot_general x3 -> x1, matrix products: 23.2 us -> 0.28 us  [whole_vectors(): jnp.einsum('dks,dkrl->srl', pick, every, preferred_element_type=f32)]
  transfers between devices with their start and end apart: 9 -> 77, of which waited for: 8 -> 26; matrix products, arithmetic and copies ran while one was open for 7% -> 9% of each run, Pallas kernels for 11% -> 21%
where the time goes in v3:
time: 390 us; the launch traced here: 386 us
  Pallas kernels  164 us (42%)
  waiting for transfers between devices  94.8 us (24%)
  starting transfers between devices  82.6 us (21%)
  other arithmetic  23.4 us (6%)
  local copies, waits for them, and re-layouts  19.1 us (5%)
    ppermute x77, waiting for transfers between devices, send(): return lax.ppermute(a, AXES, where)  94.8 us
    ppermute x77, starting transfers between devices, send(): return lax.ppermute(a, AXES, where)  82.6 us
    pallas_call x3, Pallas kernels, attend_back(): pl.pallas_call(functools.partial(attend_back_kernel, mode), grid=(seqs,),...  44 us
    pallas_call x1, Pallas kernels, middle(): pl.pallas_call(functools.partial(middle_kernel, len(ctx)), grid=(rows //...  43.4 us
    pallas_call x3, Pallas kernels, attend(): pl.pallas_call(attend_kernel, grid=(seqs,), in_specs=[seq, col(0), col(1)...  23.8 us
    pallas_call x1, Pallas kernels, grad_down(): pl.pallas_call(functools.partial(grad_down_kernel, len(ctx)), grid_spec=p...  15.8 us
    pallas_call x3, Pallas kernels, assemble(): pl.pallas_call(kernel, in_specs=[SMEM] + [VMEM] * len(parts), out_specs=[...  14.6 us
    pallas_call x1, Pallas kernels, grad_up(): pl.pallas_call(grad_up_kernel, grid=(8,), in_specs=[SMEM, pl.BlockSpec((r...  14.2 us
  transfers between devices with their start and end apart: 77, of which 26 were waited for; matrix products, arithmetic and copies ran while one was open for 9% of the time, Pallas kernels for 21%

profile of v3, /device:TPU:0, one launch (start us, length us, event | category | flops | bytes accessed | tf_op | source)
XLA Modules:
  0.0 386.2 jit_solution(5548258558043526916)
XLA Ops:
  19.5 6.7 %collective-permute-done.1 = bf16[96,1152]{1,0:T(8,128)(2,1)S(1)} collective-permute-done((bf16[96,1152]{1,0:T(8,128)(2,1)S(1)}, bf16[96,1152]{1,0:T(8,128)(2,1)S(1)}, u32[]{:S(2)}, u32[]{:S(2)}) %collective-permute-start.1) | collective-permute-done | bytes 221216 | tf_op jit(solution)/shard_map/ppermute | solution.py:471
  26.5 7.5 %collective-permute-done.2 = bf16[96,1152]{1,0:T(8,128)(2,1)S(1)} collective-permute-done((bf16[96,1152]{1,0:T(8,128)(2,1)S(1)}, bf16[96,1152]{1,0:T(8,128)(2,1)S(1)}, u32[]{:S(2)}, u32[]{:S(2)}) %collective-permute-start.2) | collective-permute-done | bytes 221216 | tf_op jit(solution)/shard_map/ppermute | solution.py:471
  53.8 4.4 %collective-permute-start.18 = (bf16[480,384]{1,0:T(8,128)(2,1)S(1)}, bf16[480,384]{1,0:T(8,128)(2,1)S(1)}, u32[]{:S(2)}, u32[]{:S(2)}) collective-permute-start(bf16[480,384]{1,0:T(8,128)(2,1)S(1)} %pad_maximum_fusion.6), channel_id=1, source_target_pairs={{0,6},{1,7},{2,0},{3,1},{4,2},{5,3},{6,4},{7,5},{8,14},{9,15},{10,... | collective-permute-start | bytes 1105928 | tf_op jit(solution)/shard_map/ppermute | solution.py:471
  60.1 5.6 %collective-permute-done.26.refs_3_ = bf16[3,48,768]{2,1,0:T(8,128)(2,1)S(1)} collective-permute-done((bf16[3,48,768]{2,1,0:T(8,128)(2,1)S(1)}, bf16[3,48,768]{2,1,0:T(8,128)(2,1)S(1)}, u32[]{:S(2)}, u32[]{:S(2)}) %collective-permute-start.26) | collective-permute-done | bytes 221216 | tf_op jit(solution)/shard_map/ppermute | solution.py:471
  67.4 7.1 %collective-permute-done.17 = bf16[480,384]{1,0:T(8,128)(2,1)S(1)} collective-permute-done((bf16[480,384]{1,0:T(8,128)(2,1)S(1)}, bf16[480,384]{1,0:T(8,128)(2,1)S(1)}, u32[]{:S(2)}, u32[]{:S(2)}) %collective-permute-start.17) | collective-permute-done | bytes 368672 | tf_op jit(solution)/shard_map/ppermute | solution.py:471
  82.7 4.1 %assemble.3.wq.wk.wv = bf16[768,2304]{1,0:T(8,128)(2,1)} custom-call(s32[4]{0:T(128)} %pad_add_fusion.at_r, bf16[96,2304]{1,0:T(8,128)(2,1)} %refs_0_.2, bf16[3,96,1152]{2,1,0:T(8,128)(2,1)} %copy-done.1, bf16[3,48,1152]{2,1,0:T(8,128)(2,1)} %copy-done.20, bf16[3,48,1152]{2,1,0:T(8,128)(2,1)} %copy-done.21, bf16[96,2304]{1,0:T(8,128)(2,1)} %copy-done.18, ...), custom_call_target="tpu_custom_call" | custom-call | bytes 7077888 | tf_op jit(solution)/shard_map/assemble/pallas_call | solution.py:540
  87.4 7.9 %attend.4 = (bf16[1024,256]{1,0:T(8,128)(2,1)}, bf16[1024,256]{1,0:T(8,128)(2,1)}, bf16[1024,256]{1,0:T(8,128)(2,1)}, bf16[1024,256]{1,0:T(8,128)(2,1)}, f32[2,8,512]{2,1,0:T(8,128)}) custom-call(bf16[1024,768]{1,0:T(8,128)(2,1)} %tok.13, bf16[768,2304]{1,0:T(8,128)(2,1)} %assemble.3.wq.wk.wv, bf16[768,2304]{1,0:T(8,128)(2,1)} %assemble.3.wq.wk.wv, ...), custom_call_target="tpu_custom_call" | custom-call | flops 4000000000 | bytes 5000000 | tf_op jit(solution)/shard_map/attend/pallas_call | solution.py:80
  95.4 7.3 %collective-permute-done.19.refs_2_ = bf16[3,240,384]{2,1,0:T(8,128)(2,1)} collective-permute-done((bf16[3,240,384]{2,1,0:T(8,128)(2,1)}, bf16[3,240,384]{2,1,0:T(8,128)(2,1)}, u32[]{:S(2)}, u32[]{:S(2)}) %collective-permute-start.19) | collective-permute-done | bytes 552992 | tf_op jit(solution)/shard_map/ppermute | solution.py:471
  103.2 7.9 %attend.5 = (bf16[1024,256]{1,0:T(8,128)(2,1)}, bf16[1024,256]{1,0:T(8,128)(2,1)}, bf16[1024,256]{1,0:T(8,128)(2,1)}, bf16[1024,256]{1,0:T(8,128)(2,1)}, f32[2,8,512]{2,1,0:T(8,128)}) custom-call(bf16[1024,768]{1,0:T(8,128)(2,1)} %tok.13, bf16[768,2304]{1,0:T(8,128)(2,1)} %assemble.3.wq.wk.wv, bf16[768,2304]{1,0:T(8,128)(2,1)} %assemble.3.wq.wk.wv, ...), custom_call_target="tpu_custom_call" | custom-call | flops 4000000000 | bytes 5000000 | tf_op jit(solution)/shard_map/attend/pallas_call | solution.py:80
  111.2 8.0 %attend.3 = (bf16[1024,256]{1,0:T(8,128)(2,1)}, bf16[1024,256]{1,0:T(8,128)(2,1)}, bf16[1024,256]{1,0:T(8,128)(2,1)}, bf16[1024,256]{1,0:T(8,128)(2,1)}, f32[2,8,512]{2,1,0:T(8,128)}) custom-call(bf16[1024,768]{1,0:T(8,128)(2,1)} %tok.13, bf16[768,2304]{1,0:T(8,128)(2,1)} %assemble.3.wq.wk.wv, bf16[768,2304]{1,0:T(8,128)(2,1)} %assemble.3.wq.wk.wv, ...), custom_call_target="tpu_custom_call" | custom-call | flops 4000000000 | bytes 5000000 | tf_op jit(solution)/shard_map/attend/pallas_call | solution.py:80
  119.9 4.8 %assemble.5.refs_6_ = bf16[768,3072]{1,0:T(8,128)(2,1)} custom-call(s32[4]{0:T(128)} %pad_add_fusion.at_r, bf16[96,3072]{1,0:T(8,128)(2,1)} %refs_0_.3, bf16[3,96,768]{2,1,0:T(8,128)(2,1)} %copy-done.3, bf16[3,48,768]{2,1,0:T(8,128)(2,1)} %copy-done.9, bf16[3,48,768]{2,1,0:T(8,128)(2,1)} %copy-done.10, ...), custom_call_target="tpu_custom_call" | custom-call | bytes 9437184 | tf_op jit(solution)/shard_map/assemble/pallas_call | solution.py:540
  126.5 5.7 %assemble.4 = (bf16[3072,768]{1,0:T(8,128)(2,1)}, bf16[768,768]{1,0:T(8,128)(2,1)}) custom-call(s32[4]{0:T(128)} %pad_add_fusion.at_r, bf16[480,768]{1,0:T(8,128)(2,1)} %copy-done.2, bf16[3,480,384]{2,1,0:T(8,128)(2,1)} %copy-done, bf16[3,240,384]{2,1,0:T(8,128)(2,1)} %collective-permute-done.19.refs_2_, ...), custom_call_target="tpu_custom_call" | custom-call | bytes 11796480 | tf_op jit(solution)/shard_map/assemble/pallas_call | solution.py:540
  132.2 43.4 %middle.1 = (bf16[1024,768]{1,0:T(8,128)(2,1)}, bf16[1024,768]{1,0:T(8,128)(2,1)}, bf16[1024,3072]{1,0:T(8,128)(2,1)}, bf16[1024,768]{1,0:T(8,128)(2,1)}, bf16[1...) custom-call(bf16[1024,768]{1,0:T(8,128)(2,1)} %tok.13, ...), custom_call_target="tpu_custom_call" | custom-call | flops 30000001024 | bytes 40000000 | tf_op jit(solution)/shard_map/middle/pallas_call | solution.py:325
  175.6 15.8 %grad_down.1 = (bf16[2,2,4,240,384]{4,3,2,1,0:T(8,128)(2,1)}, bf16[2,2,4,240,384]{4,3,2,1,0:T(8,128)(2,1)}) custom-call(s32[4]{0:T(128)} %pad_add_fusion.at_r, bf16[1024,256]{1,0:T(8,128)(2,1)} %get-tuple-element.66.refs_0_.ctx_r, bf16[1024,256]{1,0:T(8,128)(2,1)} %get-tuple-element.67.refs_1_.ctx_r, bf16[1024,256]{1,0:T(8,128)(2,1)} %get-tuple-element.68.refs_2_.ctx_r, ...), custom_call_target="tpu_custom_call" | custom-call | flops 8999999488 | bytes 14000000 | tf_op jit(solution)/shard_map/grad_down/pallas_call | solution.py:391
  191.5 14.2 %grad_up.1 = (bf16[2,2,2,4,48,768]{5,4,3,2,1,0:T(8,128)(2,1)}, bf16[2,2,2,4,48,768]{5,4,3,2,1,0:T(8,128)(2,1)}) custom-call(s32[4]{0:T(128)} %pad_add_fusion.at_r, bf16[1024,768]{1,0:T(8,128)(2,1)} %get-tuple-element.85.low, bf16[1024,3072]{1,0:T(8,128)(2,1)} %get-tuple-element.86.gu), custom_call_target="tpu_custom_call" | custom-call | flops 8999999488 | bytes 14000000 | tf_op jit(solution)/shard_map/grad_up/pallas_call | solution.py:437
  206.3 4.3 %collective-permute-done.38 = bf16[2,2,2,4,48,768]{5,4,3,2,1,0:T(8,128)(2,1)S(1)} collective-permute-done((bf16[2,2,2,4,48,768]{5,4,3,2,1,0:T(8,128)(2,1)}, bf16[2,2,2,4,48,768]{5,4,3,2,1,0:T(8,128)(2,1)S(1)}, u32[]{:S(2)}, u32[]{:S(2)}) %collective-permute-start.38) | collective-permute-done | bytes 2359328 | tf_op jit(solution)/shard_map/ppermute | solution.py:471
  218.4 11.4 %collective-permute-done.39 = bf16[2,4,48,768]{3,2,1,0:T(8,128)(2,1)S(1)} collective-permute-done((bf16[2,4,48,768]{3,2,1,0:T(8,128)(2,1)}, bf16[2,4,48,768]{3,2,1,0:T(8,128)(2,1)S(1)}, u32[]{:S(2)}, u32[]{:S(2)}) %collective-permute-start.39) | collective-permute-done | bytes 589856 | tf_op jit(solution)/shard_map/ppermute | solution.py:471
  244.8 6.7 %collective-permute-start.70 = (bf16[2,48,768]{2,1,0:T(8,128)(2,1)}, bf16[2,48,768]{2,1,0:T(8,128)(2,1)}, u32[]{:S(2)}, u32[]{:S(2)}) collective-permute-start(bf16[2,48,768]{2,1,0:T(8,128)(2,1)} %pad_maximum_fusion.14), channel_id=1, source_target_pairs={{0,2},{1,3},{2,4},{3,5},{4,6},{5,7},{6,0},{7,1},{8,10},{9,11},{10,... | collective-permute-start | bytes 442376 | tf_op jit(solution)/shard_map/ppermute | solution.py:471
  255.2 13.9 %attend_back.3 = (bf16[2,2,4,96,384]{4,3,2,1,0:T(8,128)(2,1)}, bf16[2,2,4,96,384]{4,3,2,1,0:T(8,128)(2,1)}, f32[1024,768]{1,0:T(8,128)}, f32[1,768]{1,0:T(1,128)}) custom-call(s32[4]{0:T(128)} %pad_add_fusion.at_r, bf16[1024,256]{1,0:T(8,128)(2,1)} %get-tuple-element.90.q_r, bf16[1024,256]{1,0:T(8,128)(2,1)} %get-tuple-element.91.k_r, ...), custom_call_target="tpu_custom_call" | custom-call | flops 8000000000 | bytes 8000000 | tf_op jit(solution)/shard_map/attend_back/pallas_call | solution.py:227
  279.6 14.5 %attend_back.4 = (bf16[2,2,4,96,384]{4,3,2,1,0:T(8,128)(2,1)}, bf16[2,2,4,96,384]{4,3,2,1,0:T(8,128)(2,1)}, f32[1024,768]{1,0:T(8,128)}, f32[1,768]{1,0:T(1,128)}) custom-call(s32[4]{0:T(128)} %pad_add_fusion.at_r, bf16[1024,256]{1,0:T(8,128)(2,1)} %get-tuple-element.96.q_r, ...), custom_call_target="tpu_custom_call", output_to_operand_aliasing={{0}: (14, {}), {1}: (15, {})} | custom-call | flops 8000000000 | bytes 8000000 | tf_op jit(solution)/shard_map/attend_back/pallas_call | solution.py:227
  294.1 15.5 %attend_back.5 = (bf16[2,2,4,64,384]{4,3,2,1,0:T(8,128)(2,1)}, bf16[2,2,4,64,384]{4,3,2,1,0:T(8,128)(2,1)}, bf16[1024,768]{1,0:T(8,128)(2,1)}, f32[1,768]{1,0:T(1,128)}) custom-call(s32[4]{0:T(128)} %pad_add_fusion.at_r, bf16[1024,256]{1,0:T(8,128)(2,1)} %get-tuple-element.74.q_r, bf16[1024,256]{1,0:T(8,128)(2,1)} %get-tuple-element.75.k_r, ...), custom_call_target="tpu_custom_call" | custom-call | flops 8000000000 | bytes 8000000 | tf_op jit(solution)/shard_map/attend_back/pallas_call | solution.py:227
  319.0 5.7 %collective-permute-done.64 = bf16[240,384]{1,0:T(8,128)(2,1)S(1)} collective-permute-done((bf16[240,384]{1,0:T(8,128)(2,1)S(1)}, bf16[240,384]{1,0:T(8,128)(2,1)S(1)}, u32[]{:S(2)}, u32[]{:S(2)}) %collective-permute-start.64) | collective-permute-done | bytes 184352 | tf_op jit(solution)/shard_map/ppermute | solution.py:471
  326.3 4.1 %collective-permute-done.52 = bf16[4,64,384]{2,1,0:T(8,128)(2,1)S(1)} collective-permute-done((bf16[4,64,384]{2,1,0:T(8,128)(2,1)S(1)}, bf16[4,64,384]{2,1,0:T(8,128)(2,1)S(1)}, u32[]{:S(2)}, u32[]{:S(2)}) %collective-permute-start.52) | collective-permute-done | bytes 196640 | tf_op jit(solution)/shard_map/ppermute | solution.py:471
  344.1 5.7 %collective-permute-done.42 = bf16[4,96,384]{2,1,0:T(8,128)(2,1)S(1)} collective-permute-done((bf16[4,96,384]{2,1,0:T(8,128)(2,1)S(1)}, bf16[4,96,384]{2,1,0:T(8,128)(2,1)S(1)}, u32[]{:S(2)}, u32[]{:S(2)}) %collective-permute-start.42) | collective-permute-done | bytes 294944 | tf_op jit(solution)/shard_map/ppermute | solution.py:471
  (357 shorter events, 151.6 us)
Async XLA Ops:
  2.3 24.0 %collective-permute-start.9 = (bf16[16,128]{1,0:T(8,128)(2,1)S(1)}, bf16[16,128]{1,0:T(8,128)(2,1)S(1)}, u32[]{:S(2)}, u32[]{:S(2)}) collective-permute-start(bf16[16,128]{1,0:T(8,128)(2,1)S(1)} %get-tuple-element.214), channel_id=1, source_target_pairs={{0,2},{1,3},{2,4},{3,5},{4,6},{5,7},{6,0},{7,1},{8,10},{9,11},{10,... | collective-permute-start | bytes 12296 | tf_op jit(solution)/shard_map/ppermute | solution.py:471
  5.4 21.0 %collective-permute-start.10 = (bf16[16,128]{1,0:T(8,128)(2,1)S(1)}, bf16[16,128]{1,0:T(8,128)(2,1)S(1)}, u32[]{:S(2)}, u32[]{:S(2)}) collective-permute-start(bf16[16,128]{1,0:T(8,128)(2,1)S(1)} %get-tuple-element.214), channel_id=1, source_target_pairs={{0,4},{1,5},{2,6},{3,7},{4,0},{5,1},{6,2},{7,3},{8,12},{9,13},{10,... | collective-permute-start | bytes 12296 | tf_op jit(solution)/shard_map/ppermute | solution.py:471
  11.1 40.0 %collective-permute-start.29 = (bf16[96,3072]{1,0:T(8,128)(2,1)}, bf16[96,3072]{1,0:T(8,128)(2,1)S(1)}, u32[]{:S(2)}, u32[]{:S(2)}) collective-permute-start(bf16[96,3072]{1,0:T(8,128)(2,1)} %refs_0_.3), channel_id=1, source_target_pairs={{0,1},{1,0},{2,3},{3,2},{4,5},{5,4},{6,7},{7,6},{8,9},{9,8},{10,11... | collective-permute-start | bytes 1769480 | tf_op jit(solution)/shard_map/ppermute | solution.py:471
  26.3 22.9 %collective-permute-start.5 = (bf16[96,2304]{1,0:T(8,128)(2,1)S(1)}, bf16[96,2304]{1,0:T(8,128)(2,1)S(1)}, u32[]{:S(2)}, u32[]{:S(2)}) collective-permute-start(bf16[96,2304]{1,0:T(8,128)(2,1)S(1)} %copy-done.8), channel_id=1, source_target_pairs={{0,1},{1,0},{2,3},{3,2},{4,5},{5,4},{6,7},{7,6},{8,9},{9,8},{10,11... | collective-permute-start | bytes 1327112 | tf_op jit(solution)/shard_map/ppermute | solution.py:471
  51.1 23.4 %collective-permute-start.17 = (bf16[480,384]{1,0:T(8,128)(2,1)S(1)}, bf16[480,384]{1,0:T(8,128)(2,1)S(1)}, u32[]{:S(2)}, u32[]{:S(2)}) collective-permute-start(bf16[480,384]{1,0:T(8,128)(2,1)S(1)} %pad_maximum_fusion.6), channel_id=1, source_target_pairs={{0,4},{1,5},{2,6},{3,7},{4,0},{5,1},{6,2},{7,3},{8,12},{9,13},{10,... | collective-permute-start | bytes 1105928 | tf_op jit(solution)/shard_map/ppermute | solution.py:471
  53.8 26.5 %collective-permute-start.6 = (bf16[3,96,1152]{2,1,0:T(8,128)(2,1)S(1)}, bf16[3,96,1152]{2,1,0:T(8,128)(2,1)S(1)}, u32[]{:S(2)}, u32[]{:S(2)}) collective-permute-start(bf16[3,96,1152]{2,1,0:T(8,128)(2,1)S(1)} %pad_maximum_fusion.2.refs_1_), channel_id=1, source_target_pairs={{0,1},{1,0},{2,3},{3,2},{4,5},{5,4},{6,7},{7,6},{8,9},{9,8},{10,11... | collective-permute-start | bytes 1990664 | tf_op jit(solution)/shard_map/ppermute | solution.py:471
  53.8 21.8 %collective-permute-start.18 = (bf16[480,384]{1,0:T(8,128)(2,1)S(1)}, bf16[480,384]{1,0:T(8,128)(2,1)S(1)}, u32[]{:S(2)}, u32[]{:S(2)}) collective-permute-start(bf16[480,384]{1,0:T(8,128)(2,1)S(1)} %pad_maximum_fusion.6), channel_id=1, source_target_pairs={{0,6},{1,7},{2,0},{3,1},{4,2},{5,3},{6,4},{7,5},{8,14},{9,15},{10,... | collective-permute-start | bytes 1105928 | tf_op jit(solution)/shard_map/ppermute | solution.py:471
  79.7 22.9 %collective-permute-start.19 = (bf16[3,240,384]{2,1,0:T(8,128)(2,1)}, bf16[3,240,384]{2,1,0:T(8,128)(2,1)}, u32[]{:S(2)}, u32[]{:S(2)}) collective-permute-start(bf16[3,240,384]{2,1,0:T(8,128)(2,1)} %get-tuple-element.157), channel_id=1, source_target_pairs={{0,8},{1,9},{2,10},{3,11},{4,12},{5,13},{6,14},{7,15},{8,0},{9,1},... | collective-permute-start | bytes 1658888 | tf_op jit(solution)/shard_map/ppermute | solution.py:471
  80.3 22.4 %collective-permute-start.20 = (bf16[3,240,384]{2,1,0:T(8,128)(2,1)}, bf16[3,240,384]{2,1,0:T(8,128)(2,1)}, u32[]{:S(2)}, u32[]{:S(2)}) collective-permute-start(bf16[3,240,384]{2,1,0:T(8,128)(2,1)} %get-tuple-element.156), channel_id=1, source_target_pairs={{0,16},{1,17},{2,18},{3,19},{4,20},{5,21},{6,22},{7,23},{8,24},{9,... | collective-permute-start | bytes 1658888 | tf_op jit(solution)/shard_map/ppermute | solution.py:471
  81.3 21.9 %collective-permute-start.33 = (bf16[2,3,48,768]{3,2,1,0:T(8,128)(2,1)}, bf16[2,3,48,768]{3,2,1,0:T(8,128)(2,1)}, u32[]{:S(2)}, u32[]{:S(2)}) collective-permute-start(bf16[2,3,48,768]{3,2,1,0:T(8,128)(2,1)} %collective-permute-done.27.refs_4_), channel_id=1, source_target_pairs={{0,1},{1,0},{2,3},{3,2},{4,5},{5,4},{6,7},{7,6},{8,9},{9,8},{10,11... | collective-permute-start | bytes 1327112 | tf_op jit(solution)/shard_map/ppermute | solution.py:471
  86.8 37.9 %collective-permute-start.22 = (bf16[3,480,384]{2,1,0:T(8,128)(2,1)S(1)}, bf16[3,480,384]{2,1,0:T(8,128)(2,1)S(1)}, u32[]{:S(2)}, u32[]{:S(2)}) collective-permute-start(bf16[3,480,384]{2,1,0:T(8,128)(2,1)S(1)} %pad_maximum_fusion.refs_1_), channel_id=1, source_target_pairs={{0,1},{1,0},{2,3},{3,2},{4,5},{5,4},{6,7},{7,6},{8,9},{9,8},{10,11... | collective-permute-start | bytes 3317768 | tf_op jit(solution)/shard_map/ppermute | solution.py:471
  95.3 29.4 %collective-permute-start.21 = (bf16[480,768]{1,0:T(8,128)(2,1)S(1)}, bf16[480,768]{1,0:T(8,128)(2,1)}, u32[]{:S(2)}, u32[]{:S(2)}) collective-permute-start(bf16[480,768]{1,0:T(8,128)(2,1)S(1)} %pad_maximum_fusion.1.refs_0_), channel_id=1, source_target_pairs={{0,1},{1,0},{2,3},{3,2},{4,5},{5,4},{6,7},{7,6},{8,9},{9,8},{10,11... | collective-permute-start | bytes 2211848 | tf_op jit(solution)/shard_map/ppermute | solution.py:471
  102.7 22.0 %collective-permute-start.23 = (bf16[3,240,384]{2,1,0:T(8,128)(2,1)}, bf16[3,240,384]{2,1,0:T(8,128)(2,1)S(1)}, u32[]{:S(2)}, u32[]{:S(2)}) collective-permute-start(bf16[3,240,384]{2,1,0:T(8,128)(2,1)} %collective-permute-done.19.refs_2_), channel_id=1, source_target_pairs={{0,1},{1,0},{2,3},{3,2},{4,5},{5,4},{6,7},{7,6},{8,9},{9,8},{10,11... | collective-permute-start | bytes 1658888 | tf_op jit(solution)/shard_map/ppermute | solution.py:471
  103.2 21.5 %collective-permute-start.24 = (bf16[3,240,384]{2,1,0:T(8,128)(2,1)}, bf16[3,240,384]{2,1,0:T(8,128)(2,1)}, u32[]{:S(2)}, u32[]{:S(2)}) collective-permute-start(bf16[3,240,384]{2,1,0:T(8,128)(2,1)} %collective-permute-done.20.refs_3_), channel_id=1, source_target_pairs={{0,1},{1,0},{2,3},{3,2},{4,5},{5,4},{6,7},{7,6},{8,9},{9,8},{10,11... | collective-permute-start | bytes 1658888 | tf_op jit(solution)/shard_map/ppermute | solution.py:471
  206.2 28.5 %collective-permute-start.35 = (bf16[2,2,4,240,384]{4,3,2,1,0:T(8,128)(2,1)}, bf16[2,2,4,240,384]{4,3,2,1,0:T(8,128)(2,1)}, u32[]{:S(2)}, u32[]{:S(2)}) collective-permute-start(bf16[2,2,4,240,384]{4,3,2,1,0:T(8,128)(2,1)} %get-tuple-element.82), channel_id=1, source_target_pairs={{0,1},{1,0},{2,3},{3,2},{4,5},{5,4},{6,7},{7,6},{8,9},{9,8},{10,11... | collective-permute-start | bytes 8847368 | tf_op jit(solution)/shard_map/ppermute | solution.py:471
  237.5 35.0 %collective-permute-start.36 = (bf16[4,240,384]{2,1,0:T(8,128)(2,1)}, bf16[4,240,384]{2,1,0:T(8,128)(2,1)}, u32[]{:S(2)}, u32[]{:S(2)}) collective-permute-start(bf16[4,240,384]{2,1,0:T(8,128)(2,1)} %get-tuple-element.127), channel_id=1, source_target_pairs={{0,8},{1,9},{2,10},{3,11},{4,12},{5,13},{6,14},{7,15},{8,0},{9,1},... | collective-permute-start | bytes 2211848 | tf_op jit(solution)/shard_map/ppermute | solution.py:471
  239.0 35.2 %collective-permute-start.37 = (bf16[4,240,384]{2,1,0:T(8,128)(2,1)}, bf16[4,240,384]{2,1,0:T(8,128)(2,1)S(1)}, u32[]{:S(2)}, u32[]{:S(2)}) collective-permute-start(bf16[4,240,384]{2,1,0:T(8,128)(2,1)} %get-tuple-element.126), channel_id=1, source_target_pairs={{0,16},{1,17},{2,18},{3,19},{4,20},{5,21},{6,22},{7,23},{8,24},{9,... | collective-permute-start | bytes 2211848 | tf_op jit(solution)/shard_map/ppermute | solution.py:471
  244.8 24.3 %collective-permute-start.70 = (bf16[2,48,768]{2,1,0:T(8,128)(2,1)}, bf16[2,48,768]{2,1,0:T(8,128)(2,1)}, u32[]{:S(2)}, u32[]{:S(2)}) collective-permute-start(bf16[2,48,768]{2,1,0:T(8,128)(2,1)} %pad_maximum_fusion.14), channel_id=1, source_target_pairs={{0,2},{1,3},{2,4},{3,5},{4,6},{5,7},{6,0},{7,1},{8,10},{9,11},{10,... | collective-permute-start | bytes 442376 | tf_op jit(solution)/shard_map/ppermute | solution.py:471
  271.0 38.8 %collective-permute-start.74 = (bf16[48,768]{1,0:T(8,128)(2,1)}, bf16[48,768]{1,0:T(8,128)(2,1)}, u32[]{:S(2)}, u32[]{:S(2)}) collective-permute-start(bf16[48,768]{1,0:T(8,128)(2,1)} %get-tuple-element.195.refs_1_), channel_id=1, source_target_pairs={{0,16},{1,17},{2,18},{3,19},{4,20},{5,21},{6,22},{7,23},{8,24},{9,... | collective-permute-start | bytes 221192 | tf_op jit(solution)/shard_map/ppermute | solution.py:471
  275.8 39.8 %collective-permute-start.63 = (bf16[2,240,384]{2,1,0:T(8,128)(2,1)S(1)}, bf16[2,240,384]{2,1,0:T(8,128)(2,1)S(1)}, u32[]{:S(2)}, u32[]{:S(2)}) collective-permute-start(bf16[2,240,384]{2,1,0:T(8,128)(2,1)S(1)} %pad_maximum_fusion.9), channel_id=1, source_target_pairs={{0,6},{1,7},{2,0},{3,1},{4,2},{5,3},{6,4},{7,5},{8,14},{9,15},{10,... | collective-permute-start | bytes 1105928 | tf_op jit(solution)/shard_map/ppermute | solution.py:471
  277.9 38.3 %collective-permute-start.62 = (bf16[2,240,384]{2,1,0:T(8,128)(2,1)S(1)}, bf16[2,240,384]{2,1,0:T(8,128)(2,1)S(1)}, u32[]{:S(2)}, u32[]{:S(2)}) collective-permute-start(bf16[2,240,384]{2,1,0:T(8,128)(2,1)S(1)} %pad_maximum_fusion.8), channel_id=1, source_target_pairs={{0,4},{1,5},{2,6},{3,7},{4,0},{5,1},{6,2},{7,3},{8,12},{9,13},{10,... | collective-permute-start | bytes 1105928 | tf_op jit(solution)/shard_map/ppermute | solution.py:471
  279.5 36.7 %collective-permute-start.61 = (bf16[2,240,384]{2,1,0:T(8,128)(2,1)S(1)}, bf16[2,240,384]{2,1,0:T(8,128)(2,1)S(1)}, u32[]{:S(2)}, u32[]{:S(2)}) collective-permute-start(bf16[2,240,384]{2,1,0:T(8,128)(2,1)S(1)} %pad_maximum_fusion.7), channel_id=1, source_target_pairs={{0,2},{1,3},{2,4},{3,5},{4,6},{5,7},{6,0},{7,1},{8,10},{9,11},{10,... | collective-permute-start | bytes 1105928 | tf_op jit(solution)/shard_map/ppermute | solution.py:471
  314.4 39.4 %collective-permute-start.76 = (bf16[2,48,768]{2,1,0:T(8,128)(2,1)S(1)}, bf16[2,48,768]{2,1,0:T(8,128)(2,1)S(1)}, u32[]{:S(2)}, u32[]{:S(2)}) collective-permute-start(bf16[2,48,768]{2,1,0:T(8,128)(2,1)S(1)} %pad_maximum_fusion.18), channel_id=1, source_target_pairs={{0,8},{1,9},{2,10},{3,11},{4,12},{5,13},{6,14},{7,15},{8,0},{9,1},... | collective-permute-start | bytes 442376 | tf_op jit(solution)/shard_map/ppermute | solution.py:471
  315.6 38.4 %collective-permute-start.75 = (bf16[2,48,768]{2,1,0:T(8,128)(2,1)S(1)}, bf16[2,48,768]{2,1,0:T(8,128)(2,1)S(1)}, u32[]{:S(2)}, u32[]{:S(2)}) collective-permute-start(bf16[2,48,768]{2,1,0:T(8,128)(2,1)S(1)} %pad_maximum_fusion.17), channel_id=1, source_target_pairs={{0,16},{1,17},{2,18},{3,19},{4,20},{5,21},{6,22},{7,23},{8,24},{9,... | collective-permute-start | bytes 442376 | tf_op jit(solution)/shard_map/ppermute | solution.py:471
  (105 other events, 1110.8 us)
